TPU v7x, 128 devices: a whole 4x4x4 slice. The times are simulated.
128 devices in a mesh: seq: 64 (over z, y, x), ch: 2 (over core).
Axes of the slice: x: 4, y: 4, z: 4, core: 2. Of those that a mesh axis runs over, the one named last changes fastest.
Arguments:
- tokens: bfloat16 [32768, 2048], P('seq', 'ch'), may hold values from -6 to 6
- in_weight: bfloat16 [2048, 3, 2048], P(None, None, 'ch'), may hold values from -0.125 to 0.125
- short_filter: float32 [3, 3, 2048], P(None, None, 'ch'), may hold values from -3 to 3
- residues: float32 [2048, 16], P('ch'), may hold values from -3 to 3
- rates: float32 [2048, 16], P('ch'), as said below
- out_weight: bfloat16 [2048, 2048], P('ch'), may hold values from -0.1875 to 0.1875
Outputs:
- output: float32 [32768, 2048], P('seq', 'ch')
Inputs may be any that keep to these rules, and one draw needn't show every extreme that they name: `rates`: every rate lies between 0.2 / 32768 and 1 / 30.
All inputs are finite; a program needn't handle non-finite values.
Results may differ from a plain program's by a relative error of at most 0.004.
Values may be sent and summed in bfloat16 or wider, within the bound.
No kernel may reach another device: no remote copies, remote signals or barrier semaphores. Data moves between devices by JAX's collectives and lax.ppermute only.
A program may use at most 192 MiB of HBM per device.

v0:
```python
import jax
import jax.numpy as jnp
from jax import lax
from jax.experimental import pallas as pl
from jax.experimental.pallas import tpu as pltpu
from jax.sharding import Mesh, PartitionSpec as P

SEGS = 8
HALO = 16
LANES = 128
HISTORY = 8
WIDTH = 256
AHEAD = 2
SEQ = ("z", "y", "x")
RING = 4
F32 = jnp.float32
BF16 = jnp.bfloat16
MIB = 1024 * 1024


def spread(row):
    return jnp.broadcast_to(row, (SEGS, row.shape[-1]))


def filtered_step(taps, now, one, two):
    return taps[0] * now + taps[1] * one + taps[2] * two


def tree_sum(parts):
    parts = list(parts)
    while len(parts) > 1:
        parts = [a + b for a, b in zip(parts[::2], parts[1::2])]
    return parts[0]


def stage_kernel(
    where_ref,
    own_ref,
    other_ref,
    w_ref,
    filt_ref,
    rates_ref,
    lhs_out,
    w_out,
    filt_out,
    rates_out,
    into_out,
    total_out,
    sems,
):
    rows, half = own_ref.shape
    core = lax.rem(where_ref[0], 2)
    mine = pl.multiple_of(core * half, half)
    theirs = pl.multiple_of((1 - core) * half, half)
    pairs = [
        (rates_ref, rates_out),
        (own_ref, lhs_out.at[:, pl.ds(mine, half)]),
        (other_ref, lhs_out.at[:, pl.ds(theirs, half)]),
        (filt_ref, filt_out),
        (w_ref.at[:, :, pl.ds(0, w_out.shape[2])], w_out),
    ]
    copies = [pltpu.make_async_copy(src, dst, sems.at[i]) for i, (src, dst) in enumerate(pairs)]
    for copy in copies:
        copy.start()
    copies[0].wait()
    rates = rates_out[...]
    rest, span, after = where_ref[0] // 2, rows, 0

    def decay(tokens):
        return jnp.exp(-rates * jnp.asarray(tokens, F32))

    for level in range(len(SEQ)):
        here = lax.rem(rest, RING)
        rest = rest // RING
        total_out[RING * level] = decay(span * (RING - 1 - here))
        for k in range(1, RING):
            inside = (k <= here).astype(F32)
            into_out[(RING - 1) * level + k - 1] = inside * decay(span * (k - 1) + after)
            place = lax.rem(here - k + RING, RING)
            total_out[RING * level + k] = decay(span * (RING - 1 - place))
        after = after + span * here
        span = span * RING
    for copy in copies[1:]:
        copy.wait()


def stage_call(where, own, other, weight, filt, rates):
    rows, half = own.shape
    vmem = pl.BlockSpec(memory_space=pltpu.VMEM)
    anywhere = pl.BlockSpec(memory_space=pl.ANY)
    inputs = [pltpu.with_memory_space_constraint(x, pltpu.HBM) for x in (own, weight, filt, rates)]
    return pl.pallas_call(
        stage_kernel,
        in_specs=[pl.BlockSpec(memory_space=pltpu.SMEM)] + [anywhere] * 5,
        out_specs=[vmem] * 6,
        out_shape=[
            pltpu.VMEM((rows, 2 * half), BF16),
            pltpu.VMEM((*weight.shape[:2], AHEAD * WIDTH), BF16),
            pltpu.VMEM(filt.shape, F32),
            pltpu.VMEM(rates.shape, F32),
            pltpu.VMEM((len(SEQ) * (RING - 1), *rates.shape), F32),
            pltpu.VMEM((len(SEQ) * RING, *rates.shape), F32),
        ],
        scratch_shapes=[pltpu.SemaphoreType.DMA((5,))],
        compiler_params=pltpu.CompilerParams(vmem_limit_bytes=4 * MIB),
        name="stage",
    )(where, inputs[0], other, *inputs[1:])


def front_kernel(
    where_ref,
    lhs_ref,
    halo_own_ref,
    halo_other_ref,
    ahead_ref,
    w_ref,
    filt_ref,
    rates_ref,
    gain_ref,
    pair_ref,
    ends_ref,
    total_ref,
    halo_ref,
    rest_ref,
    proj_a,
    proj_b,
    sem,
):
    rows = lhs_ref.shape[0]
    half = halo_own_ref.shape[1]
    steps = rows // SEGS
    pitch = steps + HISTORY
    modes = rates_ref.shape[0]
    streams = w_ref.shape[0]
    tiles = w_ref.shape[2] // WIDTH
    parts_of_rows = 2
    per = SEGS // parts_of_rows
    proj = (proj_a, proj_b)

    rest = pltpu.make_async_copy(
        w_ref.at[:, :, pl.ds(AHEAD * WIDTH, (tiles - AHEAD) * WIDTH)], rest_ref, sem
    )
    rest.start()
    core = lax.rem(where_ref[0], 2)
    halo_ref[:, pl.ds(pl.multiple_of(core * half, half), half)] = halo_own_ref[...]
    halo_ref[:, pl.ds(pl.multiple_of((1 - core) * half, half), half)] = halo_other_ref[...]

    def projection(tile):
        held = proj[tile % 2]
        weights, column = (ahead_ref, tile) if tile < AHEAD else (rest_ref, tile - AHEAD)
        if tile == AHEAD:
            rest.wait()

        def piece(j, m):
            first = m * per
            lhs = lhs_ref[first * steps : (first + per) * steps]
            if m == 0:
                lhs = jnp.concatenate([halo_ref[...], lhs], axis=0)
            part = jnp.dot(
                lhs,
                weights[j, :, column * WIDTH : (column + 1) * WIDTH],
                preferred_element_type=F32,
            )
            for l in range(WIDTH // LANES):
                lanes = slice(l * LANES, (l + 1) * LANES)
                for g in range(first, first + per):
                    row = (g - first) * steps + (0 if m else HALO)
                    held[j, l, g * pitch + HISTORY : (g + 1) * pitch] = part[row : row + steps, lanes]
                    if g == 0:
                        held[j, l, :HISTORY] = part[row - HISTORY : row, lanes]
                    if g + 1 < SEGS:
                        held[j, l, (g + 1) * pitch : (g + 1) * pitch + HISTORY] = part[
                            row + steps - HISTORY : row + steps, lanes
                        ]

        return [lambda j=j, m=m: piece(j, m) for j in range(streams) for m in range(parts_of_rows)]

    def recurrence(tile, size=4):
        held = proj[tile % 2]
        pieces = []
        for l in range(WIDTH // LANES):
            lanes = slice(tile * WIDTH + l * LANES, tile * WIDTH + (l + 1) * LANES)
            kept = {}

            def at(j, t, l=l):
                return held[j, l, pl.ds(HISTORY + t, SEGS, stride=pitch), :]

            def begin(kept=kept, lanes=lanes, at=at):
                kept["taps"] = [
                    [spread(filt_ref[a, j : j + 1, lanes]) for a in range(3)] for j in range(streams)
                ]
                kept["decay"] = [spread(jnp.exp(-rates_ref[n : n + 1, lanes])) for n in range(modes)]
                kept["gain"] = [spread(gain_ref[n : n + 1, lanes]) for n in range(modes)]
                kept["one"] = [at(j, -1) for j in range(streams)]
                kept["two"] = [at(j, -2) for j in range(streams)]
                kept["state"] = [jnp.zeros((SEGS, LANES), F32)] * modes

            def advance(t0, kept=kept, lanes=lanes, at=at):
                for t in range(t0, t0 + size):
                    now = [at(j, t) for j in range(streams)]
                    q, k, v = [
                        filtered_step(*terms)
                        for terms in zip(kept["taps"], now, kept["one"], kept["two"])
                    ]
                    kept["one"], kept["two"] = now, kept["one"]
                    source = k * v
                    kept["state"] = [d * s + source for d, s in zip(kept["decay"], kept["state"])]
                    row = slice(t * SEGS, (t + 1) * SEGS)
                    pair_ref[0, row, lanes] = q
                    pair_ref[1, row, lanes] = tree_sum(
                        [g * s for g, s in zip(kept["gain"], kept["state"])]
                    )

            def finish(kept=kept, lanes=lanes):
                seg = lax.broadcasted_iota(jnp.int32, (SEGS, LANES), 0)
                later = (SEGS - 1 - seg).astype(F32) * float(steps)
                for n, state in enumerate(kept["state"]):
                    ends_ref[n * SEGS : (n + 1) * SEGS, lanes] = state
                    weight = jnp.exp(-spread(rates_ref[n : n + 1, lanes]) * later)
                    total_ref[n : n + 1, lanes] = jnp.sum(state * weight, axis=0, keepdims=True)

            pieces += [begin]
            pieces += [lambda t0=t0, advance=advance: advance(t0) for t0 in range(0, steps, size)]
            pieces += [finish]
        return pieces

    for work in projection(0):
        work()
    for tile in range(tiles):
        slow = projection(tile + 1) if tile + 1 < tiles else [lambda: None]
        fast = recurrence(tile)
        done = 0
        for i, work in enumerate(slow):
            work()
            upto = (i + 1) * len(fast) // len(slow)
            for step in fast[done:upto]:
                step()
            done = upto


def front_call(where, lhs, halo_own, halo_other, ahead, weight, filt, rates, gain):
    rows, full = lhs.shape
    streams, _, channels = weight.shape
    modes = rates.shape[0]
    vmem = pl.BlockSpec(memory_space=pltpu.VMEM)
    held = pltpu.VMEM((streams, WIDTH // LANES, rows + SEGS * HISTORY, LANES), F32)
    return pl.pallas_call(
        front_kernel,
        in_specs=[pl.BlockSpec(memory_space=pltpu.SMEM)]
        + [vmem] * 4
        + [pl.BlockSpec(memory_space=pl.ANY)]
        + [vmem] * 3,
        out_specs=[vmem] * 3,
        out_shape=[
            pltpu.VMEM((2, rows, channels), F32),
            pltpu.VMEM((modes * SEGS, channels), F32),
            pltpu.VMEM((modes, channels), F32),
        ],
        scratch_shapes=[
            pltpu.VMEM((HALO, full), BF16),
            pltpu.VMEM((streams, full, channels - AHEAD * WIDTH), BF16),
            held,
            held,
            pltpu.SemaphoreType.DMA,
        ],
        compiler_params=pltpu.CompilerParams(vmem_limit_bytes=18 * MIB),
        name="front",
    )(
        where,
        lhs,
        halo_own,
        halo_other,
        ahead,
        pltpu.with_memory_space_constraint(weight, pltpu.HBM),
        filt,
        rates,
        gain,
    )


def hidden_kernel(ends_ref, into_ref, pair_ref, rates_ref, gain_ref, hidden_ref):
    _, rows, channels = pair_ref.shape
    steps = rows // SEGS
    modes = rates_ref.shape[0]
    seg = lax.broadcasted_iota(jnp.int32, (SEGS, LANES), 0)
    for i in range(channels // LANES):
        lanes = slice(i * LANES, (i + 1) * LANES)
        decays, leads = [], []
        for n in range(modes):
            rate = spread(rates_ref[n : n + 1, lanes])
            state = pltpu.roll(ends_ref[n * SEGS : (n + 1) * SEGS, lanes], 1, 0)
            state = jnp.where(seg == 0, spread(into_ref[n : n + 1, lanes]), state)
            for hop in (1, 2, 4):
                earlier = pltpu.roll(state, hop, 0) * jnp.exp(-rate * float(steps * hop))
                state = state + jnp.where(seg >= hop, earlier, 0.0)
            decays.append(jnp.exp(-rate))
            leads.append(spread(gain_ref[n : n + 1, lanes]) * state)

        def body(t, leads, lanes=lanes, decays=decays):
            halves = []
            for u in range(2):
                row = pl.ds(pl.multiple_of((2 * t + u) * SEGS, SEGS), SEGS)
                leads = tuple(d * s for d, s in zip(decays, leads))
                halves.append(pair_ref[0, row, lanes] * (pair_ref[1, row, lanes] + tree_sum(leads)))
            row = pl.ds(pl.multiple_of(2 * t * SEGS, 2 * SEGS), 2 * SEGS)
            hidden_ref[row, lanes] = jnp.concatenate(halves, axis=0).astype(BF16)
            return leads

        lax.fori_loop(0, steps // 2, body, tuple(leads), unroll=8)


def hidden_call(ends, into, pair, rates, gain):
    vmem = pl.BlockSpec(memory_space=pltpu.VMEM)
    args = [pltpu.with_memory_space_constraint(x, pltpu.VMEM) for x in (ends, into, pair, rates, gain)]
    return pl.pallas_call(
        hidden_kernel,
        in_specs=[vmem] * 5,
        out_specs=vmem,
        out_shape=pltpu.VMEM(pair.shape[1:], BF16),
        compiler_params=pltpu.CompilerParams(vmem_limit_bytes=4 * MIB),
        name="hidden",
    )(*args)


def product_kernel(where_ref, hidden_ref, w_ref, w_other_ref, part_ref, staged_ref, mine_ref, sems):
    columns = part_ref.shape[1]
    lanes = pl.ds(pl.multiple_of(lax.rem(where_ref[0], 2) * columns, columns), columns)
    mine = pltpu.make_async_copy(w_ref.at[:, lanes], mine_ref, sems.at[0])
    theirs = pltpu.make_async_copy(w_other_ref.at[:, lanes], staged_ref, sems.at[1])
    mine.start()
    theirs.start()
    mine.wait()
    part_ref[...] = jnp.dot(hidden_ref[...], mine_ref[...], preferred_element_type=F32)
    theirs.wait()


def product_call(where, hidden, weight, weight_other):
    rows, channels = hidden.shape
    columns = weight.shape[1] // 2
    vmem = pl.BlockSpec(memory_space=pltpu.VMEM)
    anywhere = pl.BlockSpec(memory_space=pl.ANY)
    return pl.pallas_call(
        product_kernel,
        in_specs=[pl.BlockSpec(memory_space=pltpu.SMEM), vmem, anywhere, anywhere],
        out_specs=[vmem] * 2,
        out_shape=[pltpu.VMEM((rows, columns), F32), pltpu.VMEM((channels, columns), BF16)],
        scratch_shapes=[pltpu.VMEM((channels, columns), BF16), pltpu.SemaphoreType.DMA((2,))],
        compiler_params=pltpu.CompilerParams(vmem_limit_bytes=8 * MIB),
        name="product",
    )(where, hidden, weight, weight_other)


def output_kernel(part_ref, other_ref, w_ref, out_ref, acc_ref, rows_ref, sems):
    rows, columns = part_ref.shape
    steps = rows // SEGS
    copies = []
    for tile in range(columns // WIDTH):
        lanes = slice(tile * WIDTH, (tile + 1) * WIDTH)
        part = part_ref[:, lanes] + jnp.dot(
            other_ref[...], w_ref[:, lanes], preferred_element_type=F32
        )
        for l in range(WIDTH // LANES):
            acc_ref[tile, l] = part[:, l * LANES : (l + 1) * LANES]
            for j in range(SEGS):
                rows_ref[
                    j * steps : (j + 1) * steps,
                    tile * WIDTH + l * LANES : tile * WIDTH + (l + 1) * LANES,
                ] = acc_ref[tile, l, pl.ds(j, steps, stride=SEGS), :]
        copies.append(pltpu.make_async_copy(rows_ref.at[:, lanes], out_ref.at[:, lanes], sems.at[tile]))
        copies[-1].start()
    for copy in copies:
        copy.wait()


def output_call(part, other, weight):
    rows, columns = part.shape
    vmem = pl.BlockSpec(memory_space=pltpu.VMEM)
    args = [pltpu.with_memory_space_constraint(x, pltpu.VMEM) for x in (part, other, weight)]
    return pl.pallas_call(
        output_kernel,
        in_specs=[vmem] * 3,
        out_specs=pl.BlockSpec(memory_space=pl.ANY),
        out_shape=jax.ShapeDtypeStruct((rows, columns), F32),
        scratch_shapes=[
            pltpu.VMEM((columns // WIDTH, WIDTH // LANES, rows, LANES), F32),
            pltpu.VMEM((rows, columns), F32),
            pltpu.SemaphoreType.DMA((columns // WIDTH,)),
        ],
        compiler_params=pltpu.CompilerParams(vmem_limit_bytes=8 * MIB),
        name="output",
    )(*args)


def swapped(x):
    return lax.ppermute(x, "ch", [(0, 1), (1, 0)])


def from_before(x):
    count = RING**3
    return lax.ppermute(x, SEQ, [(i, i + 1) for i in range(count - 1)])


def round_the_ring(state, axis):
    sent = state.astype(BF16)
    return [
        lax.ppermute(sent, axis, [(i, (i + k) % RING) for i in range(RING)]).astype(F32)
        for k in range(1, RING)
    ]


def on_device(tokens, in_weight, short_filter, residues, rates, out_weight):
    rows = tokens.shape[0]
    where = lax.axis_index((*SEQ, "ch")).astype(jnp.int32).reshape(1)
    weight = in_weight.transpose(1, 0, 2)
    rates = rates.T
    gain = residues.T * jnp.sqrt(1.0 - jnp.exp(-2.0 * rates))

    halo_own = from_before(tokens[rows - HALO :])
    lhs, ahead, filt, rates, into_weights, total_weights = stage_call(
        where, tokens, swapped(tokens), weight, short_filter, rates
    )
    halo_own, lhs, out_weight = lax.optimization_barrier((halo_own, lhs, out_weight))
    halo_other = swapped(halo_own)
    lhs, halo_other, out_weight = lax.optimization_barrier((lhs, halo_other, out_weight))
    out_weight_other = swapped(out_weight)
    pair, ends, total = front_call(
        where, lhs, halo_own, halo_other, ahead, weight, filt, rates, gain
    )

    into = 0.0
    for level, axis in enumerate(reversed(SEQ)):
        arrived = round_the_ring(total, axis)
        total = total_weights[RING * level] * total
        for k, part in enumerate(arrived):
            into = into + into_weights[(RING - 1) * level + k] * part
            total = total + total_weights[RING * level + k + 1] * part

    hidden = hidden_call(ends, into, pair, rates, gain)
    part, staged = product_call(where, hidden, out_weight, out_weight_other)
    return output_call(part, swapped(hidden), staged)


def solution(mesh):
    cube = Mesh(mesh.devices.reshape(RING, RING, RING, 2), (*SEQ, "ch"))
    return jax.shard_map(
        on_device,
        mesh=cube,
        in_specs=(
            P(SEQ, "ch"),
            P(None, None, "ch"),
            P(None, None, "ch"),
            P("ch", None),
            P("ch", None),
            P("ch", None),
        ),
        out_specs=P(SEQ, "ch"),
        check_vma=False,
    )
```

profile of v0, /device:TPU:1, one launch (start us, length us, event | category | flops | bytes accessed | tf_op | source)
XLA Modules:
  0.0 59.8 jit_solution(5687450919591882864)
XLA Ops:
  0.0 1.4 %collective-permute-start.1 = (bf16[512,1024]{1,0:T(8,128)(2,1)}, bf16[512,1024]{1,0:T(8,128)(2,1)S(1)}, u32[]{:S(2)}, u32[]{:S(2)}) collective-permute-start(bf16[512,1024]{1,0:T(8,128)(2,1)} %own_ref.1), channel_id=1, source_target_pairs={{0,1},{1,0},{2,3},{3,2},{4,5},{5,4},{6,7},{7,6},{8,9},{9,8},{10,11... | collective-permute-start | bytes 3145736 | tf_op jit(solution)/shard_map/ppermute | solution.py:395
  1.4 0.8 %slice.54 = bf16[16,1024]{1,0:T(8,128)(2,1)S(1)} slice(bf16[512,1024]{1,0:T(8,128)(2,1)} %own_ref.1), slice={[496:512], [0:1024]} | slice | bytes 65536 | tf_op jit(solution)/shard_map/slice | solution.py:418
  2.2 3.2 %collective-permute-start = (bf16[16,1024]{1,0:T(8,128)(2,1)S(1)}, bf16[16,1024]{1,0:T(8,128)(2,1)S(1)}, u32[]{:S(2)}, u32[]{:S(2)}) collective-permute-start(bf16[16,1024]{1,0:T(8,128)(2,1)S(1)} %slice.54), channel_id=1, source_target_pairs={{0,2},{2,4},{4,6},{6,8},{8,10},{10,12},{12,14},{14,16},{16,18},{18... | collective-permute-start | bytes 98312 | tf_op jit(solution)/shard_map/ppermute | solution.py:400
  5.4 0.0 copy-start
  5.4 0.0 copy-start.2
  5.4 3.4 %stage.1 = (bf16[512,2048]{1,0:T(8,128)(2,1)S(1)}, bf16[3,2048,512]{2,1,0:T(8,128)(2,1)S(1)}, f32[3,3,1024]{2,1,0:T(4,128)S(1)}, f32[16,1024]{1,0:T(8,128)S(1)},...) custom-call(s32[1]{0:T(128)} %bitcast.where_ref, bf16[512,1024]{1,0:T(8,128)(2,1)} %own_ref.1, ...), custom_call_target="tpu_custom_call" | custom-call | tf_op jit(solution)/shard_map/stage/pallas_call | solution.py:92
  8.8 0.4 collective-permute-start.2
  9.2 0.9 %collective-permute-done.2.halo_other_ref = bf16[16,1024]{1,0:T(8,128)(2,1)S(1)} collective-permute-done((bf16[16,1024]{1,0:T(8,128)(2,1)S(1)}, bf16[16,1024]{1,0:T(8,128)(2,1)S(1)}, u32[]{:S(2)}, u32[]{:S(2)}) %collective-permute-start.2) | collective-permute-done | bytes 32800 | tf_op jit(solution)/shard_map/ppermute | solution.py:395
  10.1 0.3 collective-permute-start.12
  10.4 13.1 %front.1 = (f32[2,512,1024]{2,1,0:T(8,128)S(1)}, f32[128,1024]{1,0:T(8,128)S(1)}, f32[16,1024]{1,0:T(8,128)S(1)}) custom-call(s32[1]{0:T(128)} %bitcast.where_ref, bf16[512,2048]{1,0:T(8,128)(2,1)S(1)} %get-tuple-element.26.lhs_ref, bf16[16,1024]{1,0:T(8,128)(2,1)S(1)} %collective-permute-done.halo_own_ref, ...), custom_call_target="tpu_custom_call" | custom-call | tf_op jit(solution)/shard_map/front/pallas_call | solution.py:247
  23.5 2.7 %collective-permute-start.5 = (bf16[16,1024]{1,0:T(8,128)(2,1)S(1)}, bf16[16,1024]{1,0:T(8,128)(2,1)S(1)}, u32[]{:S(2)}, u32[]{:S(2)}) collective-permute-start(bf16[16,1024]{1,0:T(8,128)(2,1)S(1)} %convert_element_type.36), channel_id=1, source_target_pairs={{0,6},{2,0},{4,2},{6,4},{1,7},{3,1},{5,3},{7,5},{8,14},{10,8},{12,... | collective-permute-start | bytes 98312 | tf_op jit(solution)/shard_map/ppermute | solution.py:406
  26.3 0.5 collective-permute-start.4
  26.8 0.3 collective-permute-start.3
  27.1 0.2 collective-permute-done.5
  27.3 3.3 %collective-permute-done.4 = bf16[16,1024]{1,0:T(8,128)(2,1)S(1)} collective-permute-done((bf16[16,1024]{1,0:T(8,128)(2,1)S(1)}, bf16[16,1024]{1,0:T(8,128)(2,1)S(1)}, u32[]{:S(2)}, u32[]{:S(2)}) %collective-permute-start.4) | collective-permute-done | bytes 32800 | tf_op jit(solution)/shard_map/ppermute | solution.py:406
  30.5 0.3 collective-permute-done.3
  30.9 2.8 %collective-permute-start.8 = (bf16[16,1024]{1,0:T(8,128)(2,1)S(1)}, bf16[16,1024]{1,0:T(8,128)(2,1)S(1)}, u32[]{:S(2)}, u32[]{:S(2)}) collective-permute-start(bf16[16,1024]{1,0:T(8,128)(2,1)S(1)} %get-tuple-element.39), channel_id=1, source_target_pairs={{0,24},{8,0},{16,8},{24,16},{1,25},{9,1},{17,9},{25,17},{2,26},{10... | collective-permute-start | bytes 98312 | tf_op jit(solution)/shard_map/ppermute | solution.py:406
  33.7 0.3 collective-permute-start.7
  34.0 0.6 collective-permute-start.6
  34.6 0.1 collective-permute-done.8
  34.7 3.3 %collective-permute-done.7 = bf16[16,1024]{1,0:T(8,128)(2,1)S(1)} collective-permute-done((bf16[16,1024]{1,0:T(8,128)(2,1)S(1)}, bf16[16,1024]{1,0:T(8,128)(2,1)S(1)}, u32[]{:S(2)}, u32[]{:S(2)}) %collective-permute-start.7) | collective-permute-done | bytes 32800 | tf_op jit(solution)/shard_map/ppermute | solution.py:406
  38.0 0.3 collective-permute-done.6
  38.4 3.7 %collective-permute-start.11 = (bf16[16,1024]{1,0:T(8,128)(2,1)S(1)}, bf16[16,1024]{1,0:T(8,128)(2,1)S(1)}, u32[]{:S(2)}, u32[]{:S(2)}) collective-permute-start(bf16[16,1024]{1,0:T(8,128)(2,1)S(1)} %fusion.14), channel_id=1, source_target_pairs={{0,96},{32,0},{64,32},{96,64},{1,97},{33,1},{65,33},{97,65},{2,98}... | collective-permute-start | bytes 98312 | tf_op jit(solution)/shard_map/ppermute | solution.py:406
  42.1 0.7 %collective-permute-start.9 = (bf16[16,1024]{1,0:T(8,128)(2,1)S(1)}, bf16[16,1024]{1,0:T(8,128)(2,1)S(1)}, u32[]{:S(2)}, u32[]{:S(2)}) collective-permute-start(bf16[16,1024]{1,0:T(8,128)(2,1)S(1)} %fusion.14), channel_id=1, source_target_pairs={{0,32},{32,64},{64,96},{96,0},{1,33},{33,65},{65,97},{97,1},{2,34}... | collective-permute-start | bytes 98312 | tf_op jit(solution)/shard_map/ppermute | solution.py:406
  42.8 0.3 collective-permute-done.11
  43.1 3.3 %collective-permute-done.10 = bf16[16,1024]{1,0:T(8,128)(2,1)S(1)} collective-permute-done((bf16[16,1024]{1,0:T(8,128)(2,1)S(1)}, bf16[16,1024]{1,0:T(8,128)(2,1)S(1)}, u32[]{:S(2)}, u32[]{:S(2)}) %collective-permute-start.10) | collective-permute-done | bytes 32800 | tf_op jit(solution)/shard_map/ppermute | solution.py:406
  46.4 0.1 fusion.7.into_ref
  46.5 3.4 %hidden.1.hidden_ref = bf16[512,1024]{1,0:T(8,128)(2,1)S(1)} custom-call(f32[128,1024]{1,0:T(8,128)S(1)} %get-tuple-element.31.ends_ref, f32[16,1024]{1,0:T(8,128)S(1)} %fusion.7.into_ref, f32[2,512,1024]{2,1,0:T(8,128)S(1)} %get-tuple-element.35.pair_ref, f32[16,1024]{1,0:T(8,128)S(1)} %get-tuple-element.30.rates_ref, ...), custom_call_target="tpu_custom_call" | custom-call | tf_op jit(solution)/shard_map/hidden/pallas_call | solution.py:315
  49.9 4.9 %collective-permute-start.13 = (bf16[512,1024]{1,0:T(8,128)(2,1)S(1)}, bf16[512,1024]{1,0:T(8,128)(2,1)S(1)}, u32[]{:S(2)}, u32[]{:S(2)}) collective-permute-start(bf16[512,1024]{1,0:T(8,128)(2,1)S(1)} %hidden.1.hidden_ref), channel_id=1, source_target_pairs={{0,1},{1,0},{2,3},{3,2},{4,5},{5,4},{6,7},{7,6},{8,9},{9,8},{10,11... | collective-permute-start | bytes 3145736 | tf_op jit(solution)/shard_map/ppermute | solution.py:395
  54.8 2.0 %product.1 = (f32[512,1024]{1,0:T(8,128)S(1)}, bf16[1024,1024]{1,0:T(8,128)(2,1)S(1)}) custom-call(s32[1]{0:T(128)} %bitcast.where_ref, bf16[512,1024]{1,0:T(8,128)(2,1)S(1)} %hidden.1.hidden_ref, bf16[1024,2048]{1,0:T(8,128)(2,1)S(1)} %copy-done, bf16[1024,2048]{1,0:T(8,128)(2,1)S(1)} %collective-permute-done.12.w_other_ref), custom_call_target="tpu_custom_call" | custom-call | tf_op jit(solution)/shard_map/product/pallas_call | solution.py:342
  56.7 0.3 collective-permute-done.13.other_ref
  57.0 2.6 %output.1 = f32[512,1024]{1,0:T(8,128)} custom-call(f32[512,1024]{1,0:T(8,128)S(1)} %get-tuple-element.37.part_ref, bf16[512,1024]{1,0:T(8,128)(2,1)S(1)} %collective-permute-done.13.other_ref, bf16[1024,1024]{1,0:T(8,128)(2,1)S(1)} %get-tuple-element.38.w_ref), custom_call_target="tpu_custom_call" | custom-call | tf_op jit(solution)/shard_map/output/pallas_call | solution.py:379
  (13 shorter events, 0.1 us)
Async XLA Ops:
  0.0 5.4 %collective-permute-start.1 = (bf16[512,1024]{1,0:T(8,128)(2,1)}, bf16[512,1024]{1,0:T(8,128)(2,1)S(1)}, u32[]{:S(2)}, u32[]{:S(2)}) collective-permute-start(bf16[512,1024]{1,0:T(8,128)(2,1)} %own_ref.1), channel_id=1, source_target_pairs={{0,1},{1,0},{2,3},{3,2},{4,5},{5,4},{6,7},{7,6},{8,9},{9,8},{10,11... | collective-permute-start | bytes 3145736 | tf_op jit(solution)/shard_map/ppermute | solution.py:395
  2.2 6.6 %collective-permute-start = (bf16[16,1024]{1,0:T(8,128)(2,1)S(1)}, bf16[16,1024]{1,0:T(8,128)(2,1)S(1)}, u32[]{:S(2)}, u32[]{:S(2)}) collective-permute-start(bf16[16,1024]{1,0:T(8,128)(2,1)S(1)} %slice.54), channel_id=1, source_target_pairs={{0,2},{2,4},{4,6},{6,8},{8,10},{10,12},{12,14},{14,16},{16,18},{18... | collective-permute-start | bytes 98312 | tf_op jit(solution)/shard_map/ppermute | solution.py:400
  5.4 4.7 %copy-start = (bf16[1024,2048]{1,0:T(8,128)(2,1)S(1)}, bf16[1024,2048]{1,0:T(8,128)(2,1)}, u32[]{:S(2)}) copy-start(bf16[1024,2048]{1,0:T(8,128)(2,1)} %w_ref) | copy-start | bytes 12582916
  5.4 5.0 %copy-start.1 = (f32[1024,16]{0,1:T(8,128)S(1)}, f32[1024,16]{0,1:T(8,128)}, u32[]{:S(2)}) copy-start(f32[1024,16]{0,1:T(8,128)} %param.10) | copy-start | bytes 196612
  5.4 5.0 %copy-start.2 = (f32[1024,16]{0,1:T(8,128)S(1)}, f32[1024,16]{0,1:T(8,128)}, u32[]{:S(2)}) copy-start(f32[1024,16]{0,1:T(8,128)} %param.9) | copy-start | bytes 196612
  8.8 1.3 %collective-permute-start.2 = (bf16[16,1024]{1,0:T(8,128)(2,1)S(1)}, bf16[16,1024]{1,0:T(8,128)(2,1)S(1)}, u32[]{:S(2)}, u32[]{:S(2)}) collective-permute-start(bf16[16,1024]{1,0:T(8,128)(2,1)S(1)} %collective-permute-done.halo_own_ref), channel_id=1, source_target_pairs={{0,1},{1,0},{2,3},{3,2},{4,5},{5,4},{6,7},{7,6},{8,9},{9,8},{10,11... | collective-permute-start | bytes 98312 | tf_op jit(solution)/shard_map/ppermute | solution.py:395
  10.1 44.6 %collective-permute-start.12 = (bf16[1024,2048]{1,0:T(8,128)(2,1)S(1)}, bf16[1024,2048]{1,0:T(8,128)(2,1)S(1)}, u32[]{:S(2)}, u32[]{:S(2)}) collective-permute-start(bf16[1024,2048]{1,0:T(8,128)(2,1)S(1)} %copy-done), channel_id=1, source_target_pairs={{0,1},{1,0},{2,3},{3,2},{4,5},{5,4},{6,7},{7,6},{8,9},{9,8},{10,11... | collective-permute-start | bytes 12582920 | tf_op jit(solution)/shard_map/ppermute | solution.py:395
  23.5 3.8 %collective-permute-start.5 = (bf16[16,1024]{1,0:T(8,128)(2,1)S(1)}, bf16[16,1024]{1,0:T(8,128)(2,1)S(1)}, u32[]{:S(2)}, u32[]{:S(2)}) collective-permute-start(bf16[16,1024]{1,0:T(8,128)(2,1)S(1)} %convert_element_type.36), channel_id=1, source_target_pairs={{0,6},{2,0},{4,2},{6,4},{1,7},{3,1},{5,3},{7,5},{8,14},{10,8},{12,... | collective-permute-start | bytes 98312 | tf_op jit(solution)/shard_map/ppermute | solution.py:406
  26.3 4.3 %collective-permute-start.4 = (bf16[16,1024]{1,0:T(8,128)(2,1)S(1)}, bf16[16,1024]{1,0:T(8,128)(2,1)S(1)}, u32[]{:S(2)}, u32[]{:S(2)}) collective-permute-start(bf16[16,1024]{1,0:T(8,128)(2,1)S(1)} %convert_element_type.36), channel_id=1, source_target_pairs={{0,4},{2,6},{4,0},{6,2},{1,5},{3,7},{5,1},{7,3},{8,12},{10,14},{12... | collective-permute-start | bytes 98312 | tf_op jit(solution)/shard_map/ppermute | solution.py:406
  26.8 4.1 %collective-permute-start.3 = (bf16[16,1024]{1,0:T(8,128)(2,1)S(1)}, bf16[16,1024]{1,0:T(8,128)(2,1)S(1)}, u32[]{:S(2)}, u32[]{:S(2)}) collective-permute-start(bf16[16,1024]{1,0:T(8,128)(2,1)S(1)} %convert_element_type.36), channel_id=1, source_target_pairs={{0,2},{2,4},{4,6},{6,0},{1,3},{3,5},{5,7},{7,1},{8,10},{10,12},{12... | collective-permute-start | bytes 98312 | tf_op jit(solution)/shard_map/ppermute | solution.py:406
  30.9 3.8 %collective-permute-start.8 = (bf16[16,1024]{1,0:T(8,128)(2,1)S(1)}, bf16[16,1024]{1,0:T(8,128)(2,1)S(1)}, u32[]{:S(2)}, u32[]{:S(2)}) collective-permute-start(bf16[16,1024]{1,0:T(8,128)(2,1)S(1)} %get-tuple-element.39), channel_id=1, source_target_pairs={{0,24},{8,0},{16,8},{24,16},{1,25},{9,1},{17,9},{25,17},{2,26},{10... | collective-permute-start | bytes 98312 | tf_op jit(solution)/shard_map/ppermute | solution.py:406
  33.7 4.3 %collective-permute-start.7 = (bf16[16,1024]{1,0:T(8,128)(2,1)S(1)}, bf16[16,1024]{1,0:T(8,128)(2,1)S(1)}, u32[]{:S(2)}, u32[]{:S(2)}) collective-permute-start(bf16[16,1024]{1,0:T(8,128)(2,1)S(1)} %get-tuple-element.39), channel_id=1, source_target_pairs={{0,16},{8,24},{16,0},{24,8},{1,17},{9,25},{17,1},{25,9},{2,18},{10... | collective-permute-start | bytes 98312 | tf_op jit(solution)/shard_map/ppermute | solution.py:406
  34.0 4.3 %collective-permute-start.6 = (bf16[16,1024]{1,0:T(8,128)(2,1)S(1)}, bf16[16,1024]{1,0:T(8,128)(2,1)S(1)}, u32[]{:S(2)}, u32[]{:S(2)}) collective-permute-start(bf16[16,1024]{1,0:T(8,128)(2,1)S(1)} %get-tuple-element.39), channel_id=1, source_target_pairs={{0,8},{8,16},{16,24},{24,0},{1,9},{9,17},{17,25},{25,1},{2,10},{10... | collective-permute-start | bytes 98312 | tf_op jit(solution)/shard_map/ppermute | solution.py:406
  38.4 4.7 %collective-permute-start.11 = (bf16[16,1024]{1,0:T(8,128)(2,1)S(1)}, bf16[16,1024]{1,0:T(8,128)(2,1)S(1)}, u32[]{:S(2)}, u32[]{:S(2)}) collective-permute-start(bf16[16,1024]{1,0:T(8,128)(2,1)S(1)} %fusion.14), channel_id=1, source_target_pairs={{0,96},{32,0},{64,32},{96,64},{1,97},{33,1},{65,33},{97,65},{2,98}... | collective-permute-start | bytes 98312 | tf_op jit(solution)/shard_map/ppermute | solution.py:406
  42.1 4.3 %collective-permute-start.10 = (bf16[16,1024]{1,0:T(8,128)(2,1)S(1)}, bf16[16,1024]{1,0:T(8,128)(2,1)S(1)}, u32[]{:S(2)}, u32[]{:S(2)}) collective-permute-start(bf16[16,1024]{1,0:T(8,128)(2,1)S(1)} %fusion.14), channel_id=1, source_target_pairs={{0,64},{32,96},{64,0},{96,32},{1,65},{33,97},{65,1},{97,33},{2,66}... | collective-permute-start | bytes 98312 | tf_op jit(solution)/shard_map/ppermute | solution.py:406
  42.1 4.3 %collective-permute-start.9 = (bf16[16,1024]{1,0:T(8,128)(2,1)S(1)}, bf16[16,1024]{1,0:T(8,128)(2,1)S(1)}, u32[]{:S(2)}, u32[]{:S(2)}) collective-permute-start(bf16[16,1024]{1,0:T(8,128)(2,1)S(1)} %fusion.14), channel_id=1, source_target_pairs={{0,32},{32,64},{64,96},{96,0},{1,33},{33,65},{65,97},{97,1},{2,34}... | collective-permute-start | bytes 98312 | tf_op jit(solution)/shard_map/ppermute | solution.py:406
  49.9 7.1 %collective-permute-start.13 = (bf16[512,1024]{1,0:T(8,128)(2,1)S(1)}, bf16[512,1024]{1,0:T(8,128)(2,1)S(1)}, u32[]{:S(2)}, u32[]{:S(2)}) collective-permute-start(bf16[512,1024]{1,0:T(8,128)(2,1)S(1)} %hidden.1.hidden_ref), channel_id=1, source_target_pairs={{0,1},{1,0},{2,3},{3,2},{4,5},{5,4},{6,7},{7,6},{8,9},{9,8},{10,11... | collective-permute-start | bytes 3145736 | tf_op jit(solution)/shard_map/ppermute | solution.py:395
where the time goes:
time: 60 us; the launch traced here: 59.8 us
  Pallas kernels  24.4 us (41%)
  starting transfers between devices  21.7 us (36%)
  waiting for transfers between devices  12.4 us (21%)
  local copies, waits for them, and re-layouts  0.78 us (1%)
    pallas_call x1, Pallas kernels, front_call(): pl.pallas_call(front_kernel, in_specs=[pl.BlockSpec(memory_space=pltpu.SM...  13.1 us
    ppermute x9, starting transfers between devices, round_the_ring(): lax.ppermute(sent, axis, [(i, (i + k) % RING) for i in range(RING)])  11.6 us
    ppermute x9, waiting for transfers between devices, round_the_ring(): lax.ppermute(sent, axis, [(i, (i + k) % RING) for i in range(RING)])  11.2 us
    ppermute x4, starting transfers between devices, swapped(): return lax.ppermute(x, 'ch', [(0, 1), (1, 0)])  6.93 us
    pallas_call x1, Pallas kernels, hidden_call(): pl.pallas_call(hidden_kernel, in_specs=[vmem] * 5, out_specs=vmem, out_sh...  3.41 us
    pallas_call x1, Pallas kernels, stage_call(): pl.pallas_call(stage_kernel, in_specs=[pl.BlockSpec(memory_space=pltpu.SM...  3.37 us
    ppermute x1, starting transfers between devices, from_before(): return lax.ppermute(x, SEQ, [(i, i + 1) for i in range(count - 1)])  3.19 us
    pallas_call x1, Pallas kernels, output_call(): pl.pallas_call(output_kernel, in_specs=[vmem] * 3, out_specs=pl.BlockSpec...  2.57 us
  transfers between devices with their start and end apart: 14, of which 10 were waited for; matrix products, arithmetic and copies ran while one was open for 2% of the time, Pallas kernels for 36%

commit v1 on v0

--- a/solution.py
+++ b/solution.py
@@ -10,7 +10,6 @@
 LANES = 128
 HISTORY = 8
 WIDTH = 256
-AHEAD = 2
 SEQ = ("z", "y", "x")
 RING = 4
 F32 = jnp.float32
@@ -57,7 +56,7 @@
         (own_ref, lhs_out.at[:, pl.ds(mine, half)]),
         (other_ref, lhs_out.at[:, pl.ds(theirs, half)]),
         (filt_ref, filt_out),
-        (w_ref.at[:, :, pl.ds(0, w_out.shape[2])], w_out),
+        (w_ref.at[pl.ds(1, w_out.shape[0])], w_out),
     ]
     copies = [pltpu.make_async_copy(src, dst, sems.at[i]) for i, (src, dst) in enumerate(pairs)]
     for copy in copies:
@@ -95,7 +94,7 @@
         out_specs=[vmem] * 6,
         out_shape=[
             pltpu.VMEM((rows, 2 * half), BF16),
-            pltpu.VMEM((*weight.shape[:2], AHEAD * WIDTH), BF16),
+            pltpu.VMEM((weight.shape[0] - 1, *weight.shape[1:]), BF16),
             pltpu.VMEM(filt.shape, F32),
             pltpu.VMEM(rates.shape, F32),
             pltpu.VMEM((len(SEQ) * (RING - 1), *rates.shape), F32),
@@ -107,73 +106,83 @@
     )(where, inputs[0], other, *inputs[1:])
 
 
+def hold_segments(held, part, first, per):
+    steps = held.shape[1] // SEGS - HISTORY
+    pitch = steps + HISTORY
+    for l in range(WIDTH // LANES):
+        lanes = slice(l * LANES, (l + 1) * LANES)
+        for g in range(first, first + per):
+            row = (g - first) * steps + (0 if first else HALO)
+            held[l, g * pitch + HISTORY : (g + 1) * pitch] = part[row : row + steps, lanes]
+            if g == 0:
+                held[l, :HISTORY] = part[row - HISTORY : row, lanes]
+            if g + 1 < SEGS:
+                held[l, (g + 1) * pitch : (g + 1) * pitch + HISTORY] = part[
+                    row + steps - HISTORY : row + steps, lanes
+                ]
+
+
+def join_halo(where_ref, halo_ref, own_ref, other_ref):
+    half = own_ref.shape[1]
+    core = lax.rem(where_ref[0], 2)
+    halo_ref[:, pl.ds(pl.multiple_of(core * half, half), half)] = own_ref[...]
+    halo_ref[:, pl.ds(pl.multiple_of((1 - core) * half, half), half)] = other_ref[...]
+
+
+def segment_rows(lhs_ref, halo_ref, first, per):
+    steps = lhs_ref.shape[0] // SEGS
+    rows = lhs_ref[first * steps : (first + per) * steps]
+    return rows if first else jnp.concatenate([halo_ref[...], rows], axis=0)
+
+
 def front_kernel(
     where_ref,
     lhs_ref,
     halo_own_ref,
     halo_other_ref,
-    ahead_ref,
     w_ref,
+    wq_ref,
     filt_ref,
     rates_ref,
     gain_ref,
-    pair_ref,
+    local_ref,
     ends_ref,
     total_ref,
+    staged_ref,
     halo_ref,
-    rest_ref,
     proj_a,
     proj_b,
     sem,
 ):
     rows = lhs_ref.shape[0]
-    half = halo_own_ref.shape[1]
     steps = rows // SEGS
     pitch = steps + HISTORY
     modes = rates_ref.shape[0]
     streams = w_ref.shape[0]
     tiles = w_ref.shape[2] // WIDTH
-    parts_of_rows = 2
-    per = SEGS // parts_of_rows
+    per = SEGS // 2
     proj = (proj_a, proj_b)
 
-    rest = pltpu.make_async_copy(
-        w_ref.at[:, :, pl.ds(AHEAD * WIDTH, (tiles - AHEAD) * WIDTH)], rest_ref, sem
-    )
-    rest.start()
-    core = lax.rem(where_ref[0], 2)
-    halo_ref[:, pl.ds(pl.multiple_of(core * half, half), half)] = halo_own_ref[...]
-    halo_ref[:, pl.ds(pl.multiple_of((1 - core) * half, half), half)] = halo_other_ref[...]
+    stage = pltpu.make_async_copy(wq_ref.at[0], staged_ref, sem)
+    stage.start()
+    join_halo(where_ref, halo_ref, halo_own_ref, halo_other_ref)
 
     def projection(tile):
         held = proj[tile % 2]
-        weights, column = (ahead_ref, tile) if tile < AHEAD else (rest_ref, tile - AHEAD)
-        if tile == AHEAD:
-            rest.wait()
-
-        def piece(j, m):
-            first = m * per
-            lhs = lhs_ref[first * steps : (first + per) * steps]
-            if m == 0:
-                lhs = jnp.concatenate([halo_ref[...], lhs], axis=0)
+
+        def piece(j, first):
             part = jnp.dot(
-                lhs,
-                weights[j, :, column * WIDTH : (column + 1) * WIDTH],
+                segment_rows(lhs_ref, halo_ref, first, per),
+                w_ref[j, :, tile * WIDTH : (tile + 1) * WIDTH],
                 preferred_element_type=F32,
             )
-            for l in range(WIDTH // LANES):
-                lanes = slice(l * LANES, (l + 1) * LANES)
-                for g in range(first, first + per):
-                    row = (g - first) * steps + (0 if m else HALO)
-                    held[j, l, g * pitch + HISTORY : (g + 1) * pitch] = part[row : row + steps, lanes]
-                    if g == 0:
-                        held[j, l, :HISTORY] = part[row - HISTORY : row, lanes]
-                    if g + 1 < SEGS:
-                        held[j, l, (g + 1) * pitch : (g + 1) * pitch + HISTORY] = part[
-                            row + steps - HISTORY : row + steps, lanes
-                        ]
-
-        return [lambda j=j, m=m: piece(j, m) for j in range(streams) for m in range(parts_of_rows)]
+            hold_segments(held.at[j], part, first, per)
+
+        return [
+            lambda j=j, first=first: piece(j, first)
+            for j in range(streams)
+            for first in range(0, SEGS, per)
+        ]
 
     def recurrence(tile, size=4):
         held = proj[tile % 2]
@@ -187,7 +196,8 @@
 
             def begin(kept=kept, lanes=lanes, at=at):
                 kept["taps"] = [
-                    [spread(filt_ref[a, j : j + 1, lanes]) for a in range(3)] for j in range(streams)
+                    [spread(filt_ref[a, j + 1 : j + 2, lanes]) for a in range(3)]
+                    for j in range(streams)
                 ]
                 kept["decay"] = [spread(jnp.exp(-rates_ref[n : n + 1, lanes])) for n in range(modes)]
                 kept["gain"] = [spread(gain_ref[n : n + 1, lanes]) for n in range(modes)]
@@ -198,16 +208,14 @@
             def advance(t0, kept=kept, lanes=lanes, at=at):
                 for t in range(t0, t0 + size):
                     now = [at(j, t) for j in range(streams)]
-                    q, k, v = [
+                    k, v = [
                         filtered_step(*terms)
                         for terms in zip(kept["taps"], now, kept["one"], kept["two"])
                     ]
                     kept["one"], kept["two"] = now, kept["one"]
                     source = k * v
                     kept["state"] = [d * s + source for d, s in zip(kept["decay"], kept["state"])]
-                    row = slice(t * SEGS, (t + 1) * SEGS)
-                    pair_ref[0, row, lanes] = q
-                    pair_ref[1, row, lanes] = tree_sum(
+                    local_ref[t * SEGS : (t + 1) * SEGS, lanes] = tree_sum(
                         [g * s for g, s in zip(kept["gain"], kept["state"])]
                     )
 
@@ -236,11 +244,12 @@
             for step in fast[done:upto]:
                 step()
             done = upto
-
-
-def front_call(where, lhs, halo_own, halo_other, ahead, weight, filt, rates, gain):
+    stage.wait()
+
+
+def front_call(where, lhs, halo_own, halo_other, staged, weight, filt, rates, gain):
     rows, full = lhs.shape
-    streams, _, channels = weight.shape
+    streams, _, channels = staged.shape
     modes = rates.shape[0]
     vmem = pl.BlockSpec(memory_space=pltpu.VMEM)
     held = pltpu.VMEM((streams, WIDTH // LANES, rows + SEGS * HISTORY, LANES), F32)
@@ -250,27 +259,22 @@
         + [vmem] * 4
         + [pl.BlockSpec(memory_space=pl.ANY)]
         + [vmem] * 3,
-        out_specs=[vmem] * 3,
+        out_specs=[vmem] * 4,
         out_shape=[
-            pltpu.VMEM((2, rows, channels), F32),
+            pltpu.VMEM((rows, channels), F32),
             pltpu.VMEM((modes * SEGS, channels), F32),
             pltpu.VMEM((modes, channels), F32),
+            pltpu.VMEM((full, channels), BF16),
         ],
-        scratch_shapes=[
-            pltpu.VMEM((HALO, full), BF16),
-            pltpu.VMEM((streams, full, channels - AHEAD * WIDTH), BF16),
-            held,
-            held,
-            pltpu.SemaphoreType.DMA,
-        ],
-        compiler_params=pltpu.CompilerParams(vmem_limit_bytes=18 * MIB),
+        scratch_shapes=[pltpu.VMEM((HALO, full), BF16), held, held, pltpu.SemaphoreType.DMA],
+        compiler_params=pltpu.CompilerParams(vmem_limit_bytes=10 * MIB),
         name="front",
     )(
         where,
         lhs,
         halo_own,
         halo_other,
-        ahead,
+        staged,
         pltpu.with_memory_space_constraint(weight, pltpu.HBM),
         filt,
         rates,
@@ -278,8 +282,60 @@
     )
 
 
-def hidden_kernel(ends_ref, into_ref, pair_ref, rates_ref, gain_ref, hidden_ref):
-    _, rows, channels = pair_ref.shape
+def query_kernel(where_ref, lhs_ref, halo_own_ref, halo_other_ref, w_ref, filt_ref, query_ref, halo_ref, held):
+    steps = lhs_ref.shape[0] // SEGS
+    pitch = steps + HISTORY
+    per = SEGS // 2
+    join_halo(where_ref, halo_ref, halo_own_ref, halo_other_ref)
+    for tile in range(w_ref.shape[1] // WIDTH):
+        for first in range(0, SEGS, per):
+            part = jnp.dot(
+                segment_rows(lhs_ref, halo_ref, first, per),
+                w_ref[:, tile * WIDTH : (tile + 1) * WIDTH],
+                preferred_element_type=F32,
+            )
+            hold_segments(held.at[tile], part, first, per)
+        for l in range(WIDTH // LANES):
+            lanes = slice(tile * WIDTH + l * LANES, tile * WIDTH + (l + 1) * LANES)
+            taps = [spread(filt_ref[a, 0:1, lanes]) for a in range(3)]
+
+            def at(t, tile=tile, l=l):
+                return held[tile, l, pl.ds(HISTORY + t, SEGS, stride=pitch), :]
+
+            one, two = at(-1), at(-2)
+            for t in range(steps):
+                now = at(t)
+                query_ref[t * SEGS : (t + 1) * SEGS, lanes] = filtered_step(taps, now, one, two)
+                one, two = now, one
+
+
+def query_call(where, lhs, halo_own, halo_other, weight, filt):
+    rows, full = lhs.shape
+    channels = weight.shape[1]
+    vmem = pl.BlockSpec(memory_space=pltpu.VMEM)
+    args = [
+        pltpu.with_memory_space_constraint(x, pltpu.VMEM)
+        for x in (lhs, halo_own, halo_other, weight, filt)
+    ]
+    return pl.pallas_call(
+        query_kernel,
+        in_specs=[pl.BlockSpec(memory_space=pltpu.SMEM)] + [vmem] * 5,
+        out_specs=vmem,
+        out_shape=pltpu.VMEM((rows, channels), F32),
+        scratch_shapes=[
+            pltpu.VMEM((HALO, full), BF16),
+            pltpu.VMEM((channels // WIDTH, WIDTH // LANES, rows + SEGS * HISTORY, LANES), F32),
+        ],
+        compiler_params=pltpu.CompilerParams(vmem_limit_bytes=6 * MIB),
+        cost_estimate=pl.CostEstimate(
+            flops=2 * (rows + HALO) * full * channels, transcendentals=0, bytes_accessed=0
+        ),
+        name="query",
+    )(where, *args)
+
+
+def hidden_kernel(ends_ref, into_ref, local_ref, query_ref, rates_ref, gain_ref, hidden_ref):
+    rows, channels = local_ref.shape
     steps = rows // SEGS
     modes = rates_ref.shape[0]
     seg = lax.broadcasted_iota(jnp.int32, (SEGS, LANES), 0)
@@ -301,7 +357,7 @@
             for u in range(2):
                 row = pl.ds(pl.multiple_of((2 * t + u) * SEGS, SEGS), SEGS)
                 leads = tuple(d * s for d, s in zip(decays, leads))
-                halves.append(pair_ref[0, row, lanes] * (pair_ref[1, row, lanes] + tree_sum(leads)))
+                halves.append(query_ref[row, lanes] * (local_ref[row, lanes] + tree_sum(leads)))
             row = pl.ds(pl.multiple_of(2 * t * SEGS, 2 * SEGS), 2 * SEGS)
             hidden_ref[row, lanes] = jnp.concatenate(halves, axis=0).astype(BF16)
             return leads
@@ -309,14 +365,17 @@
         lax.fori_loop(0, steps // 2, body, tuple(leads), unroll=8)
 
 
-def hidden_call(ends, into, pair, rates, gain):
+def hidden_call(ends, into, local, query, rates, gain):
     vmem = pl.BlockSpec(memory_space=pltpu.VMEM)
-    args = [pltpu.with_memory_space_constraint(x, pltpu.VMEM) for x in (ends, into, pair, rates, gain)]
+    args = [
+        pltpu.with_memory_space_constraint(x, pltpu.VMEM)
+        for x in (ends, into, local, query, rates, gain)
+    ]
     return pl.pallas_call(
         hidden_kernel,
-        in_specs=[vmem] * 5,
+        in_specs=[vmem] * 6,
         out_specs=vmem,
-        out_shape=pltpu.VMEM(pair.shape[1:], BF16),
+        out_shape=pltpu.VMEM(local.shape, BF16),
         compiler_params=pltpu.CompilerParams(vmem_limit_bytes=4 * MIB),
         name="hidden",
     )(*args)
@@ -403,7 +462,7 @@
 def round_the_ring(state, axis):
     sent = state.astype(BF16)
     return [
-        lax.ppermute(sent, axis, [(i, (i + k) % RING) for i in range(RING)]).astype(F32)
+        lax.ppermute(sent, axis, [(i, (i + k) % RING) for i in range(RING)])
         for k in range(1, RING)
     ]
 
@@ -416,28 +475,32 @@
     gain = residues.T * jnp.sqrt(1.0 - jnp.exp(-2.0 * rates))
 
     halo_own = from_before(tokens[rows - HALO :])
-    lhs, ahead, filt, rates, into_weights, total_weights = stage_call(
+    lhs, staged, filt, rates, into_weights, total_weights = stage_call(
         where, tokens, swapped(tokens), weight, short_filter, rates
     )
     halo_own, lhs, out_weight = lax.optimization_barrier((halo_own, lhs, out_weight))
     halo_other = swapped(halo_own)
     lhs, halo_other, out_weight = lax.optimization_barrier((lhs, halo_other, out_weight))
     out_weight_other = swapped(out_weight)
-    pair, ends, total = front_call(
-        where, lhs, halo_own, halo_other, ahead, weight, filt, rates, gain
+    local, ends, total, query_weight = front_call(
+        where, lhs, halo_own, halo_other, staged, weight, filt, rates, gain
     )
+    query = query_call(where, lhs, halo_own, halo_other, query_weight, filt)
 
     into = 0.0
     for level, axis in enumerate(reversed(SEQ)):
         arrived = round_the_ring(total, axis)
+        if level == 0:
+            query, *arrived = lax.optimization_barrier((query, *arrived))
         total = total_weights[RING * level] * total
         for k, part in enumerate(arrived):
+            part = part.astype(F32)
             into = into + into_weights[(RING - 1) * level + k] * part
             total = total + total_weights[RING * level + k + 1] * part
 
-    hidden = hidden_call(ends, into, pair, rates, gain)
-    part, staged = product_call(where, hidden, out_weight, out_weight_other)
-    return output_call(part, swapped(hidden), staged)
+    hidden = hidden_call(ends, into, local, query, rates, gain)
+    part, partner_weight = product_call(where, hidden, out_weight, out_weight_other)
+    return output_call(part, swapped(hidden), partner_weight)
 
 
 def solution(mesh):

time: 60 us -> 56.8 us (0.947)
  waiting for transfers between devices: 12.4 us -> 9.39 us
    pallas_call x1, Pallas kernels: 13.1 us -> 9.39 us  [front_call(): pl.pallas_call(front_kernel, in_specs=[pl.BlockSpec(memory_space=pltpu.SM...]
    ppermute x9, waiting for transfers between devices: 11.2 us -> 8.14 us  [round_the_ring(): lax.ppermute(sent, axis, [(i, (i + k) % RING) for i in range(RING)])]
    pallas_call x1 -> x2, Pallas kernels: 3.41 us -> 6.37 us  [the longest x1 3.48 us: hidden_call(): pl.pallas_call(hidden_kernel, in_specs=[vmem] * 6, out_specs=vmem, out_sh...]
  transfers between devices with their start and end apart: 14 -> 14, of which waited for: 10 -> 9; matrix products, arithmetic and copies ran while one was open for 2% -> 2% of each run, Pallas kernels for 36% -> 38%
where the time goes in v1:
time: 56.8 us; the launch traced here: 56.6 us
  Pallas kernels  24.3 us (43%)
  starting transfers between devices  21.7 us (38%)
  waiting for transfers between devices  9.39 us (17%)
  local copies, waits for them, and re-layouts  0.78 us (1%)
    ppermute x9, starting transfers between devices, round_the_ring(): lax.ppermute(sent, axis, [(i, (i + k) % RING) for i in range(RING)])  11.8 us
    pallas_call x1, Pallas kernels, front_call(): pl.pallas_call(front_kernel, in_specs=[pl.BlockSpec(memory_space=pltpu.SM...  9.39 us
    ppermute x9, waiting for transfers between devices, round_the_ring(): lax.ppermute(sent, axis, [(i, (i + k) % RING) for i in range(RING)])  8.14 us
    ppermute x4, starting transfers between devices, swapped(): return lax.ppermute(x, 'ch', [(0, 1), (1, 0)])  6.74 us
    pallas_call x1, Pallas kernels, stage_call(): pl.pallas_call(stage_kernel, in_specs=[pl.BlockSpec(memory_space=pltpu.SM...  3.96 us
    pallas_call x1, Pallas kernels, hidden_call(): pl.pallas_call(hidden_kernel, in_specs=[vmem] * 6, out_specs=vmem, out_sh...  3.48 us
    ppermute x1, starting transfers between devices, from_before(): return lax.ppermute(x, SEQ, [(i, i + 1) for i in range(count - 1)])  3.19 us
    pallas_call x1, Pallas kernels, query_call(): pl.pallas_call(query_kernel, in_specs=[pl.BlockSpec(memory_space=pltpu.SM...  2.89 us
  transfers between devices with their start and end apart: 14, of which 9 were waited for; matrix products, arithmetic and copies ran while one was open for 2% of the time, Pallas kernels for 38%

profile of v1, /device:TPU:1, one launch (start us, length us, event | category | flops | bytes accessed | tf_op | source)
XLA Modules:
  0.0 56.6 jit_solution(4768827610341067209)
XLA Ops:
  0.0 1.4 %collective-permute-start.1 = (bf16[512,1024]{1,0:T(8,128)(2,1)}, bf16[512,1024]{1,0:T(8,128)(2,1)S(1)}, u32[]{:S(2)}, u32[]{:S(2)}) collective-permute-start(bf16[512,1024]{1,0:T(8,128)(2,1)} %own_ref.1), channel_id=1, source_target_pairs={{0,1},{1,0},{2,3},{3,2},{4,5},{5,4},{6,7},{7,6},{8,9},{9,8},{10,11... | collective-permute-start | bytes 3145736 | tf_op jit(solution)/shard_map/ppermute | solution.py:454
  1.4 0.8 %slice.54 = bf16[16,1024]{1,0:T(8,128)(2,1)S(1)} slice(bf16[512,1024]{1,0:T(8,128)(2,1)} %own_ref.1), slice={[496:512], [0:1024]} | slice | bytes 65536 | tf_op jit(solution)/shard_map/slice | solution.py:477
  2.2 3.2 %collective-permute-start = (bf16[16,1024]{1,0:T(8,128)(2,1)S(1)}, bf16[16,1024]{1,0:T(8,128)(2,1)S(1)}, u32[]{:S(2)}, u32[]{:S(2)}) collective-permute-start(bf16[16,1024]{1,0:T(8,128)(2,1)S(1)} %slice.54), channel_id=1, source_target_pairs={{0,2},{2,4},{4,6},{6,8},{8,10},{10,12},{12,14},{14,16},{16,18},{18... | collective-permute-start | bytes 98312 | tf_op jit(solution)/shard_map/ppermute | solution.py:459
  5.4 4.0 %stage.1 = (bf16[512,2048]{1,0:T(8,128)(2,1)S(1)}, bf16[2,2048,1024]{2,1,0:T(8,128)(2,1)S(1)}, f32[3,3,1024]{2,1,0:T(4,128)S(1)}, f32[16,1024]{1,0:T(8,128)S(1)}...) custom-call(s32[1]{0:T(128)} %bitcast.where_ref, bf16[512,1024]{1,0:T(8,128)(2,1)} %own_ref.1, ...), custom_call_target="tpu_custom_call" | custom-call | tf_op jit(solution)/shard_map/stage/pallas_call | solution.py:91
  9.4 0.4 collective-permute-start.2
  9.8 0.9 %collective-permute-done.2.halo_other_ref = bf16[16,1024]{1,0:T(8,128)(2,1)S(1)} collective-permute-done((bf16[16,1024]{1,0:T(8,128)(2,1)S(1)}, bf16[16,1024]{1,0:T(8,128)(2,1)S(1)}, u32[]{:S(2)}, u32[]{:S(2)}) %collective-permute-start.2) | collective-permute-done | bytes 32800 | tf_op jit(solution)/shard_map/ppermute | solution.py:454
  10.7 0.3 collective-permute-start.12
  11.0 9.4 %front.1 = (f32[512,1024]{1,0:T(8,128)S(1)}, f32[128,1024]{1,0:T(8,128)S(1)}, f32[16,1024]{1,0:T(8,128)S(1)}, bf16[2048,1024]{1,0:T(8,128)(2,1)S(1)}) custom-call(s32[1]{0:T(128)} %bitcast.where_ref, bf16[512,2048]{1,0:T(8,128)(2,1)S(1)} %get-tuple-element.31.lhs_ref, bf16[16,1024]{1,0:T(8,128)(2,1)S(1)} %collective-permute-done.halo_own_ref, ...), custom_call_target="tpu_custom_call" | custom-call | tf_op jit(solution)/shard_map/front/pallas_call | solution.py:256
  20.4 2.5 %collective-permute-start.5 = (bf16[16,1024]{1,0:T(8,128)(2,1)S(1)}, bf16[16,1024]{1,0:T(8,128)(2,1)S(1)}, u32[]{:S(2)}, u32[]{:S(2)}) collective-permute-start(bf16[16,1024]{1,0:T(8,128)(2,1)S(1)} %convert_element_type.36), channel_id=1, source_target_pairs={{0,6},{2,0},{4,2},{6,4},{1,7},{3,1},{5,3},{7,5},{8,14},{10,8},{12,... | collective-permute-start | bytes 98312 | tf_op jit(solution)/shard_map/ppermute | solution.py:465
  23.0 0.5 collective-permute-start.4
  23.5 0.3 collective-permute-start.3
  23.8 2.9 %query.1.query_ref = f32[512,1024]{1,0:T(8,128)S(1)} custom-call(s32[1]{0:T(128)} %bitcast.where_ref, bf16[512,2048]{1,0:T(8,128)(2,1)S(1)} %get-tuple-element.31.lhs_ref, bf16[16,1024]{1,0:T(8,128)(2,1)S(1)} %collective-permute-done.halo_own_ref, bf16[16,1024]{1,0:T(8,128)(2,1)S(1)} %collective-permute-done.2.halo_other_ref, ...), custom_call_target="tpu_custom_call" | custom-call | flops 2214592512 | tf_op jit(solution)/shard_map/query/pallas_call | solution.py:320
  26.7 0.5 collective-permute-done.4
  27.3 0.3 collective-permute-done.3
  27.7 2.8 %collective-permute-start.8 = (bf16[16,1024]{1,0:T(8,128)(2,1)S(1)}, bf16[16,1024]{1,0:T(8,128)(2,1)S(1)}, u32[]{:S(2)}, u32[]{:S(2)}) collective-permute-start(bf16[16,1024]{1,0:T(8,128)(2,1)S(1)} %get-tuple-element.49), channel_id=1, source_target_pairs={{0,24},{8,0},{16,8},{24,16},{1,25},{9,1},{17,9},{25,17},{2,26},{10... | collective-permute-start | bytes 98312 | tf_op jit(solution)/shard_map/ppermute | solution.py:465
  30.5 0.3 collective-permute-start.7
  30.8 0.6 collective-permute-start.6
  31.4 0.1 collective-permute-done.8
  31.5 3.3 %collective-permute-done.7 = bf16[16,1024]{1,0:T(8,128)(2,1)S(1)} collective-permute-done((bf16[16,1024]{1,0:T(8,128)(2,1)S(1)}, bf16[16,1024]{1,0:T(8,128)(2,1)S(1)}, u32[]{:S(2)}, u32[]{:S(2)}) %collective-permute-start.7) | collective-permute-done | bytes 32800 | tf_op jit(solution)/shard_map/ppermute | solution.py:465
  34.8 0.3 collective-permute-done.6
  35.1 3.7 %collective-permute-start.11 = (bf16[16,1024]{1,0:T(8,128)(2,1)S(1)}, bf16[16,1024]{1,0:T(8,128)(2,1)S(1)}, u32[]{:S(2)}, u32[]{:S(2)}) collective-permute-start(bf16[16,1024]{1,0:T(8,128)(2,1)S(1)} %fusion.14), channel_id=1, source_target_pairs={{0,96},{32,0},{64,32},{96,64},{1,97},{33,1},{65,33},{97,65},{2,98}... | collective-permute-start | bytes 98312 | tf_op jit(solution)/shard_map/ppermute | solution.py:465
  38.8 0.2 collective-permute-start.10
  39.0 0.8 %collective-permute-start.9 = (bf16[16,1024]{1,0:T(8,128)(2,1)S(1)}, bf16[16,1024]{1,0:T(8,128)(2,1)S(1)}, u32[]{:S(2)}, u32[]{:S(2)}) collective-permute-start(bf16[16,1024]{1,0:T(8,128)(2,1)S(1)} %fusion.14), channel_id=1, source_target_pairs={{0,32},{32,64},{64,96},{96,0},{1,33},{33,65},{65,97},{97,1},{2,34}... | collective-permute-start | bytes 98312 | tf_op jit(solution)/shard_map/ppermute | solution.py:465
  39.8 0.1 collective-permute-done.11
  39.8 3.4 %collective-permute-done.10 = bf16[16,1024]{1,0:T(8,128)(2,1)S(1)} collective-permute-done((bf16[16,1024]{1,0:T(8,128)(2,1)S(1)}, bf16[16,1024]{1,0:T(8,128)(2,1)S(1)}, u32[]{:S(2)}, u32[]{:S(2)}) %collective-permute-start.10) | collective-permute-done | bytes 32800 | tf_op jit(solution)/shard_map/ppermute | solution.py:465
  43.2 0.2 collective-permute-done.9
  43.3 0.1 fusion.7.into_ref
  43.4 3.5 %hidden.1.hidden_ref = bf16[512,1024]{1,0:T(8,128)(2,1)S(1)} custom-call(f32[128,1024]{1,0:T(8,128)S(1)} %get-tuple-element.36.ends_ref, f32[16,1024]{1,0:T(8,128)S(1)} %fusion.7.into_ref, f32[512,1024]{1,0:T(8,128)S(1)} %get-tuple-element.44.local_ref, f32[512,1024]{1,0:T(8,128)S(1)} %query.1.query_ref, f32[16,1024]{1,0:T(8,128)S(1)} %get-tuple-element.35.rates_ref, ...), custom_call_target="tpu_custom_call" | custom-call | tf_op jit(solution)/shard_map/hidden/pallas_call | solution.py:374
  46.9 4.7 %collective-permute-start.13 = (bf16[512,1024]{1,0:T(8,128)(2,1)S(1)}, bf16[512,1024]{1,0:T(8,128)(2,1)S(1)}, u32[]{:S(2)}, u32[]{:S(2)}) collective-permute-start(bf16[512,1024]{1,0:T(8,128)(2,1)S(1)} %hidden.1.hidden_ref), channel_id=1, source_target_pairs={{0,1},{1,0},{2,3},{3,2},{4,5},{5,4},{6,7},{7,6},{8,9},{9,8},{10,11... | collective-permute-start | bytes 3145736 | tf_op jit(solution)/shard_map/ppermute | solution.py:454
  51.6 2.0 %product.1 = (f32[512,1024]{1,0:T(8,128)S(1)}, bf16[1024,1024]{1,0:T(8,128)(2,1)S(1)}) custom-call(s32[1]{0:T(128)} %bitcast.where_ref, bf16[512,1024]{1,0:T(8,128)(2,1)S(1)} %hidden.1.hidden_ref, bf16[1024,2048]{1,0:T(8,128)(2,1)S(1)} %copy-done, bf16[1024,2048]{1,0:T(8,128)(2,1)S(1)} %collective-permute-done.12.w_other_ref), custom_call_target="tpu_custom_call" | custom-call | tf_op jit(solution)/shard_map/product/pallas_call | solution.py:401
  53.5 0.3 collective-permute-done.13.other_ref
  53.9 2.6 %output.1 = f32[512,1024]{1,0:T(8,128)} custom-call(f32[512,1024]{1,0:T(8,128)S(1)} %get-tuple-element.47.part_ref, bf16[512,1024]{1,0:T(8,128)(2,1)S(1)} %collective-permute-done.13.other_ref, bf16[1024,1024]{1,0:T(8,128)(2,1)S(1)} %get-tuple-element.48.w_ref), custom_call_target="tpu_custom_call" | custom-call | tf_op jit(solution)/shard_map/output/pallas_call | solution.py:438
  (14 shorter events, 0.1 us)
Async XLA Ops:
  0.0 5.4 %collective-permute-start.1 = (bf16[512,1024]{1,0:T(8,128)(2,1)}, bf16[512,1024]{1,0:T(8,128)(2,1)S(1)}, u32[]{:S(2)}, u32[]{:S(2)}) collective-permute-start(bf16[512,1024]{1,0:T(8,128)(2,1)} %own_ref.1), channel_id=1, source_target_pairs={{0,1},{1,0},{2,3},{3,2},{4,5},{5,4},{6,7},{7,6},{8,9},{9,8},{10,11... | collective-permute-start | bytes 3145736 | tf_op jit(solution)/shard_map/ppermute | solution.py:454
  2.2 7.2 %collective-permute-start = (bf16[16,1024]{1,0:T(8,128)(2,1)S(1)}, bf16[16,1024]{1,0:T(8,128)(2,1)S(1)}, u32[]{:S(2)}, u32[]{:S(2)}) collective-permute-start(bf16[16,1024]{1,0:T(8,128)(2,1)S(1)} %slice.54), channel_id=1, source_target_pairs={{0,2},{2,4},{4,6},{6,8},{8,10},{10,12},{12,14},{14,16},{16,18},{18... | collective-permute-start | bytes 98312 | tf_op jit(solution)/shard_map/ppermute | solution.py:459
  5.4 5.3 %copy-start = (bf16[1024,2048]{1,0:T(8,128)(2,1)S(1)}, bf16[1024,2048]{1,0:T(8,128)(2,1)}, u32[]{:S(2)}) copy-start(bf16[1024,2048]{1,0:T(8,128)(2,1)} %w_ref) | copy-start | bytes 12582916
  5.4 5.6 %copy-start.1 = (f32[1024,16]{0,1:T(8,128)S(1)}, f32[1024,16]{0,1:T(8,128)}, u32[]{:S(2)}) copy-start(f32[1024,16]{0,1:T(8,128)} %param.10) | copy-start | bytes 196612
  5.4 5.6 %copy-start.2 = (f32[1024,16]{0,1:T(8,128)S(1)}, f32[1024,16]{0,1:T(8,128)}, u32[]{:S(2)}) copy-start(f32[1024,16]{0,1:T(8,128)} %param.9) | copy-start | bytes 196612
  9.4 1.3 %collective-permute-start.2 = (bf16[16,1024]{1,0:T(8,128)(2,1)S(1)}, bf16[16,1024]{1,0:T(8,128)(2,1)S(1)}, u32[]{:S(2)}, u32[]{:S(2)}) collective-permute-start(bf16[16,1024]{1,0:T(8,128)(2,1)S(1)} %collective-permute-done.halo_own_ref), channel_id=1, source_target_pairs={{0,1},{1,0},{2,3},{3,2},{4,5},{5,4},{6,7},{7,6},{8,9},{9,8},{10,11... | collective-permute-start | bytes 98312 | tf_op jit(solution)/shard_map/ppermute | solution.py:454
  10.7 40.9 %collective-permute-start.12 = (bf16[1024,2048]{1,0:T(8,128)(2,1)S(1)}, bf16[1024,2048]{1,0:T(8,128)(2,1)S(1)}, u32[]{:S(2)}, u32[]{:S(2)}) collective-permute-start(bf16[1024,2048]{1,0:T(8,128)(2,1)S(1)} %copy-done), channel_id=1, source_target_pairs={{0,1},{1,0},{2,3},{3,2},{4,5},{5,4},{6,7},{7,6},{8,9},{9,8},{10,11... | collective-permute-start | bytes 12582920 | tf_op jit(solution)/shard_map/ppermute | solution.py:454
  20.4 6.3 %collective-permute-start.5 = (bf16[16,1024]{1,0:T(8,128)(2,1)S(1)}, bf16[16,1024]{1,0:T(8,128)(2,1)S(1)}, u32[]{:S(2)}, u32[]{:S(2)}) collective-permute-start(bf16[16,1024]{1,0:T(8,128)(2,1)S(1)} %convert_element_type.36), channel_id=1, source_target_pairs={{0,6},{2,0},{4,2},{6,4},{1,7},{3,1},{5,3},{7,5},{8,14},{10,8},{12,... | collective-permute-start | bytes 98312 | tf_op jit(solution)/shard_map/ppermute | solution.py:465
  23.0 4.3 %collective-permute-start.4 = (bf16[16,1024]{1,0:T(8,128)(2,1)S(1)}, bf16[16,1024]{1,0:T(8,128)(2,1)S(1)}, u32[]{:S(2)}, u32[]{:S(2)}) collective-permute-start(bf16[16,1024]{1,0:T(8,128)(2,1)S(1)} %convert_element_type.36), channel_id=1, source_target_pairs={{0,4},{2,6},{4,0},{6,2},{1,5},{3,7},{5,1},{7,3},{8,12},{10,14},{12... | collective-permute-start | bytes 98312 | tf_op jit(solution)/shard_map/ppermute | solution.py:465
  23.5 4.1 %collective-permute-start.3 = (bf16[16,1024]{1,0:T(8,128)(2,1)S(1)}, bf16[16,1024]{1,0:T(8,128)(2,1)S(1)}, u32[]{:S(2)}, u32[]{:S(2)}) collective-permute-start(bf16[16,1024]{1,0:T(8,128)(2,1)S(1)} %convert_element_type.36), channel_id=1, source_target_pairs={{0,2},{2,4},{4,6},{6,0},{1,3},{3,5},{5,7},{7,1},{8,10},{10,12},{12... | collective-permute-start | bytes 98312 | tf_op jit(solution)/shard_map/ppermute | solution.py:465
  27.7 3.8 %collective-permute-start.8 = (bf16[16,1024]{1,0:T(8,128)(2,1)S(1)}, bf16[16,1024]{1,0:T(8,128)(2,1)S(1)}, u32[]{:S(2)}, u32[]{:S(2)}) collective-permute-start(bf16[16,1024]{1,0:T(8,128)(2,1)S(1)} %get-tuple-element.49), channel_id=1, source_target_pairs={{0,24},{8,0},{16,8},{24,16},{1,25},{9,1},{17,9},{25,17},{2,26},{10... | collective-permute-start | bytes 98312 | tf_op jit(solution)/shard_map/ppermute | solution.py:465
  30.5 4.3 %collective-permute-start.7 = (bf16[16,1024]{1,0:T(8,128)(2,1)S(1)}, bf16[16,1024]{1,0:T(8,128)(2,1)S(1)}, u32[]{:S(2)}, u32[]{:S(2)}) collective-permute-start(bf16[16,1024]{1,0:T(8,128)(2,1)S(1)} %get-tuple-element.49), channel_id=1, source_target_pairs={{0,16},{8,24},{16,0},{24,8},{1,17},{9,25},{17,1},{25,9},{2,18},{10... | collective-permute-start | bytes 98312 | tf_op jit(solution)/shard_map/ppermute | solution.py:465
  30.8 4.3 %collective-permute-start.6 = (bf16[16,1024]{1,0:T(8,128)(2,1)S(1)}, bf16[16,1024]{1,0:T(8,128)(2,1)S(1)}, u32[]{:S(2)}, u32[]{:S(2)}) collective-permute-start(bf16[16,1024]{1,0:T(8,128)(2,1)S(1)} %get-tuple-element.49), channel_id=1, source_target_pairs={{0,8},{8,16},{16,24},{24,0},{1,9},{9,17},{17,25},{25,1},{2,10},{10... | collective-permute-start | bytes 98312 | tf_op jit(solution)/shard_map/ppermute | solution.py:465
  35.1 4.7 %collective-permute-start.11 = (bf16[16,1024]{1,0:T(8,128)(2,1)S(1)}, bf16[16,1024]{1,0:T(8,128)(2,1)S(1)}, u32[]{:S(2)}, u32[]{:S(2)}) collective-permute-start(bf16[16,1024]{1,0:T(8,128)(2,1)S(1)} %fusion.14), channel_id=1, source_target_pairs={{0,96},{32,0},{64,32},{96,64},{1,97},{33,1},{65,33},{97,65},{2,98}... | collective-permute-start | bytes 98312 | tf_op jit(solution)/shard_map/ppermute | solution.py:465
  38.8 4.4 %collective-permute-start.10 = (bf16[16,1024]{1,0:T(8,128)(2,1)S(1)}, bf16[16,1024]{1,0:T(8,128)(2,1)S(1)}, u32[]{:S(2)}, u32[]{:S(2)}) collective-permute-start(bf16[16,1024]{1,0:T(8,128)(2,1)S(1)} %fusion.14), channel_id=1, source_target_pairs={{0,64},{32,96},{64,0},{96,32},{1,65},{33,97},{65,1},{97,33},{2,66}... | collective-permute-start | bytes 98312 | tf_op jit(solution)/shard_map/ppermute | solution.py:465
  39.0 4.3 %collective-permute-start.9 = (bf16[16,1024]{1,0:T(8,128)(2,1)S(1)}, bf16[16,1024]{1,0:T(8,128)(2,1)S(1)}, u32[]{:S(2)}, u32[]{:S(2)}) collective-permute-start(bf16[16,1024]{1,0:T(8,128)(2,1)S(1)} %fusion.14), channel_id=1, source_target_pairs={{0,32},{32,64},{64,96},{96,0},{1,33},{33,65},{65,97},{97,1},{2,34}... | collective-permute-start | bytes 98312 | tf_op jit(solution)/shard_map/ppermute | solution.py:465
  46.9 7.0 %collective-permute-start.13 = (bf16[512,1024]{1,0:T(8,128)(2,1)S(1)}, bf16[512,1024]{1,0:T(8,128)(2,1)S(1)}, u32[]{:S(2)}, u32[]{:S(2)}) collective-permute-start(bf16[512,1024]{1,0:T(8,128)(2,1)S(1)} %hidden.1.hidden_ref), channel_id=1, source_target_pairs={{0,1},{1,0},{2,3},{3,2},{4,5},{5,4},{6,7},{7,6},{8,9},{9,8},{10,11... | collective-permute-start | bytes 3145736 | tf_op jit(solution)/shard_map/ppermute | solution.py:454

commit v2 on v1

--- a/solution.py
+++ b/solution.py
@@ -1,3 +1,5 @@
+import functools
+
 import jax
 import jax.numpy as jnp
 from jax import lax
@@ -12,6 +14,7 @@
 WIDTH = 256
 SEQ = ("z", "y", "x")
 RING = 4
+PARTS = 2
 F32 = jnp.float32
 BF16 = jnp.bfloat16
 MIB = 1024 * 1024
@@ -144,8 +147,7 @@
     wq_ref,
     filt_ref,
     rates_ref,
-    gain_ref,
-    local_ref,
+    source_ref,
     ends_ref,
     total_ref,
     staged_ref,
@@ -200,7 +202,6 @@
                     for j in range(streams)
                 ]
                 kept["decay"] = [spread(jnp.exp(-rates_ref[n : n + 1, lanes])) for n in range(modes)]
-                kept["gain"] = [spread(gain_ref[n : n + 1, lanes]) for n in range(modes)]
                 kept["one"] = [at(j, -1) for j in range(streams)]
                 kept["two"] = [at(j, -2) for j in range(streams)]
                 kept["state"] = [jnp.zeros((SEGS, LANES), F32)] * modes
@@ -215,9 +216,7 @@
                     kept["one"], kept["two"] = now, kept["one"]
                     source = k * v
                     kept["state"] = [d * s + source for d, s in zip(kept["decay"], kept["state"])]
-                    local_ref[t * SEGS : (t + 1) * SEGS, lanes] = tree_sum(
-                        [g * s for g, s in zip(kept["gain"], kept["state"])]
-                    )
+                    source_ref[t * SEGS : (t + 1) * SEGS, lanes] = source
 
             def finish(kept=kept, lanes=lanes):
                 seg = lax.broadcasted_iota(jnp.int32, (SEGS, LANES), 0)
@@ -247,7 +246,7 @@
     stage.wait()
 
 
-def front_call(where, lhs, halo_own, halo_other, staged, weight, filt, rates, gain):
+def front_call(where, lhs, halo_own, halo_other, staged, weight, filt, rates):
     rows, full = lhs.shape
     streams, _, channels = staged.shape
     modes = rates.shape[0]
@@ -258,7 +257,7 @@
         in_specs=[pl.BlockSpec(memory_space=pltpu.SMEM)]
         + [vmem] * 4
         + [pl.BlockSpec(memory_space=pl.ANY)]
-        + [vmem] * 3,
+        + [vmem] * 2,
         out_specs=[vmem] * 4,
         out_shape=[
             pltpu.VMEM((rows, channels), F32),
@@ -278,7 +277,6 @@
         pltpu.with_memory_space_constraint(weight, pltpu.HBM),
         filt,
         rates,
-        gain,
     )
 
 
@@ -334,13 +332,54 @@
     )(where, *args)
 
 
-def hidden_kernel(ends_ref, into_ref, local_ref, query_ref, rates_ref, gain_ref, hidden_ref):
+def local_kernel(first, source_ref, rates_ref, gain_ref, local_ref):
     rows, channels = local_ref.shape
+    modes = rates_ref.shape[0]
+    for i in range(channels // LANES):
+        lanes = slice(first + i * LANES, first + (i + 1) * LANES)
+        decays = [spread(jnp.exp(-rates_ref[n : n + 1, lanes])) for n in range(modes)]
+        gains = [spread(gain_ref[n : n + 1, lanes]) for n in range(modes)]
+
+        def body(t, states, i=i, lanes=lanes, decays=decays, gains=gains):
+            row = pl.ds(pl.multiple_of(t * SEGS, SEGS), SEGS)
+            source = source_ref[row, lanes]
+            states = tuple(d * s + source for d, s in zip(decays, states))
+            local_ref[row, i * LANES : (i + 1) * LANES] = tree_sum(
+                [g * s for g, s in zip(gains, states)]
+            )
+            return states
+
+        zero = jnp.zeros((SEGS, LANES), F32)
+        lax.fori_loop(0, rows // SEGS, body, (zero,) * modes, unroll=16)
+
+
+def local_call(source, rates, gain, part):
+    rows, channels = source.shape
+    vmem = pl.BlockSpec(memory_space=pltpu.VMEM)
+    args = [pltpu.with_memory_space_constraint(x, pltpu.VMEM) for x in (source, rates, gain)]
+    return pl.pallas_call(
+        functools.partial(local_kernel, part * channels // PARTS),
+        in_specs=[vmem] * 3,
+        out_specs=vmem,
+        out_shape=pltpu.VMEM((rows, channels // PARTS), F32),
+        compiler_params=pltpu.CompilerParams(vmem_limit_bytes=4 * MIB),
+        cost_estimate=pl.CostEstimate(
+            flops=4 * rates.shape[0] * rows * channels // PARTS, transcendentals=0, bytes_accessed=0
+        ),
+        name="local",
+    )(*args)
+
+
+def hidden_kernel(ends_ref, into_ref, first_ref, second_ref, query_ref, rates_ref, gain_ref, hidden_ref):
+    rows, channels = query_ref.shape
     steps = rows // SEGS
     modes = rates_ref.shape[0]
+    local_refs = (first_ref, second_ref)
     seg = lax.broadcasted_iota(jnp.int32, (SEGS, LANES), 0)
     for i in range(channels // LANES):
         lanes = slice(i * LANES, (i + 1) * LANES)
+        local_ref = local_refs[i * LANES * PARTS // channels]
+        here = slice(lanes.start % (channels // PARTS), lanes.start % (channels // PARTS) + LANES)
         decays, leads = [], []
         for n in range(modes):
             rate = spread(rates_ref[n : n + 1, lanes])
@@ -352,12 +391,12 @@
             decays.append(jnp.exp(-rate))
             leads.append(spread(gain_ref[n : n + 1, lanes]) * state)
 
-        def body(t, leads, lanes=lanes, decays=decays):
+        def body(t, leads, lanes=lanes, here=here, local_ref=local_ref, decays=decays):
             halves = []
             for u in range(2):
                 row = pl.ds(pl.multiple_of((2 * t + u) * SEGS, SEGS), SEGS)
                 leads = tuple(d * s for d, s in zip(decays, leads))
-                halves.append(query_ref[row, lanes] * (local_ref[row, lanes] + tree_sum(leads)))
+                halves.append(query_ref[row, lanes] * (local_ref[row, here] + tree_sum(leads)))
             row = pl.ds(pl.multiple_of(2 * t * SEGS, 2 * SEGS), 2 * SEGS)
             hidden_ref[row, lanes] = jnp.concatenate(halves, axis=0).astype(BF16)
             return leads
@@ -369,13 +408,13 @@
     vmem = pl.BlockSpec(memory_space=pltpu.VMEM)
     args = [
         pltpu.with_memory_space_constraint(x, pltpu.VMEM)
-        for x in (ends, into, local, query, rates, gain)
+        for x in (ends, into, *local, query, rates, gain)
     ]
     return pl.pallas_call(
         hidden_kernel,
-        in_specs=[vmem] * 6,
+        in_specs=[vmem] * 7,
         out_specs=vmem,
-        out_shape=pltpu.VMEM(local.shape, BF16),
+        out_shape=pltpu.VMEM(query.shape, BF16),
         compiler_params=pltpu.CompilerParams(vmem_limit_bytes=4 * MIB),
         name="hidden",
     )(*args)
@@ -482,23 +521,25 @@
     halo_other = swapped(halo_own)
     lhs, halo_other, out_weight = lax.optimization_barrier((lhs, halo_other, out_weight))
     out_weight_other = swapped(out_weight)
-    local, ends, total, query_weight = front_call(
-        where, lhs, halo_own, halo_other, staged, weight, filt, rates, gain
+    source, ends, total, query_weight = front_call(
+        where, lhs, halo_own, halo_other, staged, weight, filt, rates
     )
-    query = query_call(where, lhs, halo_own, halo_other, query_weight, filt)
+    beside = [
+        query_call(where, lhs, halo_own, halo_other, query_weight, filt),
+        *[local_call(source, rates, gain, part) for part in range(PARTS)],
+    ]
 
     into = 0.0
     for level, axis in enumerate(reversed(SEQ)):
         arrived = round_the_ring(total, axis)
-        if level == 0:
-            query, *arrived = lax.optimization_barrier((query, *arrived))
+        beside[level], *arrived = lax.optimization_barrier((beside[level], *arrived))
         total = total_weights[RING * level] * total
         for k, part in enumerate(arrived):
             part = part.astype(F32)
             into = into + into_weights[(RING - 1) * level + k] * part
             total = total + total_weights[RING * level + k + 1] * part
 
-    hidden = hidden_call(ends, into, local, query, rates, gain)
+    hidden = hidden_call(ends, into, beside[1:], beside[0], rates, gain)
     part, partner_weight = product_call(where, hidden, out_weight, out_weight_other)
     return output_call(part, swapped(hidden), partner_weight)
 

time: 56.8 us -> 53.7 us (0.945)
  waiting for transfers between devices: 9.39 us -> 2.05 us
  starting transfers between devices: 21.7 us -> 24 us
  Pallas kernels: 24.3 us -> 26.2 us
    ppermute x9, waiting for transfers between devices: 8.14 us -> 0.68 us  [round_the_ring(): lax.ppermute(sent, axis, [(i, (i + k) % RING) for i in range(RING)])]
    pallas_call x1 -> x3, Pallas kernels: 3.48 us -> 7.97 us  [the longest x2 4.52 us: local_call(): pl.pallas_call(functools.partial(local_kernel, part * channels // PARTS),...]
    ppermute x9, starting transfers between devices: 11.8 us -> 14.8 us  [round_the_ring(): lax.ppermute(sent, axis, [(i, (i + k) % RING) for i in range(RING)])]
    pallas_call x1, Pallas kernels: 9.39 us -> 6.92 us  [front_call(): pl.pallas_call(front_kernel, in_specs=[pl.BlockSpec(memory_space=pltpu.SM...]
    ppermute x4, starting transfers between devices: 6.74 us -> 5.99 us  [swapped(): return lax.ppermute(x, 'ch', [(0, 1), (1, 0)])]
  transfers between devices with their start and end apart: 14 -> 14, of which waited for: 9 -> 3; matrix products, arithmetic and copies ran while one was open for 2% -> 2% of each run, Pallas kernels for 38% -> 44%
where the time goes in v2:
time: 53.7 us; the launch traced here: 53.5 us
  Pallas kernels  26.2 us (49%)
  starting transfers between devices  24 us (45%)
  waiting for transfers between devices  2.05 us (4%)
  local copies, waits for them, and re-layouts  0.77 us (1%)
    ppermute x9, starting transfers between devices, round_the_ring(): lax.ppermute(sent, axis, [(i, (i + k) % RING) for i in range(RING)])  14.8 us
    pallas_call x1, Pallas kernels, front_call(): pl.pallas_call(front_kernel, in_specs=[pl.BlockSpec(memory_space=pltpu.SM...  6.92 us
    ppermute x4, starting transfers between devices, swapped(): return lax.ppermute(x, 'ch', [(0, 1), (1, 0)])  5.99 us
    pallas_call x2, Pallas kernels, local_call(): pl.pallas_call(functools.partial(local_kernel, part * channels // PARTS),...  4.52 us
    pallas_call x1, Pallas kernels, stage_call(): pl.pallas_call(stage_kernel, in_specs=[pl.BlockSpec(memory_space=pltpu.SM...  3.96 us
    pallas_call x1, Pallas kernels, hidden_call(): pl.pallas_call(hidden_kernel, in_specs=[vmem] * 7, out_specs=vmem, out_sh...  3.45 us
    ppermute x1, starting transfers between devices, from_before(): return lax.ppermute(x, SEQ, [(i, i + 1) for i in range(count - 1)])  3.19 us
    pallas_call x1, Pallas kernels, query_call(): pl.pallas_call(query_kernel, in_specs=[pl.BlockSpec(memory_space=pltpu.SM...  2.89 us
  transfers between devices with their start and end apart: 14, of which 3 were waited for; matrix products, arithmetic and copies ran while one was open for 2% of the time, Pallas kernels for 44%

profile of v2, /device:TPU:1, one launch (start us, length us, event | category | flops | bytes accessed | tf_op | source)
XLA Modules:
  0.0 53.5 jit_solution(3394614494651374431)
XLA Ops:
  0.0 1.4 %collective-permute-start.1 = (bf16[512,1024]{1,0:T(8,128)(2,1)}, bf16[512,1024]{1,0:T(8,128)(2,1)S(1)}, u32[]{:S(2)}, u32[]{:S(2)}) collective-permute-start(bf16[512,1024]{1,0:T(8,128)(2,1)} %own_ref.1), channel_id=1, source_target_pairs={{0,1},{1,0},{2,3},{3,2},{4,5},{5,4},{6,7},{7,6},{8,9},{9,8},{10,11... | collective-permute-start | bytes 3145736 | tf_op jit(solution)/shard_map/ppermute | solution.py:493
  1.4 0.8 %slice.54 = bf16[16,1024]{1,0:T(8,128)(2,1)S(1)} slice(bf16[512,1024]{1,0:T(8,128)(2,1)} %own_ref.1), slice={[496:512], [0:1024]} | slice | bytes 65536 | tf_op jit(solution)/shard_map/slice | solution.py:516
  2.2 3.2 %collective-permute-start = (bf16[16,1024]{1,0:T(8,128)(2,1)S(1)}, bf16[16,1024]{1,0:T(8,128)(2,1)S(1)}, u32[]{:S(2)}, u32[]{:S(2)}) collective-permute-start(bf16[16,1024]{1,0:T(8,128)(2,1)S(1)} %slice.54), channel_id=1, source_target_pairs={{0,2},{2,4},{4,6},{6,8},{8,10},{10,12},{12,14},{14,16},{16,18},{18... | collective-permute-start | bytes 98312 | tf_op jit(solution)/shard_map/ppermute | solution.py:498
  5.4 0.0 copy-start
  5.4 4.0 %stage.1 = (bf16[512,2048]{1,0:T(8,128)(2,1)S(1)}, bf16[2,2048,1024]{2,1,0:T(8,128)(2,1)S(1)}, f32[3,3,1024]{2,1,0:T(4,128)S(1)}, f32[16,1024]{1,0:T(8,128)S(1)}...) custom-call(s32[1]{0:T(128)} %bitcast.where_ref, bf16[512,1024]{1,0:T(8,128)(2,1)} %own_ref.1, ...), custom_call_target="tpu_custom_call" | custom-call | tf_op jit(solution)/shard_map/stage/pallas_call | solution.py:94
  9.4 0.0 collective-permute-done.halo_own_ref
  9.4 0.4 collective-permute-start.2
  9.8 0.9 %collective-permute-done.2.halo_other_ref = bf16[16,1024]{1,0:T(8,128)(2,1)S(1)} collective-permute-done((bf16[16,1024]{1,0:T(8,128)(2,1)S(1)}, bf16[16,1024]{1,0:T(8,128)(2,1)S(1)}, u32[]{:S(2)}, u32[]{:S(2)}) %collective-permute-start.2) | collective-permute-done | bytes 32800 | tf_op jit(solution)/shard_map/ppermute | solution.py:493
  10.7 0.3 collective-permute-start.12
  11.0 6.9 %front.1 = (f32[512,1024]{1,0:T(8,128)S(1)}, f32[128,1024]{1,0:T(8,128)S(1)}, f32[16,1024]{1,0:T(8,128)S(1)}, bf16[2048,1024]{1,0:T(8,128)(2,1)S(1)}) custom-call(s32[1]{0:T(128)} %bitcast.where_ref, bf16[512,2048]{1,0:T(8,128)(2,1)S(1)} %get-tuple-element.39.lhs_ref, bf16[16,1024]{1,0:T(8,128)(2,1)S(1)} %collective-permute-done.halo_own_ref, ...), custom_call_target="tpu_custom_call" | custom-call | tf_op jit(solution)/shard_map/front/pallas_call | solution.py:255
  17.9 1.3 %collective-permute-start.3 = (bf16[16,1024]{1,0:T(8,128)(2,1)S(1)}, bf16[16,1024]{1,0:T(8,128)(2,1)S(1)}, u32[]{:S(2)}, u32[]{:S(2)}) collective-permute-start(bf16[16,1024]{1,0:T(8,128)(2,1)S(1)} %convert_element_type.36), channel_id=1, source_target_pairs={{0,2},{2,4},{4,6},{6,0},{1,3},{3,5},{5,7},{7,1},{8,10},{10,12},{12... | collective-permute-start | bytes 98312 | tf_op jit(solution)/shard_map/ppermute | solution.py:504
  19.2 2.4 %collective-permute-start.4 = (bf16[16,1024]{1,0:T(8,128)(2,1)S(1)}, bf16[16,1024]{1,0:T(8,128)(2,1)S(1)}, u32[]{:S(2)}, u32[]{:S(2)}) collective-permute-start(bf16[16,1024]{1,0:T(8,128)(2,1)S(1)} %convert_element_type.36), channel_id=1, source_target_pairs={{0,4},{2,6},{4,0},{6,2},{1,5},{3,7},{5,1},{7,3},{8,12},{10,14},{12... | collective-permute-start | bytes 98312 | tf_op jit(solution)/shard_map/ppermute | solution.py:504
  21.6 0.9 %collective-permute-start.5 = (bf16[16,1024]{1,0:T(8,128)(2,1)S(1)}, bf16[16,1024]{1,0:T(8,128)(2,1)S(1)}, u32[]{:S(2)}, u32[]{:S(2)}) collective-permute-start(bf16[16,1024]{1,0:T(8,128)(2,1)S(1)} %convert_element_type.36), channel_id=1, source_target_pairs={{0,6},{2,0},{4,2},{6,4},{1,7},{3,1},{5,3},{7,5},{8,14},{10,8},{12,... | collective-permute-start | bytes 98312 | tf_op jit(solution)/shard_map/ppermute | solution.py:504
  22.5 2.9 %query.1.query_ref = f32[512,1024]{1,0:T(8,128)S(1)} custom-call(s32[1]{0:T(128)} %bitcast.where_ref, bf16[512,2048]{1,0:T(8,128)(2,1)S(1)} %get-tuple-element.39.lhs_ref, bf16[16,1024]{1,0:T(8,128)(2,1)S(1)} %collective-permute-done.halo_own_ref, bf16[16,1024]{1,0:T(8,128)(2,1)S(1)} %collective-permute-done.2.halo_other_ref, ...), custom_call_target="tpu_custom_call" | custom-call | flops 2214592512 | tf_op jit(solution)/shard_map/query/pallas_call | solution.py:318
  25.4 0.0 collective-permute-done.3
  25.4 0.0 collective-permute-done.4
  25.5 1.4 %collective-permute-start.6 = (bf16[16,1024]{1,0:T(8,128)(2,1)S(1)}, bf16[16,1024]{1,0:T(8,128)(2,1)S(1)}, u32[]{:S(2)}, u32[]{:S(2)}) collective-permute-start(bf16[16,1024]{1,0:T(8,128)(2,1)S(1)} %get-tuple-element.65), channel_id=1, source_target_pairs={{0,8},{8,16},{16,24},{24,0},{1,9},{9,17},{17,25},{25,1},{2,10},{10... | collective-permute-start | bytes 98312 | tf_op jit(solution)/shard_map/ppermute | solution.py:504
  26.8 2.6 %collective-permute-start.7 = (bf16[16,1024]{1,0:T(8,128)(2,1)S(1)}, bf16[16,1024]{1,0:T(8,128)(2,1)S(1)}, u32[]{:S(2)}, u32[]{:S(2)}) collective-permute-start(bf16[16,1024]{1,0:T(8,128)(2,1)S(1)} %get-tuple-element.65), channel_id=1, source_target_pairs={{0,16},{8,24},{16,0},{24,8},{1,17},{9,25},{17,1},{25,9},{2,18},{10... | collective-permute-start | bytes 98312 | tf_op jit(solution)/shard_map/ppermute | solution.py:504
  29.5 1.1 %collective-permute-start.8 = (bf16[16,1024]{1,0:T(8,128)(2,1)S(1)}, bf16[16,1024]{1,0:T(8,128)(2,1)S(1)}, u32[]{:S(2)}, u32[]{:S(2)}) collective-permute-start(bf16[16,1024]{1,0:T(8,128)(2,1)S(1)} %get-tuple-element.65), channel_id=1, source_target_pairs={{0,24},{8,0},{16,8},{24,16},{1,25},{9,1},{17,9},{25,17},{2,26},{10... | collective-permute-start | bytes 98312 | tf_op jit(solution)/shard_map/ppermute | solution.py:504
  30.6 2.3 %local.2.first_ref = f32[512,512]{1,0:T(8,128)S(1)} custom-call(f32[512,1024]{1,0:T(8,128)S(1)} %get-tuple-element.51.source_ref, f32[16,1024]{1,0:T(8,128)S(1)} %get-tuple-element.43.rates_ref, f32[16,1024]{1,0:T(8,128)S(1)} %bitcast_multiply_fusion.5.gain_ref), custom_call_target="tpu_custom_call" | custom-call | flops 16777216 | tf_op jit(solution)/shard_map/local/pallas_call | solution.py:360
  32.9 0.0 collective-permute-done.7
  32.9 3.7 %collective-permute-start.10 = (bf16[16,1024]{1,0:T(8,128)(2,1)S(1)}, bf16[16,1024]{1,0:T(8,128)(2,1)S(1)}, u32[]{:S(2)}, u32[]{:S(2)}) collective-permute-start(bf16[16,1024]{1,0:T(8,128)(2,1)S(1)} %fusion.14), channel_id=1, source_target_pairs={{0,64},{32,96},{64,0},{96,32},{1,65},{33,97},{65,1},{97,33},{2,66}... | collective-permute-start | bytes 98312 | tf_op jit(solution)/shard_map/ppermute | solution.py:504
  36.6 0.4 collective-permute-start.11
  37.0 1.0 %collective-permute-start.9 = (bf16[16,1024]{1,0:T(8,128)(2,1)S(1)}, bf16[16,1024]{1,0:T(8,128)(2,1)S(1)}, u32[]{:S(2)}, u32[]{:S(2)}) collective-permute-start(bf16[16,1024]{1,0:T(8,128)(2,1)S(1)} %fusion.14), channel_id=1, source_target_pairs={{0,32},{32,64},{64,96},{96,0},{1,33},{33,65},{65,97},{97,1},{2,34}... | collective-permute-start | bytes 98312 | tf_op jit(solution)/shard_map/ppermute | solution.py:504
  38.1 2.3 %local.3.second_ref = f32[512,512]{1,0:T(8,128)S(1)} custom-call(f32[512,1024]{1,0:T(8,128)S(1)} %get-tuple-element.51.source_ref, f32[16,1024]{1,0:T(8,128)S(1)} %get-tuple-element.43.rates_ref, f32[16,1024]{1,0:T(8,128)S(1)} %bitcast_multiply_fusion.5.gain_ref), custom_call_target="tpu_custom_call" | custom-call | flops 16777216 | tf_op jit(solution)/shard_map/local/pallas_call | solution.py:360
  40.3 0.7 %collective-permute-done.9 = bf16[16,1024]{1,0:T(8,128)(2,1)S(1)} collective-permute-done((bf16[16,1024]{1,0:T(8,128)(2,1)S(1)}, bf16[16,1024]{1,0:T(8,128)(2,1)S(1)}, u32[]{:S(2)}, u32[]{:S(2)}) %collective-permute-start.9) | collective-permute-done | bytes 32800 | tf_op jit(solution)/shard_map/ppermute | solution.py:504
  41.0 0.1 fusion.7.into_ref
  41.1 3.4 %hidden.1.hidden_ref = bf16[512,1024]{1,0:T(8,128)(2,1)S(1)} custom-call(f32[128,1024]{1,0:T(8,128)S(1)} %get-tuple-element.44.ends_ref, f32[16,1024]{1,0:T(8,128)S(1)} %fusion.7.into_ref, f32[512,512]{1,0:T(8,128)S(1)} %local.2.first_ref, f32[512,512]{1,0:T(8,128)S(1)} %local.3.second_ref, f32[512,1024]{1,0:T(8,128)S(1)} %query.1.query_ref, ...), custom_call_target="tpu_custom_call" | custom-call | tf_op jit(solution)/shard_map/hidden/pallas_call | solution.py:413
  44.5 3.9 %collective-permute-start.13 = (bf16[512,1024]{1,0:T(8,128)(2,1)S(1)}, bf16[512,1024]{1,0:T(8,128)(2,1)S(1)}, u32[]{:S(2)}, u32[]{:S(2)}) collective-permute-start(bf16[512,1024]{1,0:T(8,128)(2,1)S(1)} %hidden.1.hidden_ref), channel_id=1, source_target_pairs={{0,1},{1,0},{2,3},{3,2},{4,5},{5,4},{6,7},{7,6},{8,9},{9,8},{10,11... | collective-permute-start | bytes 3145736 | tf_op jit(solution)/shard_map/ppermute | solution.py:493
  48.4 1.8 %product.1 = (f32[512,1024]{1,0:T(8,128)S(1)}, bf16[1024,1024]{1,0:T(8,128)(2,1)S(1)}) custom-call(s32[1]{0:T(128)} %bitcast.where_ref, bf16[512,1024]{1,0:T(8,128)(2,1)S(1)} %hidden.1.hidden_ref, bf16[1024,2048]{1,0:T(8,128)(2,1)S(1)} %copy-done, bf16[1024,2048]{1,0:T(8,128)(2,1)S(1)} %collective-permute-done.12.w_other_ref), custom_call_target="tpu_custom_call" | custom-call | tf_op jit(solution)/shard_map/product/pallas_call | solution.py:440
  50.3 0.4 collective-permute-done.13.other_ref
  50.7 2.6 %output.1 = f32[512,1024]{1,0:T(8,128)} custom-call(f32[512,1024]{1,0:T(8,128)S(1)} %get-tuple-element.63.part_ref, bf16[512,1024]{1,0:T(8,128)(2,1)S(1)} %collective-permute-done.13.other_ref, bf16[1024,1024]{1,0:T(8,128)(2,1)S(1)} %get-tuple-element.64.w_ref), custom_call_target="tpu_custom_call" | custom-call | tf_op jit(solution)/shard_map/output/pallas_call | solution.py:477
  (16 shorter events, 0.1 us)
Async XLA Ops:
  0.0 5.4 %collective-permute-start.1 = (bf16[512,1024]{1,0:T(8,128)(2,1)}, bf16[512,1024]{1,0:T(8,128)(2,1)S(1)}, u32[]{:S(2)}, u32[]{:S(2)}) collective-permute-start(bf16[512,1024]{1,0:T(8,128)(2,1)} %own_ref.1), channel_id=1, source_target_pairs={{0,1},{1,0},{2,3},{3,2},{4,5},{5,4},{6,7},{7,6},{8,9},{9,8},{10,11... | collective-permute-start | bytes 3145736 | tf_op jit(solution)/shard_map/ppermute | solution.py:493
  2.2 7.2 %collective-permute-start = (bf16[16,1024]{1,0:T(8,128)(2,1)S(1)}, bf16[16,1024]{1,0:T(8,128)(2,1)S(1)}, u32[]{:S(2)}, u32[]{:S(2)}) collective-permute-start(bf16[16,1024]{1,0:T(8,128)(2,1)S(1)} %slice.54), channel_id=1, source_target_pairs={{0,2},{2,4},{4,6},{6,8},{8,10},{10,12},{12,14},{14,16},{16,18},{18... | collective-permute-start | bytes 98312 | tf_op jit(solution)/shard_map/ppermute | solution.py:498
  5.4 5.3 %copy-start = (bf16[1024,2048]{1,0:T(8,128)(2,1)S(1)}, bf16[1024,2048]{1,0:T(8,128)(2,1)}, u32[]{:S(2)}) copy-start(bf16[1024,2048]{1,0:T(8,128)(2,1)} %w_ref) | copy-start | bytes 12582916
  9.4 1.3 %collective-permute-start.2 = (bf16[16,1024]{1,0:T(8,128)(2,1)S(1)}, bf16[16,1024]{1,0:T(8,128)(2,1)S(1)}, u32[]{:S(2)}, u32[]{:S(2)}) collective-permute-start(bf16[16,1024]{1,0:T(8,128)(2,1)S(1)} %collective-permute-done.halo_own_ref), channel_id=1, source_target_pairs={{0,1},{1,0},{2,3},{3,2},{4,5},{5,4},{6,7},{7,6},{8,9},{9,8},{10,11... | collective-permute-start | bytes 98312 | tf_op jit(solution)/shard_map/ppermute | solution.py:493
  10.7 37.8 %collective-permute-start.12 = (bf16[1024,2048]{1,0:T(8,128)(2,1)S(1)}, bf16[1024,2048]{1,0:T(8,128)(2,1)S(1)}, u32[]{:S(2)}, u32[]{:S(2)}) collective-permute-start(bf16[1024,2048]{1,0:T(8,128)(2,1)S(1)} %copy-done), channel_id=1, source_target_pairs={{0,1},{1,0},{2,3},{3,2},{4,5},{5,4},{6,7},{7,6},{8,9},{9,8},{10,11... | collective-permute-start | bytes 12582920 | tf_op jit(solution)/shard_map/ppermute | solution.py:493
  17.9 7.5 %collective-permute-start.3 = (bf16[16,1024]{1,0:T(8,128)(2,1)S(1)}, bf16[16,1024]{1,0:T(8,128)(2,1)S(1)}, u32[]{:S(2)}, u32[]{:S(2)}) collective-permute-start(bf16[16,1024]{1,0:T(8,128)(2,1)S(1)} %convert_element_type.36), channel_id=1, source_target_pairs={{0,2},{2,4},{4,6},{6,0},{1,3},{3,5},{5,7},{7,1},{8,10},{10,12},{12... | collective-permute-start | bytes 98312 | tf_op jit(solution)/shard_map/ppermute | solution.py:504
  19.2 6.2 %collective-permute-start.4 = (bf16[16,1024]{1,0:T(8,128)(2,1)S(1)}, bf16[16,1024]{1,0:T(8,128)(2,1)S(1)}, u32[]{:S(2)}, u32[]{:S(2)}) collective-permute-start(bf16[16,1024]{1,0:T(8,128)(2,1)S(1)} %convert_element_type.36), channel_id=1, source_target_pairs={{0,4},{2,6},{4,0},{6,2},{1,5},{3,7},{5,1},{7,3},{8,12},{10,14},{12... | collective-permute-start | bytes 98312 | tf_op jit(solution)/shard_map/ppermute | solution.py:504
  21.6 3.8 %collective-permute-start.5 = (bf16[16,1024]{1,0:T(8,128)(2,1)S(1)}, bf16[16,1024]{1,0:T(8,128)(2,1)S(1)}, u32[]{:S(2)}, u32[]{:S(2)}) collective-permute-start(bf16[16,1024]{1,0:T(8,128)(2,1)S(1)} %convert_element_type.36), channel_id=1, source_target_pairs={{0,6},{2,0},{4,2},{6,4},{1,7},{3,1},{5,3},{7,5},{8,14},{10,8},{12,... | collective-permute-start | bytes 98312 | tf_op jit(solution)/shard_map/ppermute | solution.py:504
  22.5 8.0 %copy-start.1 = (f32[1024,16]{0,1:T(8,128)S(1)}, f32[1024,16]{0,1:T(8,128)}, u32[]{:S(2)}) copy-start(f32[1024,16]{0,1:T(8,128)} %param.10) | copy-start | bytes 196612
  22.5 8.0 %copy-start.2 = (f32[1024,16]{0,1:T(8,128)S(1)}, f32[1024,16]{0,1:T(8,128)}, u32[]{:S(2)}) copy-start(f32[1024,16]{0,1:T(8,128)} %param.9) | copy-start | bytes 196612
  25.5 7.4 %collective-permute-start.6 = (bf16[16,1024]{1,0:T(8,128)(2,1)S(1)}, bf16[16,1024]{1,0:T(8,128)(2,1)S(1)}, u32[]{:S(2)}, u32[]{:S(2)}) collective-permute-start(bf16[16,1024]{1,0:T(8,128)(2,1)S(1)} %get-tuple-element.65), channel_id=1, source_target_pairs={{0,8},{8,16},{16,24},{24,0},{1,9},{9,17},{17,25},{25,1},{2,10},{10... | collective-permute-start | bytes 98312 | tf_op jit(solution)/shard_map/ppermute | solution.py:504
  26.8 6.0 %collective-permute-start.7 = (bf16[16,1024]{1,0:T(8,128)(2,1)S(1)}, bf16[16,1024]{1,0:T(8,128)(2,1)S(1)}, u32[]{:S(2)}, u32[]{:S(2)}) collective-permute-start(bf16[16,1024]{1,0:T(8,128)(2,1)S(1)} %get-tuple-element.65), channel_id=1, source_target_pairs={{0,16},{8,24},{16,0},{24,8},{1,17},{9,25},{17,1},{25,9},{2,18},{10... | collective-permute-start | bytes 98312 | tf_op jit(solution)/shard_map/ppermute | solution.py:504
  29.5 3.4 %collective-permute-start.8 = (bf16[16,1024]{1,0:T(8,128)(2,1)S(1)}, bf16[16,1024]{1,0:T(8,128)(2,1)S(1)}, u32[]{:S(2)}, u32[]{:S(2)}) collective-permute-start(bf16[16,1024]{1,0:T(8,128)(2,1)S(1)} %get-tuple-element.65), channel_id=1, source_target_pairs={{0,24},{8,0},{16,8},{24,16},{1,25},{9,1},{17,9},{25,17},{2,26},{10... | collective-permute-start | bytes 98312 | tf_op jit(solution)/shard_map/ppermute | solution.py:504
  32.9 7.4 %collective-permute-start.10 = (bf16[16,1024]{1,0:T(8,128)(2,1)S(1)}, bf16[16,1024]{1,0:T(8,128)(2,1)S(1)}, u32[]{:S(2)}, u32[]{:S(2)}) collective-permute-start(bf16[16,1024]{1,0:T(8,128)(2,1)S(1)} %fusion.14), channel_id=1, source_target_pairs={{0,64},{32,96},{64,0},{96,32},{1,65},{33,97},{65,1},{97,33},{2,66}... | collective-permute-start | bytes 98312 | tf_op jit(solution)/shard_map/ppermute | solution.py:504
  36.6 3.7 %collective-permute-start.11 = (bf16[16,1024]{1,0:T(8,128)(2,1)S(1)}, bf16[16,1024]{1,0:T(8,128)(2,1)S(1)}, u32[]{:S(2)}, u32[]{:S(2)}) collective-permute-start(bf16[16,1024]{1,0:T(8,128)(2,1)S(1)} %fusion.14), channel_id=1, source_target_pairs={{0,96},{32,0},{64,32},{96,64},{1,97},{33,1},{65,33},{97,65},{2,98}... | collective-permute-start | bytes 98312 | tf_op jit(solution)/shard_map/ppermute | solution.py:504
  37.0 4.0 %collective-permute-start.9 = (bf16[16,1024]{1,0:T(8,128)(2,1)S(1)}, bf16[16,1024]{1,0:T(8,128)(2,1)S(1)}, u32[]{:S(2)}, u32[]{:S(2)}) collective-permute-start(bf16[16,1024]{1,0:T(8,128)(2,1)S(1)} %fusion.14), channel_id=1, source_target_pairs={{0,32},{32,64},{64,96},{96,0},{1,33},{33,65},{65,97},{97,1},{2,34}... | collective-permute-start | bytes 98312 | tf_op jit(solution)/shard_map/ppermute | solution.py:504
  44.5 6.2 %collective-permute-start.13 = (bf16[512,1024]{1,0:T(8,128)(2,1)S(1)}, bf16[512,1024]{1,0:T(8,128)(2,1)S(1)}, u32[]{:S(2)}, u32[]{:S(2)}) collective-permute-start(bf16[512,1024]{1,0:T(8,128)(2,1)S(1)} %hidden.1.hidden_ref), channel_id=1, source_target_pairs={{0,1},{1,0},{2,3},{3,2},{4,5},{5,4},{6,7},{7,6},{8,9},{9,8},{10,11... | collective-permute-start | bytes 3145736 | tf_op jit(solution)/shard_map/ppermute | solution.py:493

commit v3 on v2

--- a/solution.py
+++ b/solution.py
@@ -12,6 +12,7 @@
 LANES = 128
 HISTORY = 8
 WIDTH = 256
+AHEAD = 2
 SEQ = ("z", "y", "x")
 RING = 4
 PARTS = 2
@@ -59,7 +60,7 @@
         (own_ref, lhs_out.at[:, pl.ds(mine, half)]),
         (other_ref, lhs_out.at[:, pl.ds(theirs, half)]),
         (filt_ref, filt_out),
-        (w_ref.at[pl.ds(1, w_out.shape[0])], w_out),
+        (w_ref.at[pl.ds(1, w_out.shape[0]), :, pl.ds(0, w_out.shape[2])], w_out),
     ]
     copies = [pltpu.make_async_copy(src, dst, sems.at[i]) for i, (src, dst) in enumerate(pairs)]
     for copy in copies:
@@ -97,7 +98,7 @@
         out_specs=[vmem] * 6,
         out_shape=[
             pltpu.VMEM((rows, 2 * half), BF16),
-            pltpu.VMEM((weight.shape[0] - 1, *weight.shape[1:]), BF16),
+            pltpu.VMEM((weight.shape[0] - 1, weight.shape[1], AHEAD * WIDTH), BF16),
             pltpu.VMEM(filt.shape, F32),
             pltpu.VMEM(rates.shape, F32),
             pltpu.VMEM((len(SEQ) * (RING - 1), *rates.shape), F32),
@@ -143,8 +144,8 @@
     lhs_ref,
     halo_own_ref,
     halo_other_ref,
+    ahead_ref,
     w_ref,
-    wq_ref,
     filt_ref,
     rates_ref,
     source_ref,
@@ -152,30 +153,40 @@
     total_ref,
     staged_ref,
     halo_ref,
+    rest_ref,
     proj_a,
     proj_b,
-    sem,
+    sems,
 ):
     rows = lhs_ref.shape[0]
     steps = rows // SEGS
     pitch = steps + HISTORY
     modes = rates_ref.shape[0]
-    streams = w_ref.shape[0]
+    streams = ahead_ref.shape[0]
     tiles = w_ref.shape[2] // WIDTH
     per = SEGS // 2
     proj = (proj_a, proj_b)
 
-    stage = pltpu.make_async_copy(wq_ref.at[0], staged_ref, sem)
+    rest = pltpu.make_async_copy(
+        w_ref.at[pl.ds(1, streams), :, pl.ds(AHEAD * WIDTH, (tiles - AHEAD) * WIDTH)],
+        rest_ref,
+        sems.at[0],
+    )
+    stage = pltpu.make_async_copy(w_ref.at[0], staged_ref, sems.at[1])
+    rest.start()
     stage.start()
     join_halo(where_ref, halo_ref, halo_own_ref, halo_other_ref)
 
     def projection(tile):
         held = proj[tile % 2]
+        weights, column = (ahead_ref, tile) if tile < AHEAD else (rest_ref, tile - AHEAD)
+        if tile == AHEAD:
+            rest.wait()
 
         def piece(j, first):
             part = jnp.dot(
                 segment_rows(lhs_ref, halo_ref, first, per),
-                w_ref[j, :, tile * WIDTH : (tile + 1) * WIDTH],
+                weights[j, :, column * WIDTH : (column + 1) * WIDTH],
                 preferred_element_type=F32,
             )
             hold_segments(held.at[j], part, first, per)
@@ -246,9 +257,9 @@
     stage.wait()
 
 
-def front_call(where, lhs, halo_own, halo_other, staged, weight, filt, rates):
+def front_call(where, lhs, halo_own, halo_other, ahead, weight, filt, rates):
     rows, full = lhs.shape
-    streams, _, channels = staged.shape
+    streams, channels = ahead.shape[0], weight.shape[2]
     modes = rates.shape[0]
     vmem = pl.BlockSpec(memory_space=pltpu.VMEM)
     held = pltpu.VMEM((streams, WIDTH // LANES, rows + SEGS * HISTORY, LANES), F32)
@@ -265,15 +276,21 @@
             pltpu.VMEM((modes, channels), F32),
             pltpu.VMEM((full, channels), BF16),
         ],
-        scratch_shapes=[pltpu.VMEM((HALO, full), BF16), held, held, pltpu.SemaphoreType.DMA],
-        compiler_params=pltpu.CompilerParams(vmem_limit_bytes=10 * MIB),
+        scratch_shapes=[
+            pltpu.VMEM((HALO, full), BF16),
+            pltpu.VMEM((streams, full, channels - AHEAD * WIDTH), BF16),
+            held,
+            held,
+            pltpu.SemaphoreType.DMA((2,)),
+        ],
+        compiler_params=pltpu.CompilerParams(vmem_limit_bytes=14 * MIB),
         name="front",
     )(
         where,
         lhs,
         halo_own,
         halo_other,
-        staged,
+        ahead,
         pltpu.with_memory_space_constraint(weight, pltpu.HBM),
         filt,
         rates,
@@ -401,7 +418,7 @@
             hidden_ref[row, lanes] = jnp.concatenate(halves, axis=0).astype(BF16)
             return leads
 
-        lax.fori_loop(0, steps // 2, body, tuple(leads), unroll=8)
+        lax.fori_loop(0, steps // 2, body, tuple(leads), unroll=True)
 
 
 def hidden_call(ends, into, local, query, rates, gain):
@@ -514,7 +531,7 @@
     gain = residues.T * jnp.sqrt(1.0 - jnp.exp(-2.0 * rates))
 
     halo_own = from_before(tokens[rows - HALO :])
-    lhs, staged, filt, rates, into_weights, total_weights = stage_call(
+    lhs, ahead, filt, rates, into_weights, total_weights = stage_call(
         where, tokens, swapped(tokens), weight, short_filter, rates
     )
     halo_own, lhs, out_weight = lax.optimization_barrier((halo_own, lhs, out_weight))
@@ -522,7 +539,7 @@
     lhs, halo_other, out_weight = lax.optimization_barrier((lhs, halo_other, out_weight))
     out_weight_other = swapped(out_weight)
     source, ends, total, query_weight = front_call(
-        where, lhs, halo_own, halo_other, staged, weight, filt, rates
+        where, lhs, halo_own, halo_other, ahead, weight, filt, rates
     )
     beside = [
         query_call(where, lhs, halo_own, halo_other, query_weight, filt),

time: 53.7 us -> 54.8 us (1.020)
  Pallas kernels: 26.2 us -> 27.3 us
    pallas_call x1, Pallas kernels: 6.92 us -> 10 us  [front_call(): pl.pallas_call(front_kernel, in_specs=[pl.BlockSpec(memory_space=pltpu.SM...]
    pallas_call x1, Pallas kernels: 3.96 us -> 2.76 us  [stage_call(): pl.pallas_call(stage_kernel, in_specs=[pl.BlockSpec(memory_space=pltpu.SM...]
    pallas_call x1, Pallas kernels: 3.45 us -> 2.76 us  [hidden_call(): pl.pallas_call(hidden_kernel, in_specs=[vmem] * 7, out_specs=vmem, out_sh...]
  transfers between devices with their start and end apart: 14 -> 14, of which waited for: 3 -> 3; matrix products, arithmetic and copies ran while one was open for 2% -> 2% of each run, Pallas kernels for 44% -> 45%
where the time goes in v3:
time: 54.8 us; the launch traced here: 54.6 us
  Pallas kernels  27.3 us (50%)
  starting transfers between devices  24 us (44%)
  waiting for transfers between devices  2.05 us (4%)
  local copies, waits for them, and re-layouts  0.77 us (1%)
    ppermute x9, starting transfers between devices, round_the_ring(): lax.ppermute(sent, axis, [(i, (i + k) % RING) for i in range(RING)])  14.8 us
    pallas_call x1, Pallas kernels, front_call(): pl.pallas_call(front_kernel, in_specs=[pl.BlockSpec(memory_space=pltpu.SM...  10 us
    ppermute x4, starting transfers between devices, swapped(): return lax.ppermute(x, 'ch', [(0, 1), (1, 0)])  5.98 us
    pallas_call x2, Pallas kernels, local_call(): pl.pallas_call(functools.partial(local_kernel, part * channels // PARTS),...  4.52 us
    ppermute x1, starting transfers between devices, from_before(): return lax.ppermute(x, SEQ, [(i, i + 1) for i in range(count - 1)])  3.19 us
    pallas_call x1, Pallas kernels, query_call(): pl.pallas_call(query_kernel, in_specs=[pl.BlockSpec(memory_space=pltpu.SM...  2.89 us
    pallas_call x1, Pallas kernels, stage_call(): pl.pallas_call(stage_kernel, in_specs=[pl.BlockSpec(memory_space=pltpu.SM...  2.76 us
    pallas_call x1, Pallas kernels, hidden_call(): pl.pallas_call(hidden_kernel, in_specs=[vmem] * 7, out_specs=vmem, out_sh...  2.76 us
  transfers between devices with their start and end apart: 14, of which 3 were waited for; matrix products, arithmetic and copies ran while one was open for 2% of the time, Pallas kernels for 45%

profile of v3, /device:TPU:1, one launch (start us, length us, event | category | flops | bytes accessed | tf_op | source)
XLA Modules:
  0.0 54.6 jit_solution(7326012543570455389)
XLA Ops:
  0.0 1.4 %collective-permute-start.1 = (bf16[512,1024]{1,0:T(8,128)(2,1)}, bf16[512,1024]{1,0:T(8,128)(2,1)S(1)}, u32[]{:S(2)}, u32[]{:S(2)}) collective-permute-start(bf16[512,1024]{1,0:T(8,128)(2,1)} %own_ref.1), channel_id=1, source_target_pairs={{0,1},{1,0},{2,3},{3,2},{4,5},{5,4},{6,7},{7,6},{8,9},{9,8},{10,11... | collective-permute-start | bytes 3145736 | tf_op jit(solution)/shard_map/ppermute | solution.py:510
  1.4 0.8 %slice.54 = bf16[16,1024]{1,0:T(8,128)(2,1)S(1)} slice(bf16[512,1024]{1,0:T(8,128)(2,1)} %own_ref.1), slice={[496:512], [0:1024]} | slice | bytes 65536 | tf_op jit(solution)/shard_map/slice | solution.py:533
  2.2 3.2 %collective-permute-start = (bf16[16,1024]{1,0:T(8,128)(2,1)S(1)}, bf16[16,1024]{1,0:T(8,128)(2,1)S(1)}, u32[]{:S(2)}, u32[]{:S(2)}) collective-permute-start(bf16[16,1024]{1,0:T(8,128)(2,1)S(1)} %slice.54), channel_id=1, source_target_pairs={{0,2},{2,4},{4,6},{6,8},{8,10},{10,12},{12,14},{14,16},{16,18},{18... | collective-permute-start | bytes 98312 | tf_op jit(solution)/shard_map/ppermute | solution.py:515
  5.4 0.0 collective-permute-done.1.other_ref
  5.4 0.0 copy-start
  5.4 2.8 %stage.1 = (bf16[512,2048]{1,0:T(8,128)(2,1)S(1)}, bf16[2,2048,512]{2,1,0:T(8,128)(2,1)S(1)}, f32[3,3,1024]{2,1,0:T(4,128)S(1)}, f32[16,1024]{1,0:T(8,128)S(1)},...) custom-call(s32[1]{0:T(128)} %bitcast.where_ref, bf16[512,1024]{1,0:T(8,128)(2,1)} %own_ref.1, ...), custom_call_target="tpu_custom_call" | custom-call | tf_op jit(solution)/shard_map/stage/pallas_call | solution.py:95
  8.2 0.0 collective-permute-done.halo_own_ref
  8.2 0.4 collective-permute-start.2
  8.6 0.9 %collective-permute-done.2.halo_other_ref = bf16[16,1024]{1,0:T(8,128)(2,1)S(1)} collective-permute-done((bf16[16,1024]{1,0:T(8,128)(2,1)S(1)}, bf16[16,1024]{1,0:T(8,128)(2,1)S(1)}, u32[]{:S(2)}, u32[]{:S(2)}) %collective-permute-start.2) | collective-permute-done | bytes 32800 | tf_op jit(solution)/shard_map/ppermute | solution.py:510
  9.5 0.3 collective-permute-start.12
  9.8 10.0 %front.1 = (f32[512,1024]{1,0:T(8,128)S(1)}, f32[128,1024]{1,0:T(8,128)S(1)}, f32[16,1024]{1,0:T(8,128)S(1)}, bf16[2048,1024]{1,0:T(8,128)(2,1)S(1)}) custom-call(s32[1]{0:T(128)} %bitcast.where_ref, bf16[512,2048]{1,0:T(8,128)(2,1)S(1)} %get-tuple-element.39.lhs_ref, bf16[16,1024]{1,0:T(8,128)(2,1)S(1)} %collective-permute-done.halo_own_ref, ...), custom_call_target="tpu_custom_call" | custom-call | tf_op jit(solution)/shard_map/front/pallas_call | solution.py:266
  19.8 1.3 %collective-permute-start.3 = (bf16[16,1024]{1,0:T(8,128)(2,1)S(1)}, bf16[16,1024]{1,0:T(8,128)(2,1)S(1)}, u32[]{:S(2)}, u32[]{:S(2)}) collective-permute-start(bf16[16,1024]{1,0:T(8,128)(2,1)S(1)} %convert_element_type.36), channel_id=1, source_target_pairs={{0,2},{2,4},{4,6},{6,0},{1,3},{3,5},{5,7},{7,1},{8,10},{10,12},{12... | collective-permute-start | bytes 98312 | tf_op jit(solution)/shard_map/ppermute | solution.py:521
  21.1 2.5 %collective-permute-start.4 = (bf16[16,1024]{1,0:T(8,128)(2,1)S(1)}, bf16[16,1024]{1,0:T(8,128)(2,1)S(1)}, u32[]{:S(2)}, u32[]{:S(2)}) collective-permute-start(bf16[16,1024]{1,0:T(8,128)(2,1)S(1)} %convert_element_type.36), channel_id=1, source_target_pairs={{0,4},{2,6},{4,0},{6,2},{1,5},{3,7},{5,1},{7,3},{8,12},{10,14},{12... | collective-permute-start | bytes 98312 | tf_op jit(solution)/shard_map/ppermute | solution.py:521
  23.5 0.9 %collective-permute-start.5 = (bf16[16,1024]{1,0:T(8,128)(2,1)S(1)}, bf16[16,1024]{1,0:T(8,128)(2,1)S(1)}, u32[]{:S(2)}, u32[]{:S(2)}) collective-permute-start(bf16[16,1024]{1,0:T(8,128)(2,1)S(1)} %convert_element_type.36), channel_id=1, source_target_pairs={{0,6},{2,0},{4,2},{6,4},{1,7},{3,1},{5,3},{7,5},{8,14},{10,8},{12,... | collective-permute-start | bytes 98312 | tf_op jit(solution)/shard_map/ppermute | solution.py:521
  24.4 2.9 %query.1.query_ref = f32[512,1024]{1,0:T(8,128)S(1)} custom-call(s32[1]{0:T(128)} %bitcast.where_ref, bf16[512,2048]{1,0:T(8,128)(2,1)S(1)} %get-tuple-element.39.lhs_ref, bf16[16,1024]{1,0:T(8,128)(2,1)S(1)} %collective-permute-done.halo_own_ref, bf16[16,1024]{1,0:T(8,128)(2,1)S(1)} %collective-permute-done.2.halo_other_ref, ...), custom_call_target="tpu_custom_call" | custom-call | flops 2214592512 | tf_op jit(solution)/shard_map/query/pallas_call | solution.py:335
  27.3 0.0 collective-permute-done.3
  27.3 0.0 collective-permute-done.5
  27.4 1.4 %collective-permute-start.6 = (bf16[16,1024]{1,0:T(8,128)(2,1)S(1)}, bf16[16,1024]{1,0:T(8,128)(2,1)S(1)}, u32[]{:S(2)}, u32[]{:S(2)}) collective-permute-start(bf16[16,1024]{1,0:T(8,128)(2,1)S(1)} %get-tuple-element.65), channel_id=1, source_target_pairs={{0,8},{8,16},{16,24},{24,0},{1,9},{9,17},{17,25},{25,1},{2,10},{10... | collective-permute-start | bytes 98312 | tf_op jit(solution)/shard_map/ppermute | solution.py:521
  28.7 2.6 %collective-permute-start.7 = (bf16[16,1024]{1,0:T(8,128)(2,1)S(1)}, bf16[16,1024]{1,0:T(8,128)(2,1)S(1)}, u32[]{:S(2)}, u32[]{:S(2)}) collective-permute-start(bf16[16,1024]{1,0:T(8,128)(2,1)S(1)} %get-tuple-element.65), channel_id=1, source_target_pairs={{0,16},{8,24},{16,0},{24,8},{1,17},{9,25},{17,1},{25,9},{2,18},{10... | collective-permute-start | bytes 98312 | tf_op jit(solution)/shard_map/ppermute | solution.py:521
  31.3 1.1 %collective-permute-start.8 = (bf16[16,1024]{1,0:T(8,128)(2,1)S(1)}, bf16[16,1024]{1,0:T(8,128)(2,1)S(1)}, u32[]{:S(2)}, u32[]{:S(2)}) collective-permute-start(bf16[16,1024]{1,0:T(8,128)(2,1)S(1)} %get-tuple-element.65), channel_id=1, source_target_pairs={{0,24},{8,0},{16,8},{24,16},{1,25},{9,1},{17,9},{25,17},{2,26},{10... | collective-permute-start | bytes 98312 | tf_op jit(solution)/shard_map/ppermute | solution.py:521
  32.4 2.3 %local.2.first_ref = f32[512,512]{1,0:T(8,128)S(1)} custom-call(f32[512,1024]{1,0:T(8,128)S(1)} %get-tuple-element.51.source_ref, f32[16,1024]{1,0:T(8,128)S(1)} %get-tuple-element.43.rates_ref, f32[16,1024]{1,0:T(8,128)S(1)} %bitcast_multiply_fusion.5.gain_ref), custom_call_target="tpu_custom_call" | custom-call | flops 16777216 | tf_op jit(solution)/shard_map/local/pallas_call | solution.py:377
  34.8 3.7 %collective-permute-start.10 = (bf16[16,1024]{1,0:T(8,128)(2,1)S(1)}, bf16[16,1024]{1,0:T(8,128)(2,1)S(1)}, u32[]{:S(2)}, u32[]{:S(2)}) collective-permute-start(bf16[16,1024]{1,0:T(8,128)(2,1)S(1)} %fusion.14), channel_id=1, source_target_pairs={{0,64},{32,96},{64,0},{96,32},{1,65},{33,97},{65,1},{97,33},{2,66}... | collective-permute-start | bytes 98312 | tf_op jit(solution)/shard_map/ppermute | solution.py:521
  38.5 0.4 collective-permute-start.11
  38.9 1.0 %collective-permute-start.9 = (bf16[16,1024]{1,0:T(8,128)(2,1)S(1)}, bf16[16,1024]{1,0:T(8,128)(2,1)S(1)}, u32[]{:S(2)}, u32[]{:S(2)}) collective-permute-start(bf16[16,1024]{1,0:T(8,128)(2,1)S(1)} %fusion.14), channel_id=1, source_target_pairs={{0,32},{32,64},{64,96},{96,0},{1,33},{33,65},{65,97},{97,1},{2,34}... | collective-permute-start | bytes 98312 | tf_op jit(solution)/shard_map/ppermute | solution.py:521
  39.9 2.3 %local.3.second_ref = f32[512,512]{1,0:T(8,128)S(1)} custom-call(f32[512,1024]{1,0:T(8,128)S(1)} %get-tuple-element.51.source_ref, f32[16,1024]{1,0:T(8,128)S(1)} %get-tuple-element.43.rates_ref, f32[16,1024]{1,0:T(8,128)S(1)} %bitcast_multiply_fusion.5.gain_ref), custom_call_target="tpu_custom_call" | custom-call | flops 16777216 | tf_op jit(solution)/shard_map/local/pallas_call | solution.py:377
  42.2 0.7 %collective-permute-done.9 = bf16[16,1024]{1,0:T(8,128)(2,1)S(1)} collective-permute-done((bf16[16,1024]{1,0:T(8,128)(2,1)S(1)}, bf16[16,1024]{1,0:T(8,128)(2,1)S(1)}, u32[]{:S(2)}, u32[]{:S(2)}) %collective-permute-start.9) | collective-permute-done | bytes 32800 | tf_op jit(solution)/shard_map/ppermute | solution.py:521
  42.9 0.1 fusion.7.into_ref
  42.9 2.8 %hidden.1.hidden_ref = bf16[512,1024]{1,0:T(8,128)(2,1)S(1)} custom-call(f32[128,1024]{1,0:T(8,128)S(1)} %get-tuple-element.44.ends_ref, f32[16,1024]{1,0:T(8,128)S(1)} %fusion.7.into_ref, f32[512,512]{1,0:T(8,128)S(1)} %local.2.first_ref, f32[512,512]{1,0:T(8,128)S(1)} %local.3.second_ref, f32[512,1024]{1,0:T(8,128)S(1)} %query.1.query_ref, ...), custom_call_target="tpu_custom_call" | custom-call | tf_op jit(solution)/shard_map/hidden/pallas_call | solution.py:430
  45.7 3.9 %collective-permute-start.13 = (bf16[512,1024]{1,0:T(8,128)(2,1)S(1)}, bf16[512,1024]{1,0:T(8,128)(2,1)S(1)}, u32[]{:S(2)}, u32[]{:S(2)}) collective-permute-start(bf16[512,1024]{1,0:T(8,128)(2,1)S(1)} %hidden.1.hidden_ref), channel_id=1, source_target_pairs={{0,1},{1,0},{2,3},{3,2},{4,5},{5,4},{6,7},{7,6},{8,9},{9,8},{10,11... | collective-permute-start | bytes 3145736 | tf_op jit(solution)/shard_map/ppermute | solution.py:510
  49.6 1.8 %product.1 = (f32[512,1024]{1,0:T(8,128)S(1)}, bf16[1024,1024]{1,0:T(8,128)(2,1)S(1)}) custom-call(s32[1]{0:T(128)} %bitcast.where_ref, bf16[512,1024]{1,0:T(8,128)(2,1)S(1)} %hidden.1.hidden_ref, bf16[1024,2048]{1,0:T(8,128)(2,1)S(1)} %copy-done, bf16[1024,2048]{1,0:T(8,128)(2,1)S(1)} %collective-permute-done.12.w_other_ref), custom_call_target="tpu_custom_call" | custom-call | tf_op jit(solution)/shard_map/product/pallas_call | solution.py:457
  51.5 0.4 collective-permute-done.13.other_ref
  51.9 2.6 %output.1 = f32[512,1024]{1,0:T(8,128)} custom-call(f32[512,1024]{1,0:T(8,128)S(1)} %get-tuple-element.63.part_ref, bf16[512,1024]{1,0:T(8,128)(2,1)S(1)} %collective-permute-done.13.other_ref, bf16[1024,1024]{1,0:T(8,128)(2,1)S(1)} %get-tuple-element.64.w_ref), custom_call_target="tpu_custom_call" | custom-call | tf_op jit(solution)/shard_map/output/pallas_call | solution.py:494
  (16 shorter events, 0.1 us)
Async XLA Ops:
  0.0 5.4 %collective-permute-start.1 = (bf16[512,1024]{1,0:T(8,128)(2,1)}, bf16[512,1024]{1,0:T(8,128)(2,1)S(1)}, u32[]{:S(2)}, u32[]{:S(2)}) collective-permute-start(bf16[512,1024]{1,0:T(8,128)(2,1)} %own_ref.1), channel_id=1, source_target_pairs={{0,1},{1,0},{2,3},{3,2},{4,5},{5,4},{6,7},{7,6},{8,9},{9,8},{10,11... | collective-permute-start | bytes 3145736 | tf_op jit(solution)/shard_map/ppermute | solution.py:510
  2.2 6.0 %collective-permute-start = (bf16[16,1024]{1,0:T(8,128)(2,1)S(1)}, bf16[16,1024]{1,0:T(8,128)(2,1)S(1)}, u32[]{:S(2)}, u32[]{:S(2)}) collective-permute-start(bf16[16,1024]{1,0:T(8,128)(2,1)S(1)} %slice.54), channel_id=1, source_target_pairs={{0,2},{2,4},{4,6},{6,8},{8,10},{10,12},{12,14},{14,16},{16,18},{18... | collective-permute-start | bytes 98312 | tf_op jit(solution)/shard_map/ppermute | solution.py:515
  5.4 4.1 %copy-start = (bf16[1024,2048]{1,0:T(8,128)(2,1)S(1)}, bf16[1024,2048]{1,0:T(8,128)(2,1)}, u32[]{:S(2)}) copy-start(bf16[1024,2048]{1,0:T(8,128)(2,1)} %w_ref) | copy-start | bytes 12582916
  8.2 1.3 %collective-permute-start.2 = (bf16[16,1024]{1,0:T(8,128)(2,1)S(1)}, bf16[16,1024]{1,0:T(8,128)(2,1)S(1)}, u32[]{:S(2)}, u32[]{:S(2)}) collective-permute-start(bf16[16,1024]{1,0:T(8,128)(2,1)S(1)} %collective-permute-done.halo_own_ref), channel_id=1, source_target_pairs={{0,1},{1,0},{2,3},{3,2},{4,5},{5,4},{6,7},{7,6},{8,9},{9,8},{10,11... | collective-permute-start | bytes 98312 | tf_op jit(solution)/shard_map/ppermute | solution.py:510
  9.5 40.1 %collective-permute-start.12 = (bf16[1024,2048]{1,0:T(8,128)(2,1)S(1)}, bf16[1024,2048]{1,0:T(8,128)(2,1)S(1)}, u32[]{:S(2)}, u32[]{:S(2)}) collective-permute-start(bf16[1024,2048]{1,0:T(8,128)(2,1)S(1)} %copy-done), channel_id=1, source_target_pairs={{0,1},{1,0},{2,3},{3,2},{4,5},{5,4},{6,7},{7,6},{8,9},{9,8},{10,11... | collective-permute-start | bytes 12582920 | tf_op jit(solution)/shard_map/ppermute | solution.py:510
  19.8 7.5 %collective-permute-start.3 = (bf16[16,1024]{1,0:T(8,128)(2,1)S(1)}, bf16[16,1024]{1,0:T(8,128)(2,1)S(1)}, u32[]{:S(2)}, u32[]{:S(2)}) collective-permute-start(bf16[16,1024]{1,0:T(8,128)(2,1)S(1)} %convert_element_type.36), channel_id=1, source_target_pairs={{0,2},{2,4},{4,6},{6,0},{1,3},{3,5},{5,7},{7,1},{8,10},{10,12},{12... | collective-permute-start | bytes 98312 | tf_op jit(solution)/shard_map/ppermute | solution.py:521
  21.1 6.2 %collective-permute-start.4 = (bf16[16,1024]{1,0:T(8,128)(2,1)S(1)}, bf16[16,1024]{1,0:T(8,128)(2,1)S(1)}, u32[]{:S(2)}, u32[]{:S(2)}) collective-permute-start(bf16[16,1024]{1,0:T(8,128)(2,1)S(1)} %convert_element_type.36), channel_id=1, source_target_pairs={{0,4},{2,6},{4,0},{6,2},{1,5},{3,7},{5,1},{7,3},{8,12},{10,14},{12... | collective-permute-start | bytes 98312 | tf_op jit(solution)/shard_map/ppermute | solution.py:521
  23.5 3.8 %collective-permute-start.5 = (bf16[16,1024]{1,0:T(8,128)(2,1)S(1)}, bf16[16,1024]{1,0:T(8,128)(2,1)S(1)}, u32[]{:S(2)}, u32[]{:S(2)}) collective-permute-start(bf16[16,1024]{1,0:T(8,128)(2,1)S(1)} %convert_element_type.36), channel_id=1, source_target_pairs={{0,6},{2,0},{4,2},{6,4},{1,7},{3,1},{5,3},{7,5},{8,14},{10,8},{12,... | collective-permute-start | bytes 98312 | tf_op jit(solution)/shard_map/ppermute | solution.py:521
  24.4 8.0 %copy-start.1 = (f32[1024,16]{0,1:T(8,128)S(1)}, f32[1024,16]{0,1:T(8,128)}, u32[]{:S(2)}) copy-start(f32[1024,16]{0,1:T(8,128)} %param.10) | copy-start | bytes 196612
  24.4 8.0 %copy-start.2 = (f32[1024,16]{0,1:T(8,128)S(1)}, f32[1024,16]{0,1:T(8,128)}, u32[]{:S(2)}) copy-start(f32[1024,16]{0,1:T(8,128)} %param.9) | copy-start | bytes 196612
  27.4 7.4 %collective-permute-start.6 = (bf16[16,1024]{1,0:T(8,128)(2,1)S(1)}, bf16[16,1024]{1,0:T(8,128)(2,1)S(1)}, u32[]{:S(2)}, u32[]{:S(2)}) collective-permute-start(bf16[16,1024]{1,0:T(8,128)(2,1)S(1)} %get-tuple-element.65), channel_id=1, source_target_pairs={{0,8},{8,16},{16,24},{24,0},{1,9},{9,17},{17,25},{25,1},{2,10},{10... | collective-permute-start | bytes 98312 | tf_op jit(solution)/shard_map/ppermute | solution.py:521
  28.7 6.0 %collective-permute-start.7 = (bf16[16,1024]{1,0:T(8,128)(2,1)S(1)}, bf16[16,1024]{1,0:T(8,128)(2,1)S(1)}, u32[]{:S(2)}, u32[]{:S(2)}) collective-permute-start(bf16[16,1024]{1,0:T(8,128)(2,1)S(1)} %get-tuple-element.65), channel_id=1, source_target_pairs={{0,16},{8,24},{16,0},{24,8},{1,17},{9,25},{17,1},{25,9},{2,18},{10... | collective-permute-start | bytes 98312 | tf_op jit(solution)/shard_map/ppermute | solution.py:521
  31.3 3.4 %collective-permute-start.8 = (bf16[16,1024]{1,0:T(8,128)(2,1)S(1)}, bf16[16,1024]{1,0:T(8,128)(2,1)S(1)}, u32[]{:S(2)}, u32[]{:S(2)}) collective-permute-start(bf16[16,1024]{1,0:T(8,128)(2,1)S(1)} %get-tuple-element.65), channel_id=1, source_target_pairs={{0,24},{8,0},{16,8},{24,16},{1,25},{9,1},{17,9},{25,17},{2,26},{10... | collective-permute-start | bytes 98312 | tf_op jit(solution)/shard_map/ppermute | solution.py:521
  34.8 7.4 %collective-permute-start.10 = (bf16[16,1024]{1,0:T(8,128)(2,1)S(1)}, bf16[16,1024]{1,0:T(8,128)(2,1)S(1)}, u32[]{:S(2)}, u32[]{:S(2)}) collective-permute-start(bf16[16,1024]{1,0:T(8,128)(2,1)S(1)} %fusion.14), channel_id=1, source_target_pairs={{0,64},{32,96},{64,0},{96,32},{1,65},{33,97},{65,1},{97,33},{2,66}... | collective-permute-start | bytes 98312 | tf_op jit(solution)/shard_map/ppermute | solution.py:521
  38.5 3.7 %collective-permute-start.11 = (bf16[16,1024]{1,0:T(8,128)(2,1)S(1)}, bf16[16,1024]{1,0:T(8,128)(2,1)S(1)}, u32[]{:S(2)}, u32[]{:S(2)}) collective-permute-start(bf16[16,1024]{1,0:T(8,128)(2,1)S(1)} %fusion.14), channel_id=1, source_target_pairs={{0,96},{32,0},{64,32},{96,64},{1,97},{33,1},{65,33},{97,65},{2,98}... | collective-permute-start | bytes 98312 | tf_op jit(solution)/shard_map/ppermute | solution.py:521
  38.9 4.0 %collective-permute-start.9 = (bf16[16,1024]{1,0:T(8,128)(2,1)S(1)}, bf16[16,1024]{1,0:T(8,128)(2,1)S(1)}, u32[]{:S(2)}, u32[]{:S(2)}) collective-permute-start(bf16[16,1024]{1,0:T(8,128)(2,1)S(1)} %fusion.14), channel_id=1, source_target_pairs={{0,32},{32,64},{64,96},{96,0},{1,33},{33,65},{65,97},{97,1},{2,34}... | collective-permute-start | bytes 98312 | tf_op jit(solution)/shard_map/ppermute | solution.py:521
  45.7 6.2 %collective-permute-start.13 = (bf16[512,1024]{1,0:T(8,128)(2,1)S(1)}, bf16[512,1024]{1,0:T(8,128)(2,1)S(1)}, u32[]{:S(2)}, u32[]{:S(2)}) collective-permute-start(bf16[512,1024]{1,0:T(8,128)(2,1)S(1)} %hidden.1.hidden_ref), channel_id=1, source_target_pairs={{0,1},{1,0},{2,3},{3,2},{4,5},{5,4},{6,7},{7,6},{8,9},{9,8},{10,11... | collective-permute-start | bytes 3145736 | tf_op jit(solution)/shard_map/ppermute | solution.py:510

commit v4 on v2

--- a/solution.py
+++ b/solution.py
@@ -332,87 +332,88 @@
     )(where, *args)
 
 
-def local_kernel(first, source_ref, rates_ref, gain_ref, local_ref):
+def local_kernel(first, source_ref, ends_ref, rates_ref, gain_ref, local_ref, base_ref, factor_ref):
     rows, channels = local_ref.shape
+    steps = rows // SEGS
     modes = rates_ref.shape[0]
+    seg = lax.broadcasted_iota(jnp.int32, (SEGS, LANES), 0)
     for i in range(channels // LANES):
         lanes = slice(first + i * LANES, first + (i + 1) * LANES)
-        decays = [spread(jnp.exp(-rates_ref[n : n + 1, lanes])) for n in range(modes)]
+        here = slice(i * LANES, (i + 1) * LANES)
+        rates = [spread(rates_ref[n : n + 1, lanes]) for n in range(modes)]
         gains = [spread(gain_ref[n : n + 1, lanes]) for n in range(modes)]
-
-        def body(t, states, i=i, lanes=lanes, decays=decays, gains=gains):
-            row = pl.ds(pl.multiple_of(t * SEGS, SEGS), SEGS)
+        for n in range(modes):
+            mode = slice(n * SEGS, (n + 1) * SEGS)
+            state = jnp.where(seg >= 1, pltpu.roll(ends_ref[mode, lanes], 1, 0), 0.0)
+            for hop in (1, 2, 4):
+                earlier = pltpu.roll(state, hop, 0) * jnp.exp(-rates[n] * float(steps * hop))
+                state = state + jnp.where(seg >= hop, earlier, 0.0)
+            base_ref[mode, here] = gains[n] * state
+            factor_ref[mode, here] = gains[n] * jnp.exp(-rates[n] * (seg * steps).astype(F32))
+        decays = [jnp.exp(-rate) for rate in rates]
+        states = [jnp.zeros((SEGS, LANES), F32)] * modes
+        for t in range(steps):
+            row = slice(t * SEGS, (t + 1) * SEGS)
             source = source_ref[row, lanes]
-            states = tuple(d * s + source for d, s in zip(decays, states))
-            local_ref[row, i * LANES : (i + 1) * LANES] = tree_sum(
-                [g * s for g, s in zip(gains, states)]
-            )
-            return states
-
-        zero = jnp.zeros((SEGS, LANES), F32)
-        lax.fori_loop(0, rows // SEGS, body, (zero,) * modes, unroll=16)
-
-
-def local_call(source, rates, gain, part):
+            states = [d * s + source for d, s in zip(decays, states)]
+            local_ref[row, here] = tree_sum([g * s for g, s in zip(gains, states)])
+
+
+def local_call(source, ends, rates, gain, part):
     rows, channels = source.shape
-    vmem = pl.BlockSpec(memory_space=pltpu.VMEM)
-    args = [pltpu.with_memory_space_constraint(x, pltpu.VMEM) for x in (source, rates, gain)]
-    return pl.pallas_call(
-        functools.partial(local_kernel, part * channels // PARTS),
-        in_specs=[vmem] * 3,
-        out_specs=vmem,
-        out_shape=pltpu.VMEM((rows, channels // PARTS), F32),
+    wide = channels // PARTS
+    vmem = pl.BlockSpec(memory_space=pltpu.VMEM)
+    args = [pltpu.with_memory_space_constraint(x, pltpu.VMEM) for x in (source, ends, rates, gain)]
+    return pl.pallas_call(
+        functools.partial(local_kernel, part * wide),
+        in_specs=[vmem] * 4,
+        out_specs=[vmem] * 3,
+        out_shape=[
+            pltpu.VMEM((rows, wide), F32),
+            pltpu.VMEM((ends.shape[0], wide), F32),
+            pltpu.VMEM((ends.shape[0], wide), F32),
+        ],
         compiler_params=pltpu.CompilerParams(vmem_limit_bytes=4 * MIB),
         cost_estimate=pl.CostEstimate(
-            flops=4 * rates.shape[0] * rows * channels // PARTS, transcendentals=0, bytes_accessed=0
+            flops=4 * rates.shape[0] * rows * wide, transcendentals=0, bytes_accessed=0
         ),
         name="local",
     )(*args)
 
 
-def hidden_kernel(ends_ref, into_ref, first_ref, second_ref, query_ref, rates_ref, gain_ref, hidden_ref):
+def hidden_kernel(into_ref, query_ref, rates_ref, *refs):
+    hidden_ref = refs[-1]
     rows, channels = query_ref.shape
-    steps = rows // SEGS
     modes = rates_ref.shape[0]
-    local_refs = (first_ref, second_ref)
-    seg = lax.broadcasted_iota(jnp.int32, (SEGS, LANES), 0)
+    wide = channels // PARTS
     for i in range(channels // LANES):
         lanes = slice(i * LANES, (i + 1) * LANES)
-        local_ref = local_refs[i * LANES * PARTS // channels]
-        here = slice(lanes.start % (channels // PARTS), lanes.start % (channels // PARTS) + LANES)
+        part = i * LANES // wide
+        local_ref, base_ref, factor_ref = refs[3 * part : 3 * part + 3]
+        here = slice(lanes.start - part * wide, lanes.stop - part * wide)
         decays, leads = [], []
         for n in range(modes):
-            rate = spread(rates_ref[n : n + 1, lanes])
-            state = pltpu.roll(ends_ref[n * SEGS : (n + 1) * SEGS, lanes], 1, 0)
-            state = jnp.where(seg == 0, spread(into_ref[n : n + 1, lanes]), state)
-            for hop in (1, 2, 4):
-                earlier = pltpu.roll(state, hop, 0) * jnp.exp(-rate * float(steps * hop))
-                state = state + jnp.where(seg >= hop, earlier, 0.0)
-            decays.append(jnp.exp(-rate))
-            leads.append(spread(gain_ref[n : n + 1, lanes]) * state)
-
-        def body(t, leads, lanes=lanes, here=here, local_ref=local_ref, decays=decays):
+            mode = slice(n * SEGS, (n + 1) * SEGS)
+            decays.append(spread(jnp.exp(-rates_ref[n : n + 1, lanes])))
+            incoming = spread(into_ref[n : n + 1, lanes])
+            leads.append(base_ref[mode, here] + factor_ref[mode, here] * incoming)
+        for t in range(0, rows, 2 * SEGS):
             halves = []
-            for u in range(2):
-                row = pl.ds(pl.multiple_of((2 * t + u) * SEGS, SEGS), SEGS)
-                leads = tuple(d * s for d, s in zip(decays, leads))
+            for row in (slice(t, t + SEGS), slice(t + SEGS, t + 2 * SEGS)):
+                leads = [d * s for d, s in zip(decays, leads)]
                 halves.append(query_ref[row, lanes] * (local_ref[row, here] + tree_sum(leads)))
-            row = pl.ds(pl.multiple_of(2 * t * SEGS, 2 * SEGS), 2 * SEGS)
-            hidden_ref[row, lanes] = jnp.concatenate(halves, axis=0).astype(BF16)
-            return leads
-
-        lax.fori_loop(0, steps // 2, body, tuple(leads), unroll=8)
-
-
-def hidden_call(ends, into, local, query, rates, gain):
+            hidden_ref[t : t + 2 * SEGS, lanes] = jnp.concatenate(halves, axis=0).astype(BF16)
+
+
+def hidden_call(into, query, rates, parts):
     vmem = pl.BlockSpec(memory_space=pltpu.VMEM)
     args = [
         pltpu.with_memory_space_constraint(x, pltpu.VMEM)
-        for x in (ends, into, *local, query, rates, gain)
+        for x in (into, query, rates, *(ref for part in parts for ref in part))
     ]
     return pl.pallas_call(
         hidden_kernel,
-        in_specs=[vmem] * 7,
+        in_specs=[vmem] * len(args),
         out_specs=vmem,
         out_shape=pltpu.VMEM(query.shape, BF16),
         compiler_params=pltpu.CompilerParams(vmem_limit_bytes=4 * MIB),
@@ -526,7 +527,7 @@
     )
     beside = [
         query_call(where, lhs, halo_own, halo_other, query_weight, filt),
-        *[local_call(source, rates, gain, part) for part in range(PARTS)],
+        *[local_call(source, ends, rates, gain, part) for part in range(PARTS)],
     ]
 
     into = 0.0
@@ -539,7 +540,7 @@
             into = into + into_weights[(RING - 1) * level + k] * part
             total = total + total_weights[RING * level + k + 1] * part
 
-    hidden = hidden_call(ends, into, beside[1:], beside[0], rates, gain)
+    hidden = hidden_call(into, beside[0], rates, beside[1:])
     part, partner_weight = product_call(where, hidden, out_weight, out_weight_other)
     return output_call(part, swapped(hidden), partner_weight)
 

time: 53.7 us -> 52.6 us (0.980)
    pallas_call x3, Pallas kernels: 7.97 us -> 7.43 us  [the longest x2 5.02 us: local_call(): pl.pallas_call(functools.partial(local_kernel, part * wide), in_specs=[vm...]
where the time goes in v4:
time: 52.6 us; the launch traced here: 52.4 us
  Pallas kernels  25.7 us (49%)
  starting transfers between devices  23.7 us (45%)
  waiting for transfers between devices  1.68 us (3%)
  local copies, waits for them, and re-layouts  0.77 us (1%)
    ppermute x9, starting transfers between devices, round_the_ring(): lax.ppermute(sent, axis, [(i, (i + k) % RING) for i in range(RING)])  14.8 us
    pallas_call x1, Pallas kernels, front_call(): pl.pallas_call(front_kernel, in_specs=[pl.BlockSpec(memory_space=pltpu.SM...  6.92 us
    ppermute x4, starting transfers between devices, swapped(): return lax.ppermute(x, 'ch', [(0, 1), (1, 0)])  5.77 us
    pallas_call x2, Pallas kernels, local_call(): pl.pallas_call(functools.partial(local_kernel, part * wide), in_specs=[vm...  5.02 us
    pallas_call x1, Pallas kernels, stage_call(): pl.pallas_call(stage_kernel, in_specs=[pl.BlockSpec(memory_space=pltpu.SM...  3.96 us
    ppermute x1, starting transfers between devices, from_before(): return lax.ppermute(x, SEQ, [(i, i + 1) for i in range(count - 1)])  3.19 us
    pallas_call x1, Pallas kernels, query_call(): pl.pallas_call(query_kernel, in_specs=[pl.BlockSpec(memory_space=pltpu.SM...  2.89 us
    pallas_call x1, Pallas kernels, output_call(): pl.pallas_call(output_kernel, in_specs=[vmem] * 3, out_specs=pl.BlockSpec...  2.57 us
  transfers between devices with their start and end apart: 14, of which 3 were waited for; matrix products, arithmetic and copies ran while one was open for 2% of the time, Pallas kernels for 44%

profile of v4, /device:TPU:1, one launch (start us, length us, event | category | flops | bytes accessed | tf_op | source)
XLA Modules:
  0.0 52.4 jit_solution(10447679968150562845)
XLA Ops:
  0.0 1.4 %collective-permute-start = (bf16[512,1024]{1,0:T(8,128)(2,1)}, bf16[512,1024]{1,0:T(8,128)(2,1)S(1)}, u32[]{:S(2)}, u32[]{:S(2)}) collective-permute-start(bf16[512,1024]{1,0:T(8,128)(2,1)} %own_ref.1), channel_id=1, source_target_pairs={{0,1},{1,0},{2,3},{3,2},{4,5},{5,4},{6,7},{7,6},{8,9},{9,8},{10,11... | collective-permute-start | bytes 3145736 | tf_op jit(solution)/shard_map/ppermute | solution.py:494
  1.4 0.8 %slice.55 = bf16[16,1024]{1,0:T(8,128)(2,1)S(1)} slice(bf16[512,1024]{1,0:T(8,128)(2,1)} %own_ref.1), slice={[496:512], [0:1024]} | slice | bytes 65536 | tf_op jit(solution)/shard_map/slice | solution.py:517
  2.2 3.2 %collective-permute-start.1 = (bf16[16,1024]{1,0:T(8,128)(2,1)S(1)}, bf16[16,1024]{1,0:T(8,128)(2,1)S(1)}, u32[]{:S(2)}, u32[]{:S(2)}) collective-permute-start(bf16[16,1024]{1,0:T(8,128)(2,1)S(1)} %slice.55), channel_id=1, source_target_pairs={{0,2},{2,4},{4,6},{6,8},{8,10},{10,12},{12,14},{14,16},{16,18},{18... | collective-permute-start | bytes 98312 | tf_op jit(solution)/shard_map/ppermute | solution.py:499
  5.4 0.0 collective-permute-done.other_ref
  5.4 0.0 copy-start
  5.4 4.0 %stage.1 = (bf16[512,2048]{1,0:T(8,128)(2,1)S(1)}, bf16[2,2048,1024]{2,1,0:T(8,128)(2,1)S(1)}, f32[3,3,1024]{2,1,0:T(4,128)S(1)}, f32[16,1024]{1,0:T(8,128)S(1)}...) custom-call(s32[1]{0:T(128)} %bitcast.where_ref, bf16[512,1024]{1,0:T(8,128)(2,1)} %own_ref.1, ...), custom_call_target="tpu_custom_call" | custom-call | tf_op jit(solution)/shard_map/stage/pallas_call | solution.py:94
  9.4 0.4 collective-permute-start.2
  9.8 0.9 %collective-permute-done.2.halo_other_ref = bf16[16,1024]{1,0:T(8,128)(2,1)S(1)} collective-permute-done((bf16[16,1024]{1,0:T(8,128)(2,1)S(1)}, bf16[16,1024]{1,0:T(8,128)(2,1)S(1)}, u32[]{:S(2)}, u32[]{:S(2)}) %collective-permute-start.2) | collective-permute-done | bytes 32800 | tf_op jit(solution)/shard_map/ppermute | solution.py:494
  10.7 0.3 collective-permute-start.12
  11.0 6.9 %front.1 = (f32[512,1024]{1,0:T(8,128)S(1)}, f32[128,1024]{1,0:T(8,128)S(1)}, f32[16,1024]{1,0:T(8,128)S(1)}, bf16[2048,1024]{1,0:T(8,128)(2,1)S(1)}) custom-call(s32[1]{0:T(128)} %bitcast.where_ref, bf16[512,2048]{1,0:T(8,128)(2,1)S(1)} %get-tuple-element.50.lhs_ref, bf16[16,1024]{1,0:T(8,128)(2,1)S(1)} %collective-permute-done.1.halo_own_ref, ...), custom_call_target="tpu_custom_call" | custom-call | tf_op jit(solution)/shard_map/front/pallas_call | solution.py:255
  17.9 1.3 %collective-permute-start.3 = (bf16[16,1024]{1,0:T(8,128)(2,1)S(1)}, bf16[16,1024]{1,0:T(8,128)(2,1)S(1)}, u32[]{:S(2)}, u32[]{:S(2)}) collective-permute-start(bf16[16,1024]{1,0:T(8,128)(2,1)S(1)} %convert_element_type.36), channel_id=1, source_target_pairs={{0,2},{2,4},{4,6},{6,0},{1,3},{3,5},{5,7},{7,1},{8,10},{10,12},{12... | collective-permute-start | bytes 98312 | tf_op jit(solution)/shard_map/ppermute | solution.py:505
  19.2 2.4 %collective-permute-start.4 = (bf16[16,1024]{1,0:T(8,128)(2,1)S(1)}, bf16[16,1024]{1,0:T(8,128)(2,1)S(1)}, u32[]{:S(2)}, u32[]{:S(2)}) collective-permute-start(bf16[16,1024]{1,0:T(8,128)(2,1)S(1)} %convert_element_type.36), channel_id=1, source_target_pairs={{0,4},{2,6},{4,0},{6,2},{1,5},{3,7},{5,1},{7,3},{8,12},{10,14},{12... | collective-permute-start | bytes 98312 | tf_op jit(solution)/shard_map/ppermute | solution.py:505
  21.6 0.9 %collective-permute-start.5 = (bf16[16,1024]{1,0:T(8,128)(2,1)S(1)}, bf16[16,1024]{1,0:T(8,128)(2,1)S(1)}, u32[]{:S(2)}, u32[]{:S(2)}) collective-permute-start(bf16[16,1024]{1,0:T(8,128)(2,1)S(1)} %convert_element_type.36), channel_id=1, source_target_pairs={{0,6},{2,0},{4,2},{6,4},{1,7},{3,1},{5,3},{7,5},{8,14},{10,8},{12,... | collective-permute-start | bytes 98312 | tf_op jit(solution)/shard_map/ppermute | solution.py:505
  22.5 2.9 %query.1.query_ref = f32[512,1024]{1,0:T(8,128)S(1)} custom-call(s32[1]{0:T(128)} %bitcast.where_ref, bf16[512,2048]{1,0:T(8,128)(2,1)S(1)} %get-tuple-element.50.lhs_ref, bf16[16,1024]{1,0:T(8,128)(2,1)S(1)} %collective-permute-done.1.halo_own_ref, bf16[16,1024]{1,0:T(8,128)(2,1)S(1)} %collective-permute-done.2.halo_other_ref, ...), custom_call_target="tpu_custom_call" | custom-call | flops 2214592512 | tf_op jit(solution)/shard_map/query/pallas_call | solution.py:318
  25.4 0.0 collective-permute-done.4
  25.4 0.0 collective-permute-done.5
  25.5 1.4 %collective-permute-start.6 = (bf16[16,1024]{1,0:T(8,128)(2,1)S(1)}, bf16[16,1024]{1,0:T(8,128)(2,1)S(1)}, u32[]{:S(2)}, u32[]{:S(2)}) collective-permute-start(bf16[16,1024]{1,0:T(8,128)(2,1)S(1)} %get-tuple-element.85), channel_id=1, source_target_pairs={{0,8},{8,16},{16,24},{24,0},{1,9},{9,17},{17,25},{25,1},{2,10},{10... | collective-permute-start | bytes 98312 | tf_op jit(solution)/shard_map/ppermute | solution.py:505
  26.8 2.6 %collective-permute-start.7 = (bf16[16,1024]{1,0:T(8,128)(2,1)S(1)}, bf16[16,1024]{1,0:T(8,128)(2,1)S(1)}, u32[]{:S(2)}, u32[]{:S(2)}) collective-permute-start(bf16[16,1024]{1,0:T(8,128)(2,1)S(1)} %get-tuple-element.85), channel_id=1, source_target_pairs={{0,16},{8,24},{16,0},{24,8},{1,17},{9,25},{17,1},{25,9},{2,18},{10... | collective-permute-start | bytes 98312 | tf_op jit(solution)/shard_map/ppermute | solution.py:505
  29.5 1.1 %collective-permute-start.8 = (bf16[16,1024]{1,0:T(8,128)(2,1)S(1)}, bf16[16,1024]{1,0:T(8,128)(2,1)S(1)}, u32[]{:S(2)}, u32[]{:S(2)}) collective-permute-start(bf16[16,1024]{1,0:T(8,128)(2,1)S(1)} %get-tuple-element.85), channel_id=1, source_target_pairs={{0,24},{8,0},{16,8},{24,16},{1,25},{9,1},{17,9},{25,17},{2,26},{10... | collective-permute-start | bytes 98312 | tf_op jit(solution)/shard_map/ppermute | solution.py:505
  30.6 2.5 %local.2 = (f32[512,512]{1,0:T(8,128)S(1)}, f32[128,512]{1,0:T(8,128)S(1)}, f32[128,512]{1,0:T(8,128)S(1)}) custom-call(f32[512,1024]{1,0:T(8,128)S(1)} %get-tuple-element.60.source_ref, f32[128,1024]{1,0:T(8,128)S(1)} %get-tuple-element.61.ends_ref, f32[16,1024]{1,0:T(8,128)S(1)} %get-tuple-element.54.rates_ref, f32[16,1024]{1,0:T(8,128)S(1)} %bitcast_multiply_fusion.5.gain_ref), custom_call_target="tpu_custom_call" | custom-call | flops 16777216 | tf_op jit(solution)/shard_map/local/pallas_call | solution.py:367
  33.1 0.0 collective-permute-done.7
  33.2 3.7 %collective-permute-start.10 = (bf16[16,1024]{1,0:T(8,128)(2,1)S(1)}, bf16[16,1024]{1,0:T(8,128)(2,1)S(1)}, u32[]{:S(2)}, u32[]{:S(2)}) collective-permute-start(bf16[16,1024]{1,0:T(8,128)(2,1)S(1)} %fusion.14), channel_id=1, source_target_pairs={{0,64},{32,96},{64,0},{96,32},{1,65},{33,97},{65,1},{97,33},{2,66}... | collective-permute-start | bytes 98312 | tf_op jit(solution)/shard_map/ppermute | solution.py:505
  36.8 0.4 collective-permute-start.11
  37.3 1.0 %collective-permute-start.9 = (bf16[16,1024]{1,0:T(8,128)(2,1)S(1)}, bf16[16,1024]{1,0:T(8,128)(2,1)S(1)}, u32[]{:S(2)}, u32[]{:S(2)}) collective-permute-start(bf16[16,1024]{1,0:T(8,128)(2,1)S(1)} %fusion.14), channel_id=1, source_target_pairs={{0,32},{32,64},{64,96},{96,0},{1,33},{33,65},{65,97},{97,1},{2,34}... | collective-permute-start | bytes 98312 | tf_op jit(solution)/shard_map/ppermute | solution.py:505
  38.3 2.5 %local.3 = (f32[512,512]{1,0:T(8,128)S(1)}, f32[128,512]{1,0:T(8,128)S(1)}, f32[128,512]{1,0:T(8,128)S(1)}) custom-call(f32[512,1024]{1,0:T(8,128)S(1)} %get-tuple-element.60.source_ref, f32[128,1024]{1,0:T(8,128)S(1)} %get-tuple-element.61.ends_ref, f32[16,1024]{1,0:T(8,128)S(1)} %get-tuple-element.54.rates_ref, f32[16,1024]{1,0:T(8,128)S(1)} %bitcast_multiply_fusion.5.gain_ref), custom_call_target="tpu_custom_call" | custom-call | flops 16777216 | tf_op jit(solution)/shard_map/local/pallas_call | solution.py:367
  40.8 0.4 collective-permute-done.9
  41.2 0.1 fusion.7.into_ref
  41.3 2.4 %hidden.1.hidden_ref = bf16[512,1024]{1,0:T(8,128)(2,1)S(1)} custom-call(f32[16,1024]{1,0:T(8,128)S(1)} %fusion.7.into_ref, f32[512,1024]{1,0:T(8,128)S(1)} %query.1.query_ref, f32[16,1024]{1,0:T(8,128)S(1)} %get-tuple-element.54.rates_ref, f32[512,512]{1,0:T(8,128)S(1)} %get-tuple-element.76.refs_0_, f32[128,512]{1,0:T(8,128)S(1)} %get-tuple-element.77.refs_1_, ...), custom_call_target="tpu_custom_call" | custom-call | tf_op jit(solution)/shard_map/hidden/pallas_call | solution.py:414
  43.7 3.7 %collective-permute-start.13 = (bf16[512,1024]{1,0:T(8,128)(2,1)S(1)}, bf16[512,1024]{1,0:T(8,128)(2,1)S(1)}, u32[]{:S(2)}, u32[]{:S(2)}) collective-permute-start(bf16[512,1024]{1,0:T(8,128)(2,1)S(1)} %hidden.1.hidden_ref), channel_id=1, source_target_pairs={{0,1},{1,0},{2,3},{3,2},{4,5},{5,4},{6,7},{7,6},{8,9},{9,8},{10,11... | collective-permute-start | bytes 3145736 | tf_op jit(solution)/shard_map/ppermute | solution.py:494
  47.4 2.0 %product.1 = (f32[512,1024]{1,0:T(8,128)S(1)}, bf16[1024,1024]{1,0:T(8,128)(2,1)S(1)}) custom-call(s32[1]{0:T(128)} %bitcast.where_ref, bf16[512,1024]{1,0:T(8,128)(2,1)S(1)} %hidden.1.hidden_ref, bf16[1024,2048]{1,0:T(8,128)(2,1)S(1)} %copy-done, bf16[1024,2048]{1,0:T(8,128)(2,1)S(1)} %collective-permute-done.12.w_other_ref), custom_call_target="tpu_custom_call" | custom-call | tf_op jit(solution)/shard_map/product/pallas_call | solution.py:441
  49.4 0.3 collective-permute-done.13.other_ref
  49.7 2.6 %output.1 = f32[512,1024]{1,0:T(8,128)} custom-call(f32[512,1024]{1,0:T(8,128)S(1)} %get-tuple-element.83.part_ref, bf16[512,1024]{1,0:T(8,128)(2,1)S(1)} %collective-permute-done.13.other_ref, bf16[1024,1024]{1,0:T(8,128)(2,1)S(1)} %get-tuple-element.84.w_ref), custom_call_target="tpu_custom_call" | custom-call | tf_op jit(solution)/shard_map/output/pallas_call | solution.py:478
  (16 shorter events, 0.1 us)
Async XLA Ops:
  0.0 5.4 %collective-permute-start = (bf16[512,1024]{1,0:T(8,128)(2,1)}, bf16[512,1024]{1,0:T(8,128)(2,1)S(1)}, u32[]{:S(2)}, u32[]{:S(2)}) collective-permute-start(bf16[512,1024]{1,0:T(8,128)(2,1)} %own_ref.1), channel_id=1, source_target_pairs={{0,1},{1,0},{2,3},{3,2},{4,5},{5,4},{6,7},{7,6},{8,9},{9,8},{10,11... | collective-permute-start | bytes 3145736 | tf_op jit(solution)/shard_map/ppermute | solution.py:494
  2.2 7.2 %collective-permute-start.1 = (bf16[16,1024]{1,0:T(8,128)(2,1)S(1)}, bf16[16,1024]{1,0:T(8,128)(2,1)S(1)}, u32[]{:S(2)}, u32[]{:S(2)}) collective-permute-start(bf16[16,1024]{1,0:T(8,128)(2,1)S(1)} %slice.55), channel_id=1, source_target_pairs={{0,2},{2,4},{4,6},{6,8},{8,10},{10,12},{12,14},{14,16},{16,18},{18... | collective-permute-start | bytes 98312 | tf_op jit(solution)/shard_map/ppermute | solution.py:499
  5.4 5.3 %copy-start = (bf16[1024,2048]{1,0:T(8,128)(2,1)S(1)}, bf16[1024,2048]{1,0:T(8,128)(2,1)}, u32[]{:S(2)}) copy-start(bf16[1024,2048]{1,0:T(8,128)(2,1)} %w_ref) | copy-start | bytes 12582916
  9.4 1.3 %collective-permute-start.2 = (bf16[16,1024]{1,0:T(8,128)(2,1)S(1)}, bf16[16,1024]{1,0:T(8,128)(2,1)S(1)}, u32[]{:S(2)}, u32[]{:S(2)}) collective-permute-start(bf16[16,1024]{1,0:T(8,128)(2,1)S(1)} %collective-permute-done.1.halo_own_ref), channel_id=1, source_target_pairs={{0,1},{1,0},{2,3},{3,2},{4,5},{5,4},{6,7},{7,6},{8,9},{9,8},{10,11... | collective-permute-start | bytes 98312 | tf_op jit(solution)/shard_map/ppermute | solution.py:494
  10.7 36.7 %collective-permute-start.12 = (bf16[1024,2048]{1,0:T(8,128)(2,1)S(1)}, bf16[1024,2048]{1,0:T(8,128)(2,1)S(1)}, u32[]{:S(2)}, u32[]{:S(2)}) collective-permute-start(bf16[1024,2048]{1,0:T(8,128)(2,1)S(1)} %copy-done), channel_id=1, source_target_pairs={{0,1},{1,0},{2,3},{3,2},{4,5},{5,4},{6,7},{7,6},{8,9},{9,8},{10,11... | collective-permute-start | bytes 12582920 | tf_op jit(solution)/shard_map/ppermute | solution.py:494
  17.9 7.5 %collective-permute-start.3 = (bf16[16,1024]{1,0:T(8,128)(2,1)S(1)}, bf16[16,1024]{1,0:T(8,128)(2,1)S(1)}, u32[]{:S(2)}, u32[]{:S(2)}) collective-permute-start(bf16[16,1024]{1,0:T(8,128)(2,1)S(1)} %convert_element_type.36), channel_id=1, source_target_pairs={{0,2},{2,4},{4,6},{6,0},{1,3},{3,5},{5,7},{7,1},{8,10},{10,12},{12... | collective-permute-start | bytes 98312 | tf_op jit(solution)/shard_map/ppermute | solution.py:505
  19.2 6.2 %collective-permute-start.4 = (bf16[16,1024]{1,0:T(8,128)(2,1)S(1)}, bf16[16,1024]{1,0:T(8,128)(2,1)S(1)}, u32[]{:S(2)}, u32[]{:S(2)}) collective-permute-start(bf16[16,1024]{1,0:T(8,128)(2,1)S(1)} %convert_element_type.36), channel_id=1, source_target_pairs={{0,4},{2,6},{4,0},{6,2},{1,5},{3,7},{5,1},{7,3},{8,12},{10,14},{12... | collective-permute-start | bytes 98312 | tf_op jit(solution)/shard_map/ppermute | solution.py:505
  21.6 3.8 %collective-permute-start.5 = (bf16[16,1024]{1,0:T(8,128)(2,1)S(1)}, bf16[16,1024]{1,0:T(8,128)(2,1)S(1)}, u32[]{:S(2)}, u32[]{:S(2)}) collective-permute-start(bf16[16,1024]{1,0:T(8,128)(2,1)S(1)} %convert_element_type.36), channel_id=1, source_target_pairs={{0,6},{2,0},{4,2},{6,4},{1,7},{3,1},{5,3},{7,5},{8,14},{10,8},{12,... | collective-permute-start | bytes 98312 | tf_op jit(solution)/shard_map/ppermute | solution.py:505
  22.5 8.0 %copy-start.1 = (f32[1024,16]{0,1:T(8,128)S(1)}, f32[1024,16]{0,1:T(8,128)}, u32[]{:S(2)}) copy-start(f32[1024,16]{0,1:T(8,128)} %param.10) | copy-start | bytes 196612
  22.5 8.0 %copy-start.2 = (f32[1024,16]{0,1:T(8,128)S(1)}, f32[1024,16]{0,1:T(8,128)}, u32[]{:S(2)}) copy-start(f32[1024,16]{0,1:T(8,128)} %param.9) | copy-start | bytes 196612
  25.5 7.6 %collective-permute-start.6 = (bf16[16,1024]{1,0:T(8,128)(2,1)S(1)}, bf16[16,1024]{1,0:T(8,128)(2,1)S(1)}, u32[]{:S(2)}, u32[]{:S(2)}) collective-permute-start(bf16[16,1024]{1,0:T(8,128)(2,1)S(1)} %get-tuple-element.85), channel_id=1, source_target_pairs={{0,8},{8,16},{16,24},{24,0},{1,9},{9,17},{17,25},{25,1},{2,10},{10... | collective-permute-start | bytes 98312 | tf_op jit(solution)/shard_map/ppermute | solution.py:505
  26.8 6.3 %collective-permute-start.7 = (bf16[16,1024]{1,0:T(8,128)(2,1)S(1)}, bf16[16,1024]{1,0:T(8,128)(2,1)S(1)}, u32[]{:S(2)}, u32[]{:S(2)}) collective-permute-start(bf16[16,1024]{1,0:T(8,128)(2,1)S(1)} %get-tuple-element.85), channel_id=1, source_target_pairs={{0,16},{8,24},{16,0},{24,8},{1,17},{9,25},{17,1},{25,9},{2,18},{10... | collective-permute-start | bytes 98312 | tf_op jit(solution)/shard_map/ppermute | solution.py:505
  29.5 3.7 %collective-permute-start.8 = (bf16[16,1024]{1,0:T(8,128)(2,1)S(1)}, bf16[16,1024]{1,0:T(8,128)(2,1)S(1)}, u32[]{:S(2)}, u32[]{:S(2)}) collective-permute-start(bf16[16,1024]{1,0:T(8,128)(2,1)S(1)} %get-tuple-element.85), channel_id=1, source_target_pairs={{0,24},{8,0},{16,8},{24,16},{1,25},{9,1},{17,9},{25,17},{2,26},{10... | collective-permute-start | bytes 98312 | tf_op jit(solution)/shard_map/ppermute | solution.py:505
  33.2 7.7 %collective-permute-start.10 = (bf16[16,1024]{1,0:T(8,128)(2,1)S(1)}, bf16[16,1024]{1,0:T(8,128)(2,1)S(1)}, u32[]{:S(2)}, u32[]{:S(2)}) collective-permute-start(bf16[16,1024]{1,0:T(8,128)(2,1)S(1)} %fusion.14), channel_id=1, source_target_pairs={{0,64},{32,96},{64,0},{96,32},{1,65},{33,97},{65,1},{97,33},{2,66}... | collective-permute-start | bytes 98312 | tf_op jit(solution)/shard_map/ppermute | solution.py:505
  36.8 4.0 %collective-permute-start.11 = (bf16[16,1024]{1,0:T(8,128)(2,1)S(1)}, bf16[16,1024]{1,0:T(8,128)(2,1)S(1)}, u32[]{:S(2)}, u32[]{:S(2)}) collective-permute-start(bf16[16,1024]{1,0:T(8,128)(2,1)S(1)} %fusion.14), channel_id=1, source_target_pairs={{0,96},{32,0},{64,32},{96,64},{1,97},{33,1},{65,33},{97,65},{2,98}... | collective-permute-start | bytes 98312 | tf_op jit(solution)/shard_map/ppermute | solution.py:505
  37.3 4.0 %collective-permute-start.9 = (bf16[16,1024]{1,0:T(8,128)(2,1)S(1)}, bf16[16,1024]{1,0:T(8,128)(2,1)S(1)}, u32[]{:S(2)}, u32[]{:S(2)}) collective-permute-start(bf16[16,1024]{1,0:T(8,128)(2,1)S(1)} %fusion.14), channel_id=1, source_target_pairs={{0,32},{32,64},{64,96},{96,0},{1,33},{33,65},{65,97},{97,1},{2,34}... | collective-permute-start | bytes 98312 | tf_op jit(solution)/shard_map/ppermute | solution.py:505
  43.7 6.0 %collective-permute-start.13 = (bf16[512,1024]{1,0:T(8,128)(2,1)S(1)}, bf16[512,1024]{1,0:T(8,128)(2,1)S(1)}, u32[]{:S(2)}, u32[]{:S(2)}) collective-permute-start(bf16[512,1024]{1,0:T(8,128)(2,1)S(1)} %hidden.1.hidden_ref), channel_id=1, source_target_pairs={{0,1},{1,0},{2,3},{3,2},{4,5},{5,4},{6,7},{7,6},{8,9},{9,8},{10,11... | collective-permute-start | bytes 3145736 | tf_op jit(solution)/shard_map/ppermute | solution.py:494

commit v5 on v4

--- a/solution.py
+++ b/solution.py
@@ -145,16 +145,19 @@
     halo_other_ref,
     w_ref,
     wq_ref,
+    wout_ref,
     filt_ref,
     rates_ref,
     source_ref,
     ends_ref,
     total_ref,
     staged_ref,
+    mine_ref,
+    theirs_ref,
     halo_ref,
     proj_a,
     proj_b,
-    sem,
+    sems,
 ):
     rows = lhs_ref.shape[0]
     steps = rows // SEGS
@@ -165,8 +168,22 @@
     per = SEGS // 2
     proj = (proj_a, proj_b)
 
-    stage = pltpu.make_async_copy(wq_ref.at[0], staged_ref, sem)
-    stage.start()
+    columns = mine_ref.shape[1]
+    core = lax.rem(where_ref[0], 2)
+    mine = pl.ds(pl.multiple_of(core * columns, columns), columns)
+    theirs = pl.ds(pl.multiple_of((1 - core) * columns, columns), columns)
+    stages = [
+        pltpu.make_async_copy(src, dst, sems.at[i])
+        for i, (src, dst) in enumerate(
+            (
+                (wq_ref.at[0], staged_ref),
+                (wout_ref.at[:, theirs], theirs_ref),
+                (wout_ref.at[:, mine], mine_ref),
+            )
+        )
+    ]
+    for stage in stages:
+        stage.start()
     join_halo(where_ref, halo_ref, halo_own_ref, halo_other_ref)
 
     def projection(tile):
@@ -243,10 +260,11 @@
             for step in fast[done:upto]:
                 step()
             done = upto
-    stage.wait()
-
-
-def front_call(where, lhs, halo_own, halo_other, staged, weight, filt, rates):
+    for stage in stages:
+        stage.wait()
+
+
+def front_call(where, lhs, halo_own, halo_other, staged, weight, out_weight, filt, rates):
     rows, full = lhs.shape
     streams, _, channels = staged.shape
     modes = rates.shape[0]
@@ -256,16 +274,18 @@
         front_kernel,
         in_specs=[pl.BlockSpec(memory_space=pltpu.SMEM)]
         + [vmem] * 4
-        + [pl.BlockSpec(memory_space=pl.ANY)]
+        + [pl.BlockSpec(memory_space=pl.ANY)] * 2
         + [vmem] * 2,
-        out_specs=[vmem] * 4,
+        out_specs=[vmem] * 6,
         out_shape=[
             pltpu.VMEM((rows, channels), F32),
             pltpu.VMEM((modes * SEGS, channels), F32),
             pltpu.VMEM((modes, channels), F32),
             pltpu.VMEM((full, channels), BF16),
+            pltpu.VMEM((channels, out_weight.shape[1] // 2), BF16),
+            pltpu.VMEM((channels, out_weight.shape[1] // 2), BF16),
         ],
-        scratch_shapes=[pltpu.VMEM((HALO, full), BF16), held, held, pltpu.SemaphoreType.DMA],
+        scratch_shapes=[pltpu.VMEM((HALO, full), BF16), held, held, pltpu.SemaphoreType.DMA((3,))],
         compiler_params=pltpu.CompilerParams(vmem_limit_bytes=10 * MIB),
         name="front",
     )(
@@ -275,6 +295,7 @@
         halo_other,
         staged,
         pltpu.with_memory_space_constraint(weight, pltpu.HBM),
+        pltpu.with_memory_space_constraint(out_weight, pltpu.HBM),
         filt,
         rates,
     )
@@ -421,32 +442,25 @@
     )(*args)
 
 
-def product_kernel(where_ref, hidden_ref, w_ref, w_other_ref, part_ref, staged_ref, mine_ref, sems):
-    columns = part_ref.shape[1]
-    lanes = pl.ds(pl.multiple_of(lax.rem(where_ref[0], 2) * columns, columns), columns)
-    mine = pltpu.make_async_copy(w_ref.at[:, lanes], mine_ref, sems.at[0])
-    theirs = pltpu.make_async_copy(w_other_ref.at[:, lanes], staged_ref, sems.at[1])
-    mine.start()
-    theirs.start()
-    mine.wait()
-    part_ref[...] = jnp.dot(hidden_ref[...], mine_ref[...], preferred_element_type=F32)
-    theirs.wait()
-
-
-def product_call(where, hidden, weight, weight_other):
-    rows, channels = hidden.shape
-    columns = weight.shape[1] // 2
-    vmem = pl.BlockSpec(memory_space=pltpu.VMEM)
-    anywhere = pl.BlockSpec(memory_space=pl.ANY)
+def product_kernel(hidden_ref, w_ref, part_ref):
+    for tile in range(part_ref.shape[1] // WIDTH):
+        lanes = slice(tile * WIDTH, (tile + 1) * WIDTH)
+        part_ref[:, lanes] = jnp.dot(
+            hidden_ref[...], w_ref[:, lanes], preferred_element_type=F32
+        )
+
+
+def product_call(hidden, weight):
+    vmem = pl.BlockSpec(memory_space=pltpu.VMEM)
+    args = [pltpu.with_memory_space_constraint(x, pltpu.VMEM) for x in (hidden, weight)]
     return pl.pallas_call(
         product_kernel,
-        in_specs=[pl.BlockSpec(memory_space=pltpu.SMEM), vmem, anywhere, anywhere],
-        out_specs=[vmem] * 2,
-        out_shape=[pltpu.VMEM((rows, columns), F32), pltpu.VMEM((channels, columns), BF16)],
-        scratch_shapes=[pltpu.VMEM((channels, columns), BF16), pltpu.SemaphoreType.DMA((2,))],
-        compiler_params=pltpu.CompilerParams(vmem_limit_bytes=8 * MIB),
+        in_specs=[vmem] * 2,
+        out_specs=vmem,
+        out_shape=pltpu.VMEM((hidden.shape[0], weight.shape[1]), F32),
+        compiler_params=pltpu.CompilerParams(vmem_limit_bytes=4 * MIB),
         name="product",
-    )(where, hidden, weight, weight_other)
+    )(*args)
 
 
 def output_kernel(part_ref, other_ref, w_ref, out_ref, acc_ref, rows_ref, sems):
@@ -518,12 +532,10 @@
     lhs, staged, filt, rates, into_weights, total_weights = stage_call(
         where, tokens, swapped(tokens), weight, short_filter, rates
     )
-    halo_own, lhs, out_weight = lax.optimization_barrier((halo_own, lhs, out_weight))
+    halo_own, lhs = lax.optimization_barrier((halo_own, lhs))
     halo_other = swapped(halo_own)
-    lhs, halo_other, out_weight = lax.optimization_barrier((lhs, halo_other, out_weight))
-    out_weight_other = swapped(out_weight)
-    source, ends, total, query_weight = front_call(
-        where, lhs, halo_own, halo_other, staged, weight, filt, rates
+    source, ends, total, query_weight, mine, theirs = front_call(
+        where, lhs, halo_own, halo_other, staged, weight, out_weight, filt, rates
     )
     beside = [
         query_call(where, lhs, halo_own, halo_other, query_weight, filt),
@@ -541,8 +553,7 @@
             total = total + total_weights[RING * level + k + 1] * part
 
     hidden = hidden_call(into, beside[0], rates, beside[1:])
-    part, partner_weight = product_call(where, hidden, out_weight, out_weight_other)
-    return output_call(part, swapped(hidden), partner_weight)
+    return output_call(product_call(hidden, mine), swapped(hidden), swapped(theirs))
 
 
 def solution(mesh):

time: 52.6 us -> 54.5 us (1.036)
  Pallas kernels: 25.7 us -> 27.1 us
  waiting for transfers between devices: 1.68 us -> 2.37 us
    pallas_call x1, Pallas kernels: 6.92 us -> 9.09 us  [front_call(): pl.pallas_call(front_kernel, in_specs=[pl.BlockSpec(memory_space=pltpu.SM...]
    ppermute x4, waiting for transfers between devices: 1.25 us -> 1.95 us  [swapped(): return lax.ppermute(x, 'ch', [(0, 1), (1, 0)])]
    pallas_call x1, Pallas kernels: 1.95 us -> 1.26 us  [product_call(): pl.pallas_call(product_kernel, in_specs=[vmem] * 2, out_specs=vmem, out_s...]
  transfers between devices with their start and end apart: 14 -> 14, of which waited for: 3 -> 3; matrix products, arithmetic and copies ran while one was open for 2% -> 2% of each run, Pallas kernels for 44% -> 28%
where the time goes in v5:
time: 54.5 us; the launch traced here: 54.3 us
  Pallas kernels  27.1 us (50%)
  starting transfers between devices  23.5 us (43%)
  waiting for transfers between devices  2.37 us (4%)
  local copies, waits for them, and re-layouts  0.77 us (1%)
    ppermute x9, starting transfers between devices, round_the_ring(): lax.ppermute(sent, axis, [(i, (i + k) % RING) for i in range(RING)])  14.8 us
    pallas_call x1, Pallas kernels, front_call(): pl.pallas_call(front_kernel, in_specs=[pl.BlockSpec(memory_space=pltpu.SM...  9.09 us
    ppermute x4, starting transfers between devices, swapped(): return lax.ppermute(x, 'ch', [(0, 1), (1, 0)])  5.53 us
    pallas_call x2, Pallas kernels, local_call(): pl.pallas_call(functools.partial(local_kernel, part * wide), in_specs=[vm...  5.02 us
    pallas_call x1, Pallas kernels, stage_call(): pl.pallas_call(stage_kernel, in_specs=[pl.BlockSpec(memory_space=pltpu.SM...  3.85 us
    ppermute x1, starting transfers between devices, from_before(): return lax.ppermute(x, SEQ, [(i, i + 1) for i in range(count - 1)])  3.19 us
    pallas_call x1, Pallas kernels, query_call(): pl.pallas_call(query_kernel, in_specs=[pl.BlockSpec(memory_space=pltpu.SM...  2.89 us
    pallas_call x1, Pallas kernels, output_call(): pl.pallas_call(output_kernel, in_specs=[vmem] * 3, out_specs=pl.BlockSpec...  2.58 us
  transfers between devices with their start and end apart: 14, of which 3 were waited for; matrix products, arithmetic and copies ran while one was open for 2% of the time, Pallas kernels for 28%

profile of v5, /device:TPU:1, one launch (start us, length us, event | category | flops | bytes accessed | tf_op | source)
XLA Modules:
  0.0 54.3 jit_solution(17596719337170724918)
XLA Ops:
  0.0 1.4 %collective-permute-start = (bf16[512,1024]{1,0:T(8,128)(2,1)}, bf16[512,1024]{1,0:T(8,128)(2,1)S(1)}, u32[]{:S(2)}, u32[]{:S(2)}) collective-permute-start(bf16[512,1024]{1,0:T(8,128)(2,1)} %own_ref.1), channel_id=1, source_target_pairs={{0,1},{1,0},{2,3},{3,2},{4,5},{5,4},{6,7},{7,6},{8,9},{9,8},{10,11... | collective-permute-start | bytes 3145736 | tf_op jit(solution)/shard_map/ppermute | solution.py:508
  1.4 0.8 %slice.55 = bf16[16,1024]{1,0:T(8,128)(2,1)S(1)} slice(bf16[512,1024]{1,0:T(8,128)(2,1)} %own_ref.1), slice={[496:512], [0:1024]} | slice | bytes 65536 | tf_op jit(solution)/shard_map/slice | solution.py:531
  2.2 3.2 %collective-permute-start.1 = (bf16[16,1024]{1,0:T(8,128)(2,1)S(1)}, bf16[16,1024]{1,0:T(8,128)(2,1)S(1)}, u32[]{:S(2)}, u32[]{:S(2)}) collective-permute-start(bf16[16,1024]{1,0:T(8,128)(2,1)S(1)} %slice.55), channel_id=1, source_target_pairs={{0,2},{2,4},{4,6},{6,8},{8,10},{10,12},{12,14},{14,16},{16,18},{18... | collective-permute-start | bytes 98312 | tf_op jit(solution)/shard_map/ppermute | solution.py:513
  5.4 0.0 collective-permute-done.other_ref
  5.4 3.8 %stage.1 = (bf16[512,2048]{1,0:T(8,128)(2,1)S(1)}, bf16[2,2048,1024]{2,1,0:T(8,128)(2,1)S(1)}, f32[3,3,1024]{2,1,0:T(4,128)S(1)}, f32[16,1024]{1,0:T(8,128)S(1)}...) custom-call(s32[1]{0:T(128)} %bitcast.where_ref, bf16[512,1024]{1,0:T(8,128)(2,1)} %own_ref.1, ...), custom_call_target="tpu_custom_call" | custom-call | tf_op jit(solution)/shard_map/stage/pallas_call | solution.py:94
  9.3 0.0 collective-permute-done.1.halo_own_ref
  9.3 0.4 collective-permute-start.2
  9.6 0.9 %collective-permute-done.2.halo_other_ref = bf16[16,1024]{1,0:T(8,128)(2,1)S(1)} collective-permute-done((bf16[16,1024]{1,0:T(8,128)(2,1)S(1)}, bf16[16,1024]{1,0:T(8,128)(2,1)S(1)}, u32[]{:S(2)}, u32[]{:S(2)}) %collective-permute-start.2) | collective-permute-done | bytes 32800 | tf_op jit(solution)/shard_map/ppermute | solution.py:508
  10.6 9.1 %front.1 = (f32[512,1024]{1,0:T(8,128)S(1)}, f32[128,1024]{1,0:T(8,128)S(1)}, f32[16,1024]{1,0:T(8,128)S(1)}, bf16[2048,1024]{1,0:T(8,128)(2,1)S(1)}, bf16[1024,...) custom-call(s32[1]{0:T(128)} %bitcast.where_ref, bf16[512,2048]{1,0:T(8,128)(2,1)S(1)} %get-tuple-element.43.lhs_ref, ...), custom_call_target="tpu_custom_call" | custom-call | tf_op jit(solution)/shard_map/front/pallas_call | solution.py:273
  19.7 1.3 %collective-permute-start.3 = (bf16[16,1024]{1,0:T(8,128)(2,1)S(1)}, bf16[16,1024]{1,0:T(8,128)(2,1)S(1)}, u32[]{:S(2)}, u32[]{:S(2)}) collective-permute-start(bf16[16,1024]{1,0:T(8,128)(2,1)S(1)} %convert_element_type.36), channel_id=1, source_target_pairs={{0,2},{2,4},{4,6},{6,0},{1,3},{3,5},{5,7},{7,1},{8,10},{10,12},{12... | collective-permute-start | bytes 98312 | tf_op jit(solution)/shard_map/ppermute | solution.py:519
  20.9 2.5 %collective-permute-start.4 = (bf16[16,1024]{1,0:T(8,128)(2,1)S(1)}, bf16[16,1024]{1,0:T(8,128)(2,1)S(1)}, u32[]{:S(2)}, u32[]{:S(2)}) collective-permute-start(bf16[16,1024]{1,0:T(8,128)(2,1)S(1)} %convert_element_type.36), channel_id=1, source_target_pairs={{0,4},{2,6},{4,0},{6,2},{1,5},{3,7},{5,1},{7,3},{8,12},{10,14},{12... | collective-permute-start | bytes 98312 | tf_op jit(solution)/shard_map/ppermute | solution.py:519
  23.4 0.9 %collective-permute-start.5 = (bf16[16,1024]{1,0:T(8,128)(2,1)S(1)}, bf16[16,1024]{1,0:T(8,128)(2,1)S(1)}, u32[]{:S(2)}, u32[]{:S(2)}) collective-permute-start(bf16[16,1024]{1,0:T(8,128)(2,1)S(1)} %convert_element_type.36), channel_id=1, source_target_pairs={{0,6},{2,0},{4,2},{6,4},{1,7},{3,1},{5,3},{7,5},{8,14},{10,8},{12,... | collective-permute-start | bytes 98312 | tf_op jit(solution)/shard_map/ppermute | solution.py:519
  24.3 1.1 %collective-permute-start.13 = (bf16[1024,1024]{1,0:T(8,128)(2,1)S(1)}, bf16[1024,1024]{1,0:T(8,128)(2,1)S(1)}, u32[]{:S(2)}, u32[]{:S(2)}) collective-permute-start(bf16[1024,1024]{1,0:T(8,128)(2,1)S(1)} %get-tuple-element.76), channel_id=1, source_target_pairs={{0,1},{1,0},{2,3},{3,2},{4,5},{5,4},{6,7},{7,6},{8,9},{9,8},{10,11... | collective-permute-start | bytes 6291464 | tf_op jit(solution)/shard_map/ppermute | solution.py:508
  25.4 2.9 %query.1.query_ref = f32[512,1024]{1,0:T(8,128)S(1)} custom-call(s32[1]{0:T(128)} %bitcast.where_ref, bf16[512,2048]{1,0:T(8,128)(2,1)S(1)} %get-tuple-element.43.lhs_ref, bf16[16,1024]{1,0:T(8,128)(2,1)S(1)} %collective-permute-done.1.halo_own_ref, bf16[16,1024]{1,0:T(8,128)(2,1)S(1)} %collective-permute-done.2.halo_other_ref, ...), custom_call_target="tpu_custom_call" | custom-call | flops 2214592512 | tf_op jit(solution)/shard_map/query/pallas_call | solution.py:339
  28.3 0.0 collective-permute-done.5
  28.4 1.4 %collective-permute-start.6 = (bf16[16,1024]{1,0:T(8,128)(2,1)S(1)}, bf16[16,1024]{1,0:T(8,128)(2,1)S(1)}, u32[]{:S(2)}, u32[]{:S(2)}) collective-permute-start(bf16[16,1024]{1,0:T(8,128)(2,1)S(1)} %get-tuple-element.77), channel_id=1, source_target_pairs={{0,8},{8,16},{16,24},{24,0},{1,9},{9,17},{17,25},{25,1},{2,10},{10... | collective-permute-start | bytes 98312 | tf_op jit(solution)/shard_map/ppermute | solution.py:519
  29.7 2.6 %collective-permute-start.7 = (bf16[16,1024]{1,0:T(8,128)(2,1)S(1)}, bf16[16,1024]{1,0:T(8,128)(2,1)S(1)}, u32[]{:S(2)}, u32[]{:S(2)}) collective-permute-start(bf16[16,1024]{1,0:T(8,128)(2,1)S(1)} %get-tuple-element.77), channel_id=1, source_target_pairs={{0,16},{8,24},{16,0},{24,8},{1,17},{9,25},{17,1},{25,9},{2,18},{10... | collective-permute-start | bytes 98312 | tf_op jit(solution)/shard_map/ppermute | solution.py:519
  32.3 1.1 %collective-permute-start.8 = (bf16[16,1024]{1,0:T(8,128)(2,1)S(1)}, bf16[16,1024]{1,0:T(8,128)(2,1)S(1)}, u32[]{:S(2)}, u32[]{:S(2)}) collective-permute-start(bf16[16,1024]{1,0:T(8,128)(2,1)S(1)} %get-tuple-element.77), channel_id=1, source_target_pairs={{0,24},{8,0},{16,8},{24,16},{1,25},{9,1},{17,9},{25,17},{2,26},{10... | collective-permute-start | bytes 98312 | tf_op jit(solution)/shard_map/ppermute | solution.py:519
  33.5 2.5 %local.2 = (f32[512,512]{1,0:T(8,128)S(1)}, f32[128,512]{1,0:T(8,128)S(1)}, f32[128,512]{1,0:T(8,128)S(1)}) custom-call(f32[512,1024]{1,0:T(8,128)S(1)} %get-tuple-element.53.source_ref, f32[128,1024]{1,0:T(8,128)S(1)} %get-tuple-element.54.ends_ref, f32[16,1024]{1,0:T(8,128)S(1)} %get-tuple-element.47.rates_ref, f32[16,1024]{1,0:T(8,128)S(1)} %bitcast_multiply_fusion.5.gain_ref), custom_call_target="tpu_custom_call" | custom-call | flops 16777216 | tf_op jit(solution)/shard_map/local/pallas_call | solution.py:388
  36.0 0.0 collective-permute-done.8
  36.0 3.7 %collective-permute-start.10 = (bf16[16,1024]{1,0:T(8,128)(2,1)S(1)}, bf16[16,1024]{1,0:T(8,128)(2,1)S(1)}, u32[]{:S(2)}, u32[]{:S(2)}) collective-permute-start(bf16[16,1024]{1,0:T(8,128)(2,1)S(1)} %fusion.14), channel_id=1, source_target_pairs={{0,64},{32,96},{64,0},{96,32},{1,65},{33,97},{65,1},{97,33},{2,66}... | collective-permute-start | bytes 98312 | tf_op jit(solution)/shard_map/ppermute | solution.py:519
  39.7 0.4 collective-permute-start.11
  40.1 1.0 %collective-permute-start.9 = (bf16[16,1024]{1,0:T(8,128)(2,1)S(1)}, bf16[16,1024]{1,0:T(8,128)(2,1)S(1)}, u32[]{:S(2)}, u32[]{:S(2)}) collective-permute-start(bf16[16,1024]{1,0:T(8,128)(2,1)S(1)} %fusion.14), channel_id=1, source_target_pairs={{0,32},{32,64},{64,96},{96,0},{1,33},{33,65},{65,97},{97,1},{2,34}... | collective-permute-start | bytes 98312 | tf_op jit(solution)/shard_map/ppermute | solution.py:519
  41.2 2.5 %local.3 = (f32[512,512]{1,0:T(8,128)S(1)}, f32[128,512]{1,0:T(8,128)S(1)}, f32[128,512]{1,0:T(8,128)S(1)}) custom-call(f32[512,1024]{1,0:T(8,128)S(1)} %get-tuple-element.53.source_ref, f32[128,1024]{1,0:T(8,128)S(1)} %get-tuple-element.54.ends_ref, f32[16,1024]{1,0:T(8,128)S(1)} %get-tuple-element.47.rates_ref, f32[16,1024]{1,0:T(8,128)S(1)} %bitcast_multiply_fusion.5.gain_ref), custom_call_target="tpu_custom_call" | custom-call | flops 16777216 | tf_op jit(solution)/shard_map/local/pallas_call | solution.py:388
  43.7 0.0 collective-permute-done.11
  43.7 0.4 collective-permute-done.9
  44.1 0.1 fusion.7.into_ref
  44.2 2.4 %hidden.1.hidden_ref = bf16[512,1024]{1,0:T(8,128)(2,1)S(1)} custom-call(f32[16,1024]{1,0:T(8,128)S(1)} %fusion.7.into_ref, f32[512,1024]{1,0:T(8,128)S(1)} %query.1.query_ref, f32[16,1024]{1,0:T(8,128)S(1)} %get-tuple-element.47.rates_ref, f32[512,512]{1,0:T(8,128)S(1)} %get-tuple-element.69.refs_0_, f32[128,512]{1,0:T(8,128)S(1)} %get-tuple-element.70.refs_1_, ...), custom_call_target="tpu_custom_call" | custom-call | tf_op jit(solution)/shard_map/hidden/pallas_call | solution.py:435
  46.6 2.6 %collective-permute-start.12 = (bf16[512,1024]{1,0:T(8,128)(2,1)S(1)}, bf16[512,1024]{1,0:T(8,128)(2,1)S(1)}, u32[]{:S(2)}, u32[]{:S(2)}) collective-permute-start(bf16[512,1024]{1,0:T(8,128)(2,1)S(1)} %hidden.1.hidden_ref), channel_id=1, source_target_pairs={{0,1},{1,0},{2,3},{3,2},{4,5},{5,4},{6,7},{7,6},{8,9},{9,8},{10,11... | collective-permute-start | bytes 3145736 | tf_op jit(solution)/shard_map/ppermute | solution.py:508
  49.2 1.3 %product.1.part_ref = f32[512,1024]{1,0:T(8,128)S(1)} custom-call(bf16[512,1024]{1,0:T(8,128)(2,1)S(1)} %hidden.1.hidden_ref, bf16[1024,1024]{1,0:T(8,128)(2,1)S(1)} %get-tuple-element.75.w_ref), custom_call_target="tpu_custom_call" | custom-call | tf_op jit(solution)/shard_map/product/pallas_call | solution.py:456
  50.5 1.0 %collective-permute-done.12.other_ref = bf16[512,1024]{1,0:T(8,128)(2,1)S(1)} collective-permute-done((bf16[512,1024]{1,0:T(8,128)(2,1)S(1)}, bf16[512,1024]{1,0:T(8,128)(2,1)S(1)}, u32[]{:S(2)}, u32[]{:S(2)}) %collective-permute-start.12) | collective-permute-done | bytes 1048608 | tf_op jit(solution)/shard_map/ppermute | solution.py:508
  51.5 2.6 %output.1 = f32[512,1024]{1,0:T(8,128)} custom-call(f32[512,1024]{1,0:T(8,128)S(1)} %product.1.part_ref, bf16[512,1024]{1,0:T(8,128)(2,1)S(1)} %collective-permute-done.12.other_ref, bf16[1024,1024]{1,0:T(8,128)(2,1)S(1)} %collective-permute-done.13.w_ref), custom_call_target="tpu_custom_call" | custom-call | tf_op jit(solution)/shard_map/output/pallas_call | solution.py:492
  (14 shorter events, 0.1 us)
Async XLA Ops:
  0.0 5.4 %collective-permute-start = (bf16[512,1024]{1,0:T(8,128)(2,1)}, bf16[512,1024]{1,0:T(8,128)(2,1)S(1)}, u32[]{:S(2)}, u32[]{:S(2)}) collective-permute-start(bf16[512,1024]{1,0:T(8,128)(2,1)} %own_ref.1), channel_id=1, source_target_pairs={{0,1},{1,0},{2,3},{3,2},{4,5},{5,4},{6,7},{7,6},{8,9},{9,8},{10,11... | collective-permute-start | bytes 3145736 | tf_op jit(solution)/shard_map/ppermute | solution.py:508
  2.2 7.1 %collective-permute-start.1 = (bf16[16,1024]{1,0:T(8,128)(2,1)S(1)}, bf16[16,1024]{1,0:T(8,128)(2,1)S(1)}, u32[]{:S(2)}, u32[]{:S(2)}) collective-permute-start(bf16[16,1024]{1,0:T(8,128)(2,1)S(1)} %slice.55), channel_id=1, source_target_pairs={{0,2},{2,4},{4,6},{6,8},{8,10},{10,12},{12,14},{14,16},{16,18},{18... | collective-permute-start | bytes 98312 | tf_op jit(solution)/shard_map/ppermute | solution.py:513
  9.3 1.3 %collective-permute-start.2 = (bf16[16,1024]{1,0:T(8,128)(2,1)S(1)}, bf16[16,1024]{1,0:T(8,128)(2,1)S(1)}, u32[]{:S(2)}, u32[]{:S(2)}) collective-permute-start(bf16[16,1024]{1,0:T(8,128)(2,1)S(1)} %collective-permute-done.1.halo_own_ref), channel_id=1, source_target_pairs={{0,1},{1,0},{2,3},{3,2},{4,5},{5,4},{6,7},{7,6},{8,9},{9,8},{10,11... | collective-permute-start | bytes 98312 | tf_op jit(solution)/shard_map/ppermute | solution.py:508
  19.7 8.6 %collective-permute-start.3 = (bf16[16,1024]{1,0:T(8,128)(2,1)S(1)}, bf16[16,1024]{1,0:T(8,128)(2,1)S(1)}, u32[]{:S(2)}, u32[]{:S(2)}) collective-permute-start(bf16[16,1024]{1,0:T(8,128)(2,1)S(1)} %convert_element_type.36), channel_id=1, source_target_pairs={{0,2},{2,4},{4,6},{6,0},{1,3},{3,5},{5,7},{7,1},{8,10},{10,12},{12... | collective-permute-start | bytes 98312 | tf_op jit(solution)/shard_map/ppermute | solution.py:519
  20.9 7.4 %collective-permute-start.4 = (bf16[16,1024]{1,0:T(8,128)(2,1)S(1)}, bf16[16,1024]{1,0:T(8,128)(2,1)S(1)}, u32[]{:S(2)}, u32[]{:S(2)}) collective-permute-start(bf16[16,1024]{1,0:T(8,128)(2,1)S(1)} %convert_element_type.36), channel_id=1, source_target_pairs={{0,4},{2,6},{4,0},{6,2},{1,5},{3,7},{5,1},{7,3},{8,12},{10,14},{12... | collective-permute-start | bytes 98312 | tf_op jit(solution)/shard_map/ppermute | solution.py:519
  23.4 4.9 %collective-permute-start.5 = (bf16[16,1024]{1,0:T(8,128)(2,1)S(1)}, bf16[16,1024]{1,0:T(8,128)(2,1)S(1)}, u32[]{:S(2)}, u32[]{:S(2)}) collective-permute-start(bf16[16,1024]{1,0:T(8,128)(2,1)S(1)} %convert_element_type.36), channel_id=1, source_target_pairs={{0,6},{2,0},{4,2},{6,4},{1,7},{3,1},{5,3},{7,5},{8,14},{10,8},{12,... | collective-permute-start | bytes 98312 | tf_op jit(solution)/shard_map/ppermute | solution.py:519
  24.3 27.3 %collective-permute-start.13 = (bf16[1024,1024]{1,0:T(8,128)(2,1)S(1)}, bf16[1024,1024]{1,0:T(8,128)(2,1)S(1)}, u32[]{:S(2)}, u32[]{:S(2)}) collective-permute-start(bf16[1024,1024]{1,0:T(8,128)(2,1)S(1)} %get-tuple-element.76), channel_id=1, source_target_pairs={{0,1},{1,0},{2,3},{3,2},{4,5},{5,4},{6,7},{7,6},{8,9},{9,8},{10,11... | collective-permute-start | bytes 6291464 | tf_op jit(solution)/shard_map/ppermute | solution.py:508
  25.4 8.0 %copy-start = (f32[1024,16]{0,1:T(8,128)S(1)}, f32[1024,16]{0,1:T(8,128)}, u32[]{:S(2)}) copy-start(f32[1024,16]{0,1:T(8,128)} %param.10) | copy-start | bytes 196612
  25.4 8.0 %copy-start.1 = (f32[1024,16]{0,1:T(8,128)S(1)}, f32[1024,16]{0,1:T(8,128)}, u32[]{:S(2)}) copy-start(f32[1024,16]{0,1:T(8,128)} %param.9) | copy-start | bytes 196612
  28.4 7.6 %collective-permute-start.6 = (bf16[16,1024]{1,0:T(8,128)(2,1)S(1)}, bf16[16,1024]{1,0:T(8,128)(2,1)S(1)}, u32[]{:S(2)}, u32[]{:S(2)}) collective-permute-start(bf16[16,1024]{1,0:T(8,128)(2,1)S(1)} %get-tuple-element.77), channel_id=1, source_target_pairs={{0,8},{8,16},{16,24},{24,0},{1,9},{9,17},{17,25},{25,1},{2,10},{10... | collective-permute-start | bytes 98312 | tf_op jit(solution)/shard_map/ppermute | solution.py:519
  29.7 6.3 %collective-permute-start.7 = (bf16[16,1024]{1,0:T(8,128)(2,1)S(1)}, bf16[16,1024]{1,0:T(8,128)(2,1)S(1)}, u32[]{:S(2)}, u32[]{:S(2)}) collective-permute-start(bf16[16,1024]{1,0:T(8,128)(2,1)S(1)} %get-tuple-element.77), channel_id=1, source_target_pairs={{0,16},{8,24},{16,0},{24,8},{1,17},{9,25},{17,1},{25,9},{2,18},{10... | collective-permute-start | bytes 98312 | tf_op jit(solution)/shard_map/ppermute | solution.py:519
  32.3 3.7 %collective-permute-start.8 = (bf16[16,1024]{1,0:T(8,128)(2,1)S(1)}, bf16[16,1024]{1,0:T(8,128)(2,1)S(1)}, u32[]{:S(2)}, u32[]{:S(2)}) collective-permute-start(bf16[16,1024]{1,0:T(8,128)(2,1)S(1)} %get-tuple-element.77), channel_id=1, source_target_pairs={{0,24},{8,0},{16,8},{24,16},{1,25},{9,1},{17,9},{25,17},{2,26},{10... | collective-permute-start | bytes 98312 | tf_op jit(solution)/shard_map/ppermute | solution.py:519
  36.0 7.7 %collective-permute-start.10 = (bf16[16,1024]{1,0:T(8,128)(2,1)S(1)}, bf16[16,1024]{1,0:T(8,128)(2,1)S(1)}, u32[]{:S(2)}, u32[]{:S(2)}) collective-permute-start(bf16[16,1024]{1,0:T(8,128)(2,1)S(1)} %fusion.14), channel_id=1, source_target_pairs={{0,64},{32,96},{64,0},{96,32},{1,65},{33,97},{65,1},{97,33},{2,66}... | collective-permute-start | bytes 98312 | tf_op jit(solution)/shard_map/ppermute | solution.py:519
  39.7 4.0 %collective-permute-start.11 = (bf16[16,1024]{1,0:T(8,128)(2,1)S(1)}, bf16[16,1024]{1,0:T(8,128)(2,1)S(1)}, u32[]{:S(2)}, u32[]{:S(2)}) collective-permute-start(bf16[16,1024]{1,0:T(8,128)(2,1)S(1)} %fusion.14), channel_id=1, source_target_pairs={{0,96},{32,0},{64,32},{96,64},{1,97},{33,1},{65,33},{97,65},{2,98}... | collective-permute-start | bytes 98312 | tf_op jit(solution)/shard_map/ppermute | solution.py:519
  40.1 4.0 %collective-permute-start.9 = (bf16[16,1024]{1,0:T(8,128)(2,1)S(1)}, bf16[16,1024]{1,0:T(8,128)(2,1)S(1)}, u32[]{:S(2)}, u32[]{:S(2)}) collective-permute-start(bf16[16,1024]{1,0:T(8,128)(2,1)S(1)} %fusion.14), channel_id=1, source_target_pairs={{0,32},{32,64},{64,96},{96,0},{1,33},{33,65},{65,97},{97,1},{2,34}... | collective-permute-start | bytes 98312 | tf_op jit(solution)/shard_map/ppermute | solution.py:519
  46.6 4.9 %collective-permute-start.12 = (bf16[512,1024]{1,0:T(8,128)(2,1)S(1)}, bf16[512,1024]{1,0:T(8,128)(2,1)S(1)}, u32[]{:S(2)}, u32[]{:S(2)}) collective-permute-start(bf16[512,1024]{1,0:T(8,128)(2,1)S(1)} %hidden.1.hidden_ref), channel_id=1, source_target_pairs={{0,1},{1,0},{2,3},{3,2},{4,5},{5,4},{6,7},{7,6},{8,9},{9,8},{10,11... | collective-permute-start | bytes 3145736 | tf_op jit(solution)/shard_map/ppermute | solution.py:508

commit v6 on v4

--- a/solution.py
+++ b/solution.py
@@ -144,17 +144,14 @@
     halo_own_ref,
     halo_other_ref,
     w_ref,
-    wq_ref,
     filt_ref,
     rates_ref,
     source_ref,
     ends_ref,
     total_ref,
-    staged_ref,
     halo_ref,
     proj_a,
     proj_b,
-    sem,
 ):
     rows = lhs_ref.shape[0]
     steps = rows // SEGS
@@ -165,8 +162,6 @@
     per = SEGS // 2
     proj = (proj_a, proj_b)
 
-    stage = pltpu.make_async_copy(wq_ref.at[0], staged_ref, sem)
-    stage.start()
     join_halo(where_ref, halo_ref, halo_own_ref, halo_other_ref)
 
     def projection(tile):
@@ -243,10 +238,9 @@
             for step in fast[done:upto]:
                 step()
             done = upto
-    stage.wait()
-
-
-def front_call(where, lhs, halo_own, halo_other, staged, weight, filt, rates):
+
+
+def front_call(where, lhs, halo_own, halo_other, staged, filt, rates):
     rows, full = lhs.shape
     streams, _, channels = staged.shape
     modes = rates.shape[0]
@@ -255,17 +249,14 @@
     return pl.pallas_call(
         front_kernel,
         in_specs=[pl.BlockSpec(memory_space=pltpu.SMEM)]
-        + [vmem] * 4
-        + [pl.BlockSpec(memory_space=pl.ANY)]
-        + [vmem] * 2,
-        out_specs=[vmem] * 4,
+        + [vmem] * 6,
+        out_specs=[vmem] * 3,
         out_shape=[
             pltpu.VMEM((rows, channels), F32),
             pltpu.VMEM((modes * SEGS, channels), F32),
             pltpu.VMEM((modes, channels), F32),
-            pltpu.VMEM((full, channels), BF16),
         ],
-        scratch_shapes=[pltpu.VMEM((HALO, full), BF16), held, held, pltpu.SemaphoreType.DMA],
+        scratch_shapes=[pltpu.VMEM((HALO, full), BF16), held, held],
         compiler_params=pltpu.CompilerParams(vmem_limit_bytes=10 * MIB),
         name="front",
     )(
@@ -274,7 +265,6 @@
         halo_own,
         halo_other,
         staged,
-        pltpu.with_memory_space_constraint(weight, pltpu.HBM),
         filt,
         rates,
     )
@@ -332,7 +322,22 @@
     )(where, *args)
 
 
-def local_kernel(first, source_ref, ends_ref, rates_ref, gain_ref, local_ref, base_ref, factor_ref):
+def local_kernel(
+    first,
+    carried,
+    source_ref,
+    ends_ref,
+    rates_ref,
+    gain_ref,
+    *refs,
+):
+    copies = []
+    if carried:
+        refs, (w_ref, staged_ref, sem) = refs[1:4], (refs[0], *refs[4:])
+        copies.append(pltpu.make_async_copy(w_ref.at[0], staged_ref, sem))
+    for copy in copies:
+        copy.start()
+    local_ref, base_ref, factor_ref = refs
     rows, channels = local_ref.shape
     steps = rows // SEGS
     modes = rates_ref.shape[0]
@@ -357,28 +362,34 @@
             source = source_ref[row, lanes]
             states = [d * s + source for d, s in zip(decays, states)]
             local_ref[row, here] = tree_sum([g * s for g, s in zip(gains, states)])
-
-
-def local_call(source, ends, rates, gain, part):
+    for copy in copies:
+        copy.wait()
+
+
+def local_call(source, ends, rates, gain, part, weight=None):
     rows, channels = source.shape
     wide = channels // PARTS
     vmem = pl.BlockSpec(memory_space=pltpu.VMEM)
     args = [pltpu.with_memory_space_constraint(x, pltpu.VMEM) for x in (source, ends, rates, gain)]
-    return pl.pallas_call(
-        functools.partial(local_kernel, part * wide),
-        in_specs=[vmem] * 4,
-        out_specs=[vmem] * 3,
+    carried = weight is not None
+    extra = [pltpu.with_memory_space_constraint(weight, pltpu.HBM)] if carried else []
+    return pl.pallas_call(
+        functools.partial(local_kernel, part * wide, carried),
+        in_specs=[vmem] * 4 + [pl.BlockSpec(memory_space=pl.ANY)] * len(extra),
+        out_specs=[vmem] * (3 + len(extra)),
         out_shape=[
             pltpu.VMEM((rows, wide), F32),
             pltpu.VMEM((ends.shape[0], wide), F32),
             pltpu.VMEM((ends.shape[0], wide), F32),
+            *[pltpu.VMEM(x.shape[1:], BF16) for x in extra],
         ],
+        scratch_shapes=[pltpu.SemaphoreType.DMA] * len(extra),
         compiler_params=pltpu.CompilerParams(vmem_limit_bytes=4 * MIB),
         cost_estimate=pl.CostEstimate(
             flops=4 * rates.shape[0] * rows * wide, transcendentals=0, bytes_accessed=0
         ),
         name="local",
-    )(*args)
+    )(*args, *extra)
 
 
 def hidden_kernel(into_ref, query_ref, rates_ref, *refs):
@@ -522,13 +533,11 @@
     halo_other = swapped(halo_own)
     lhs, halo_other, out_weight = lax.optimization_barrier((lhs, halo_other, out_weight))
     out_weight_other = swapped(out_weight)
-    source, ends, total, query_weight = front_call(
-        where, lhs, halo_own, halo_other, staged, weight, filt, rates
-    )
-    beside = [
-        query_call(where, lhs, halo_own, halo_other, query_weight, filt),
-        *[local_call(source, ends, rates, gain, part) for part in range(PARTS)],
-    ]
+    source, ends, total = front_call(where, lhs, halo_own, halo_other, staged, filt, rates)
+    *first, query_weight = local_call(source, ends, rates, gain, 0, weight)
+    query = query_call(where, lhs, halo_own, halo_other, query_weight, filt)
+    second = local_call(source, ends, rates, gain, 1)
+    beside = [tuple(first), query, tuple(second)]
 
     into = 0.0
     for level, axis in enumerate(reversed(SEQ)):
@@ -540,7 +549,7 @@
             into = into + into_weights[(RING - 1) * level + k] * part
             total = total + total_weights[RING * level + k + 1] * part
 
-    hidden = hidden_call(into, beside[0], rates, beside[1:])
+    hidden = hidden_call(into, beside[1], rates, (beside[0], beside[2]))
     part, partner_weight = product_call(where, hidden, out_weight, out_weight_other)
     return output_call(part, swapped(hidden), partner_weight)
 

time: 52.6 us -> 52.6 us (level)
  no operation moved by 1% of the time
where the time goes in v6:
time: 52.6 us; the launch traced here: 52.4 us
  Pallas kernels  25.7 us (49%)
  starting transfers between devices  23.7 us (45%)
  waiting for transfers between devices  1.68 us (3%)
  local copies, waits for them, and re-layouts  0.77 us (1%)
    ppermute x9, starting transfers between devices, round_the_ring(): lax.ppermute(sent, axis, [(i, (i + k) % RING) for i in range(RING)])  14.8 us
    pallas_call x1, Pallas kernels, front_call(): pl.pallas_call(front_kernel, in_specs=[pl.BlockSpec(memory_space=pltpu.SM...  6.9 us
    ppermute x4, starting transfers between devices, swapped(): return lax.ppermute(x, 'ch', [(0, 1), (1, 0)])  5.76 us
    pallas_call x2, Pallas kernels, local_call(): pl.pallas_call(functools.partial(local_kernel, part * wide, carried), in_...  5.03 us
    pallas_call x1, Pallas kernels, stage_call(): pl.pallas_call(stage_kernel, in_specs=[pl.BlockSpec(memory_space=pltpu.SM...  3.96 us
    ppermute x1, starting transfers between devices, from_before(): return lax.ppermute(x, SEQ, [(i, i + 1) for i in range(count - 1)])  3.19 us
    pallas_call x1, Pallas kernels, query_call(): pl.pallas_call(query_kernel, in_specs=[pl.BlockSpec(memory_space=pltpu.SM...  2.89 us
    pallas_call x1, Pallas kernels, output_call(): pl.pallas_call(output_kernel, in_specs=[vmem] * 3, out_specs=pl.BlockSpec...  2.57 us
  transfers between devices with their start and end apart: 14, of which 3 were waited for; matrix products, arithmetic and copies ran while one was open for 2% of the time, Pallas kernels for 44%

profile of v6, /device:TPU:1, one launch (start us, length us, event | category | flops | bytes accessed | tf_op | source)
XLA Modules:
  0.0 52.4 jit_solution(12706802836658302222)
XLA Ops:
  0.0 1.4 %collective-permute-start = (bf16[512,1024]{1,0:T(8,128)(2,1)}, bf16[512,1024]{1,0:T(8,128)(2,1)S(1)}, u32[]{:S(2)}, u32[]{:S(2)}) collective-permute-start(bf16[512,1024]{1,0:T(8,128)(2,1)} %own_ref.1), channel_id=1, source_target_pairs={{0,1},{1,0},{2,3},{3,2},{4,5},{5,4},{6,7},{7,6},{8,9},{9,8},{10,11... | collective-permute-start | bytes 3145736 | tf_op jit(solution)/shard_map/ppermute | solution.py:505
  1.4 0.8 %slice.55 = bf16[16,1024]{1,0:T(8,128)(2,1)S(1)} slice(bf16[512,1024]{1,0:T(8,128)(2,1)} %own_ref.1), slice={[496:512], [0:1024]} | slice | bytes 65536 | tf_op jit(solution)/shard_map/slice | solution.py:528
  2.2 3.2 %collective-permute-start.1 = (bf16[16,1024]{1,0:T(8,128)(2,1)S(1)}, bf16[16,1024]{1,0:T(8,128)(2,1)S(1)}, u32[]{:S(2)}, u32[]{:S(2)}) collective-permute-start(bf16[16,1024]{1,0:T(8,128)(2,1)S(1)} %slice.55), channel_id=1, source_target_pairs={{0,2},{2,4},{4,6},{6,8},{8,10},{10,12},{12,14},{14,16},{16,18},{18... | collective-permute-start | bytes 98312 | tf_op jit(solution)/shard_map/ppermute | solution.py:510
  5.4 0.0 collective-permute-done.other_ref
  5.4 0.0 copy-start
  5.4 4.0 %stage.1 = (bf16[512,2048]{1,0:T(8,128)(2,1)S(1)}, bf16[2,2048,1024]{2,1,0:T(8,128)(2,1)S(1)}, f32[3,3,1024]{2,1,0:T(4,128)S(1)}, f32[16,1024]{1,0:T(8,128)S(1)}...) custom-call(s32[1]{0:T(128)} %bitcast.where_ref, bf16[512,1024]{1,0:T(8,128)(2,1)} %own_ref.1, ...), custom_call_target="tpu_custom_call" | custom-call | tf_op jit(solution)/shard_map/stage/pallas_call | solution.py:94
  9.4 0.0 collective-permute-done.1.halo_own_ref
  9.4 0.4 collective-permute-start.2
  9.8 0.9 %collective-permute-done.2.halo_other_ref = bf16[16,1024]{1,0:T(8,128)(2,1)S(1)} collective-permute-done((bf16[16,1024]{1,0:T(8,128)(2,1)S(1)}, bf16[16,1024]{1,0:T(8,128)(2,1)S(1)}, u32[]{:S(2)}, u32[]{:S(2)}) %collective-permute-start.2) | collective-permute-done | bytes 32800 | tf_op jit(solution)/shard_map/ppermute | solution.py:505
  10.7 0.3 collective-permute-start.12
  11.0 6.9 %front.1 = (f32[512,1024]{1,0:T(8,128)S(1)}, f32[128,1024]{1,0:T(8,128)S(1)}, f32[16,1024]{1,0:T(8,128)S(1)}) custom-call(s32[1]{0:T(128)} %bitcast.where_ref, bf16[512,2048]{1,0:T(8,128)(2,1)S(1)} %get-tuple-element.50.lhs_ref, bf16[16,1024]{1,0:T(8,128)(2,1)S(1)} %collective-permute-done.1.halo_own_ref, ...), custom_call_target="tpu_custom_call" | custom-call | tf_op jit(solution)/shard_map/front/pallas_call | solution.py:249
  17.9 1.3 %collective-permute-start.3 = (bf16[16,1024]{1,0:T(8,128)(2,1)S(1)}, bf16[16,1024]{1,0:T(8,128)(2,1)S(1)}, u32[]{:S(2)}, u32[]{:S(2)}) collective-permute-start(bf16[16,1024]{1,0:T(8,128)(2,1)S(1)} %convert_element_type.36), channel_id=1, source_target_pairs={{0,2},{2,4},{4,6},{6,0},{1,3},{3,5},{5,7},{7,1},{8,10},{10,12},{12... | collective-permute-start | bytes 98312 | tf_op jit(solution)/shard_map/ppermute | solution.py:516
  19.2 2.5 %collective-permute-start.4 = (bf16[16,1024]{1,0:T(8,128)(2,1)S(1)}, bf16[16,1024]{1,0:T(8,128)(2,1)S(1)}, u32[]{:S(2)}, u32[]{:S(2)}) collective-permute-start(bf16[16,1024]{1,0:T(8,128)(2,1)S(1)} %convert_element_type.36), channel_id=1, source_target_pairs={{0,4},{2,6},{4,0},{6,2},{1,5},{3,7},{5,1},{7,3},{8,12},{10,14},{12... | collective-permute-start | bytes 98312 | tf_op jit(solution)/shard_map/ppermute | solution.py:516
  21.6 0.9 %collective-permute-start.5 = (bf16[16,1024]{1,0:T(8,128)(2,1)S(1)}, bf16[16,1024]{1,0:T(8,128)(2,1)S(1)}, u32[]{:S(2)}, u32[]{:S(2)}) collective-permute-start(bf16[16,1024]{1,0:T(8,128)(2,1)S(1)} %convert_element_type.36), channel_id=1, source_target_pairs={{0,6},{2,0},{4,2},{6,4},{1,7},{3,1},{5,3},{7,5},{8,14},{10,8},{12,... | collective-permute-start | bytes 98312 | tf_op jit(solution)/shard_map/ppermute | solution.py:516
  22.5 2.5 %local.2 = (f32[512,512]{1,0:T(8,128)S(1)}, f32[128,512]{1,0:T(8,128)S(1)}, f32[128,512]{1,0:T(8,128)S(1)}, bf16[2048,1024]{1,0:T(8,128)(2,1)S(1)}) custom-call(f32[512,1024]{1,0:T(8,128)S(1)} %get-tuple-element.55.source_ref, f32[128,1024]{1,0:T(8,128)S(1)} %get-tuple-element.56.ends_ref, f32[16,1024]{1,0:T(8,128)S(1)} %get-tuple-element.54.rates_ref, ...), custom_call_target="tpu_custom_call" | custom-call | flops 16777216 | tf_op jit(solution)/shard_map/local/pallas_call | solution.py:376
  25.1 0.0 collective-permute-done.3
  25.1 0.0 collective-permute-done.5
  25.1 1.4 %collective-permute-start.6 = (bf16[16,1024]{1,0:T(8,128)(2,1)S(1)}, bf16[16,1024]{1,0:T(8,128)(2,1)S(1)}, u32[]{:S(2)}, u32[]{:S(2)}) collective-permute-start(bf16[16,1024]{1,0:T(8,128)(2,1)S(1)} %get-tuple-element.85), channel_id=1, source_target_pairs={{0,8},{8,16},{16,24},{24,0},{1,9},{9,17},{17,25},{25,1},{2,10},{10... | collective-permute-start | bytes 98312 | tf_op jit(solution)/shard_map/ppermute | solution.py:516
  26.5 2.6 %collective-permute-start.7 = (bf16[16,1024]{1,0:T(8,128)(2,1)S(1)}, bf16[16,1024]{1,0:T(8,128)(2,1)S(1)}, u32[]{:S(2)}, u32[]{:S(2)}) collective-permute-start(bf16[16,1024]{1,0:T(8,128)(2,1)S(1)} %get-tuple-element.85), channel_id=1, source_target_pairs={{0,16},{8,24},{16,0},{24,8},{1,17},{9,25},{17,1},{25,9},{2,18},{10... | collective-permute-start | bytes 98312 | tf_op jit(solution)/shard_map/ppermute | solution.py:516
  29.1 1.1 %collective-permute-start.8 = (bf16[16,1024]{1,0:T(8,128)(2,1)S(1)}, bf16[16,1024]{1,0:T(8,128)(2,1)S(1)}, u32[]{:S(2)}, u32[]{:S(2)}) collective-permute-start(bf16[16,1024]{1,0:T(8,128)(2,1)S(1)} %get-tuple-element.85), channel_id=1, source_target_pairs={{0,24},{8,0},{16,8},{24,16},{1,25},{9,1},{17,9},{25,17},{2,26},{10... | collective-permute-start | bytes 98312 | tf_op jit(solution)/shard_map/ppermute | solution.py:516
  30.2 2.9 %query.1.query_ref = f32[512,1024]{1,0:T(8,128)S(1)} custom-call(s32[1]{0:T(128)} %bitcast.where_ref, bf16[512,2048]{1,0:T(8,128)(2,1)S(1)} %get-tuple-element.50.lhs_ref, bf16[16,1024]{1,0:T(8,128)(2,1)S(1)} %collective-permute-done.1.halo_own_ref, bf16[16,1024]{1,0:T(8,128)(2,1)S(1)} %collective-permute-done.2.halo_other_ref, ...), custom_call_target="tpu_custom_call" | custom-call | flops 2214592512 | tf_op jit(solution)/shard_map/query/pallas_call | solution.py:308
  33.2 3.7 %collective-permute-start.10 = (bf16[16,1024]{1,0:T(8,128)(2,1)S(1)}, bf16[16,1024]{1,0:T(8,128)(2,1)S(1)}, u32[]{:S(2)}, u32[]{:S(2)}) collective-permute-start(bf16[16,1024]{1,0:T(8,128)(2,1)S(1)} %fusion.14), channel_id=1, source_target_pairs={{0,64},{32,96},{64,0},{96,32},{1,65},{33,97},{65,1},{97,33},{2,66}... | collective-permute-start | bytes 98312 | tf_op jit(solution)/shard_map/ppermute | solution.py:516
  36.8 0.4 collective-permute-start.11
  37.3 1.0 %collective-permute-start.9 = (bf16[16,1024]{1,0:T(8,128)(2,1)S(1)}, bf16[16,1024]{1,0:T(8,128)(2,1)S(1)}, u32[]{:S(2)}, u32[]{:S(2)}) collective-permute-start(bf16[16,1024]{1,0:T(8,128)(2,1)S(1)} %fusion.14), channel_id=1, source_target_pairs={{0,32},{32,64},{64,96},{96,0},{1,33},{33,65},{65,97},{97,1},{2,34}... | collective-permute-start | bytes 98312 | tf_op jit(solution)/shard_map/ppermute | solution.py:516
  38.3 2.5 %local.3 = (f32[512,512]{1,0:T(8,128)S(1)}, f32[128,512]{1,0:T(8,128)S(1)}, f32[128,512]{1,0:T(8,128)S(1)}) custom-call(f32[512,1024]{1,0:T(8,128)S(1)} %get-tuple-element.55.source_ref, f32[128,1024]{1,0:T(8,128)S(1)} %get-tuple-element.56.ends_ref, f32[16,1024]{1,0:T(8,128)S(1)} %get-tuple-element.54.rates_ref, f32[16,1024]{1,0:T(8,128)S(1)} %bitcast_multiply_fusion.5.gain_ref), custom_call_target="tpu_custom_call" | custom-call | flops 16777216 | tf_op jit(solution)/shard_map/local/pallas_call | solution.py:376
  40.8 0.4 collective-permute-done.9
  41.2 0.1 fusion.7.into_ref
  41.3 2.4 %hidden.1.hidden_ref = bf16[512,1024]{1,0:T(8,128)(2,1)S(1)} custom-call(f32[16,1024]{1,0:T(8,128)S(1)} %fusion.7.into_ref, f32[512,1024]{1,0:T(8,128)S(1)} %query.1.query_ref, f32[16,1024]{1,0:T(8,128)S(1)} %get-tuple-element.54.rates_ref, f32[512,512]{1,0:T(8,128)S(1)} %get-tuple-element.76.refs_0_, f32[128,512]{1,0:T(8,128)S(1)} %get-tuple-element.77.refs_1_, ...), custom_call_target="tpu_custom_call" | custom-call | tf_op jit(solution)/shard_map/hidden/pallas_call | solution.py:425
  43.7 3.7 %collective-permute-start.13 = (bf16[512,1024]{1,0:T(8,128)(2,1)S(1)}, bf16[512,1024]{1,0:T(8,128)(2,1)S(1)}, u32[]{:S(2)}, u32[]{:S(2)}) collective-permute-start(bf16[512,1024]{1,0:T(8,128)(2,1)S(1)} %hidden.1.hidden_ref), channel_id=1, source_target_pairs={{0,1},{1,0},{2,3},{3,2},{4,5},{5,4},{6,7},{7,6},{8,9},{9,8},{10,11... | collective-permute-start | bytes 3145736 | tf_op jit(solution)/shard_map/ppermute | solution.py:505
  47.4 2.0 %product.1 = (f32[512,1024]{1,0:T(8,128)S(1)}, bf16[1024,1024]{1,0:T(8,128)(2,1)S(1)}) custom-call(s32[1]{0:T(128)} %bitcast.where_ref, bf16[512,1024]{1,0:T(8,128)(2,1)S(1)} %hidden.1.hidden_ref, bf16[1024,2048]{1,0:T(8,128)(2,1)S(1)} %copy-done, bf16[1024,2048]{1,0:T(8,128)(2,1)S(1)} %collective-permute-done.12.w_other_ref), custom_call_target="tpu_custom_call" | custom-call | tf_op jit(solution)/shard_map/product/pallas_call | solution.py:452
  49.4 0.3 collective-permute-done.13.other_ref
  49.7 2.6 %output.1 = f32[512,1024]{1,0:T(8,128)} custom-call(f32[512,1024]{1,0:T(8,128)S(1)} %get-tuple-element.83.part_ref, bf16[512,1024]{1,0:T(8,128)(2,1)S(1)} %collective-permute-done.13.other_ref, bf16[1024,1024]{1,0:T(8,128)(2,1)S(1)} %get-tuple-element.84.w_ref), custom_call_target="tpu_custom_call" | custom-call | tf_op jit(solution)/shard_map/output/pallas_call | solution.py:489
  (16 shorter events, 0.1 us)
Async XLA Ops:
  0.0 5.4 %collective-permute-start = (bf16[512,1024]{1,0:T(8,128)(2,1)}, bf16[512,1024]{1,0:T(8,128)(2,1)S(1)}, u32[]{:S(2)}, u32[]{:S(2)}) collective-permute-start(bf16[512,1024]{1,0:T(8,128)(2,1)} %own_ref.1), channel_id=1, source_target_pairs={{0,1},{1,0},{2,3},{3,2},{4,5},{5,4},{6,7},{7,6},{8,9},{9,8},{10,11... | collective-permute-start | bytes 3145736 | tf_op jit(solution)/shard_map/ppermute | solution.py:505
  2.2 7.2 %collective-permute-start.1 = (bf16[16,1024]{1,0:T(8,128)(2,1)S(1)}, bf16[16,1024]{1,0:T(8,128)(2,1)S(1)}, u32[]{:S(2)}, u32[]{:S(2)}) collective-permute-start(bf16[16,1024]{1,0:T(8,128)(2,1)S(1)} %slice.55), channel_id=1, source_target_pairs={{0,2},{2,4},{4,6},{6,8},{8,10},{10,12},{12,14},{14,16},{16,18},{18... | collective-permute-start | bytes 98312 | tf_op jit(solution)/shard_map/ppermute | solution.py:510
  5.4 5.3 %copy-start = (bf16[1024,2048]{1,0:T(8,128)(2,1)S(1)}, bf16[1024,2048]{1,0:T(8,128)(2,1)}, u32[]{:S(2)}) copy-start(bf16[1024,2048]{1,0:T(8,128)(2,1)} %w_ref) | copy-start | bytes 12582916
  9.4 1.3 %collective-permute-start.2 = (bf16[16,1024]{1,0:T(8,128)(2,1)S(1)}, bf16[16,1024]{1,0:T(8,128)(2,1)S(1)}, u32[]{:S(2)}, u32[]{:S(2)}) collective-permute-start(bf16[16,1024]{1,0:T(8,128)(2,1)S(1)} %collective-permute-done.1.halo_own_ref), channel_id=1, source_target_pairs={{0,1},{1,0},{2,3},{3,2},{4,5},{5,4},{6,7},{7,6},{8,9},{9,8},{10,11... | collective-permute-start | bytes 98312 | tf_op jit(solution)/shard_map/ppermute | solution.py:505
  10.7 36.7 %collective-permute-start.12 = (bf16[1024,2048]{1,0:T(8,128)(2,1)S(1)}, bf16[1024,2048]{1,0:T(8,128)(2,1)S(1)}, u32[]{:S(2)}, u32[]{:S(2)}) collective-permute-start(bf16[1024,2048]{1,0:T(8,128)(2,1)S(1)} %copy-done), channel_id=1, source_target_pairs={{0,1},{1,0},{2,3},{3,2},{4,5},{5,4},{6,7},{7,6},{8,9},{9,8},{10,11... | collective-permute-start | bytes 12582920 | tf_op jit(solution)/shard_map/ppermute | solution.py:505
  11.0 11.5 %copy-start.1 = (f32[1024,16]{0,1:T(8,128)S(1)}, f32[1024,16]{0,1:T(8,128)}, u32[]{:S(2)}) copy-start(f32[1024,16]{0,1:T(8,128)} %param.10) | copy-start | bytes 196612
  11.0 11.5 %copy-start.2 = (f32[1024,16]{0,1:T(8,128)S(1)}, f32[1024,16]{0,1:T(8,128)}, u32[]{:S(2)}) copy-start(f32[1024,16]{0,1:T(8,128)} %param.9) | copy-start | bytes 196612
  17.9 7.2 %collective-permute-start.3 = (bf16[16,1024]{1,0:T(8,128)(2,1)S(1)}, bf16[16,1024]{1,0:T(8,128)(2,1)S(1)}, u32[]{:S(2)}, u32[]{:S(2)}) collective-permute-start(bf16[16,1024]{1,0:T(8,128)(2,1)S(1)} %convert_element_type.36), channel_id=1, source_target_pairs={{0,2},{2,4},{4,6},{6,0},{1,3},{3,5},{5,7},{7,1},{8,10},{10,12},{12... | collective-permute-start | bytes 98312 | tf_op jit(solution)/shard_map/ppermute | solution.py:516
  19.2 5.9 %collective-permute-start.4 = (bf16[16,1024]{1,0:T(8,128)(2,1)S(1)}, bf16[16,1024]{1,0:T(8,128)(2,1)S(1)}, u32[]{:S(2)}, u32[]{:S(2)}) collective-permute-start(bf16[16,1024]{1,0:T(8,128)(2,1)S(1)} %convert_element_type.36), channel_id=1, source_target_pairs={{0,4},{2,6},{4,0},{6,2},{1,5},{3,7},{5,1},{7,3},{8,12},{10,14},{12... | collective-permute-start | bytes 98312 | tf_op jit(solution)/shard_map/ppermute | solution.py:516
  21.6 3.5 %collective-permute-start.5 = (bf16[16,1024]{1,0:T(8,128)(2,1)S(1)}, bf16[16,1024]{1,0:T(8,128)(2,1)S(1)}, u32[]{:S(2)}, u32[]{:S(2)}) collective-permute-start(bf16[16,1024]{1,0:T(8,128)(2,1)S(1)} %convert_element_type.36), channel_id=1, source_target_pairs={{0,6},{2,0},{4,2},{6,4},{1,7},{3,1},{5,3},{7,5},{8,14},{10,8},{12,... | collective-permute-start | bytes 98312 | tf_op jit(solution)/shard_map/ppermute | solution.py:516
  25.1 8.0 %collective-permute-start.6 = (bf16[16,1024]{1,0:T(8,128)(2,1)S(1)}, bf16[16,1024]{1,0:T(8,128)(2,1)S(1)}, u32[]{:S(2)}, u32[]{:S(2)}) collective-permute-start(bf16[16,1024]{1,0:T(8,128)(2,1)S(1)} %get-tuple-element.85), channel_id=1, source_target_pairs={{0,8},{8,16},{16,24},{24,0},{1,9},{9,17},{17,25},{25,1},{2,10},{10... | collective-permute-start | bytes 98312 | tf_op jit(solution)/shard_map/ppermute | solution.py:516
  26.5 6.6 %collective-permute-start.7 = (bf16[16,1024]{1,0:T(8,128)(2,1)S(1)}, bf16[16,1024]{1,0:T(8,128)(2,1)S(1)}, u32[]{:S(2)}, u32[]{:S(2)}) collective-permute-start(bf16[16,1024]{1,0:T(8,128)(2,1)S(1)} %get-tuple-element.85), channel_id=1, source_target_pairs={{0,16},{8,24},{16,0},{24,8},{1,17},{9,25},{17,1},{25,9},{2,18},{10... | collective-permute-start | bytes 98312 | tf_op jit(solution)/shard_map/ppermute | solution.py:516
  29.1 4.0 %collective-permute-start.8 = (bf16[16,1024]{1,0:T(8,128)(2,1)S(1)}, bf16[16,1024]{1,0:T(8,128)(2,1)S(1)}, u32[]{:S(2)}, u32[]{:S(2)}) collective-permute-start(bf16[16,1024]{1,0:T(8,128)(2,1)S(1)} %get-tuple-element.85), channel_id=1, source_target_pairs={{0,24},{8,0},{16,8},{24,16},{1,25},{9,1},{17,9},{25,17},{2,26},{10... | collective-permute-start | bytes 98312 | tf_op jit(solution)/shard_map/ppermute | solution.py:516
  33.2 7.7 %collective-permute-start.10 = (bf16[16,1024]{1,0:T(8,128)(2,1)S(1)}, bf16[16,1024]{1,0:T(8,128)(2,1)S(1)}, u32[]{:S(2)}, u32[]{:S(2)}) collective-permute-start(bf16[16,1024]{1,0:T(8,128)(2,1)S(1)} %fusion.14), channel_id=1, source_target_pairs={{0,64},{32,96},{64,0},{96,32},{1,65},{33,97},{65,1},{97,33},{2,66}... | collective-permute-start | bytes 98312 | tf_op jit(solution)/shard_map/ppermute | solution.py:516
  36.8 4.0 %collective-permute-start.11 = (bf16[16,1024]{1,0:T(8,128)(2,1)S(1)}, bf16[16,1024]{1,0:T(8,128)(2,1)S(1)}, u32[]{:S(2)}, u32[]{:S(2)}) collective-permute-start(bf16[16,1024]{1,0:T(8,128)(2,1)S(1)} %fusion.14), channel_id=1, source_target_pairs={{0,96},{32,0},{64,32},{96,64},{1,97},{33,1},{65,33},{97,65},{2,98}... | collective-permute-start | bytes 98312 | tf_op jit(solution)/shard_map/ppermute | solution.py:516
  37.3 4.0 %collective-permute-start.9 = (bf16[16,1024]{1,0:T(8,128)(2,1)S(1)}, bf16[16,1024]{1,0:T(8,128)(2,1)S(1)}, u32[]{:S(2)}, u32[]{:S(2)}) collective-permute-start(bf16[16,1024]{1,0:T(8,128)(2,1)S(1)} %fusion.14), channel_id=1, source_target_pairs={{0,32},{32,64},{64,96},{96,0},{1,33},{33,65},{65,97},{97,1},{2,34}... | collective-permute-start | bytes 98312 | tf_op jit(solution)/shard_map/ppermute | solution.py:516
  43.7 6.0 %collective-permute-start.13 = (bf16[512,1024]{1,0:T(8,128)(2,1)S(1)}, bf16[512,1024]{1,0:T(8,128)(2,1)S(1)}, u32[]{:S(2)}, u32[]{:S(2)}) collective-permute-start(bf16[512,1024]{1,0:T(8,128)(2,1)S(1)} %hidden.1.hidden_ref), channel_id=1, source_target_pairs={{0,1},{1,0},{2,3},{3,2},{4,5},{5,4},{6,7},{7,6},{8,9},{9,8},{10,11... | collective-permute-start | bytes 3145736 | tf_op jit(solution)/shard_map/ppermute | solution.py:505
